TPU v7x, 256 devices: a whole 4x4x8 slice. The times are simulated.
256 devices in a mesh: gx: 16 (over y, x_lo, core), gy: 16 (over z, x_hi).
Axes of the slice: x: 4 (x_hi: 2, x_lo: 2; x = x_hi * 2 + x_lo), y: 4, z: 8, core: 2. Of those that a mesh axis runs over, the one named last changes fastest.
Arguments:
- features: bfloat16 [16, 16, 1, 96, 4096], P('gx', 'gy'), may hold values from -6 to 6
- weight: bfloat16 [96, 2592], replicated, may hold values from -0.125 to 0.125
- occupancy: int32 [16, 16, 1, 4096], P('gx', 'gy'), may hold values from 0 to 1, as said below
- adjacency: int32 [16, 16, 1, 6], P('gx', 'gy'), may hold values from -1 to 0, as said below
- cotangent: bfloat16 [16, 16, 1, 96, 4096], P('gx', 'gy'), may hold values from -6 to 6
Outputs:
- outputs: bfloat16 [16, 16, 1, 96, 4096], P('gx', 'gy')
- feature_grad: bfloat16 [16, 16, 1, 96, 4096], P('gx', 'gy')
- weight_grad: float32 [96, 2592], replicated
Inputs may be any that keep to these rules, and one draw needn't show every extreme that they name: `occupancy`: 1 marks an occupied voxel; every voxel of a slot that holds no block is 0. `adjacency`: column (i, j) holds exactly one block, in slot 0 (so faces 4 and 5 are always -1). Face 0 and 1 name a slot of column (i - 1, j) and (i + 1, j), faces 2 and 3 of column (i, j - 1) and (i, j + 1), faces 4 and 5 the slots s - 1 and s + 1 of the same column; -1 where no block lies across the face or the slot is empty. The relation is symmetric.
All inputs are finite; a program needn't handle non-finite values.
Results may differ from a plain program's by a relative error of at most 0.0028.
Values may be sent and summed in bfloat16 or wider, within the bound.
No kernel may reach another device: no remote copies, remote signals or barrier semaphores. Data moves between devices by JAX's collectives and lax.ppermute only.
A program may use at most 192 MiB of HBM per device.

v0:
```python
import math

import jax
import jax.numpy as jnp
from jax import lax
from jax.sharding import PartitionSpec as P

BS = 16


def shifted(array, axis, by):
    size = lax.axis_size(axis)
    pairs = [(i, i + by) for i in range(size) if 0 <= i + by < size]
    return lax.ppermute(array, axis, pairs)


def select_slots(layers, slot_ids):
    chosen = jnp.zeros_like(layers)
    matches = (slot_ids == 0)[..., None, None, None]
    chosen = jnp.where(matches, layers[..., 0, :, :, :][..., None, :, :, :], chosen)
    return chosen


def with_shells(values, neighbours):
    from_west = shifted(values[:, :, -1], "gx", 1)
    from_east = shifted(values[:, :, 0], "gx", -1)
    west = select_slots(from_west, neighbours[:, 0])
    east = select_slots(from_east, neighbours[:, 1])
    along_x = jnp.concatenate([west[:, :, None], values, east[:, :, None]], 2)
    from_south = shifted(along_x[:, :, :, -1], "gy", 1)
    from_north = shifted(along_x[:, :, :, 0], "gy", -1)
    south = select_slots(from_south, neighbours[:, 2])
    north = select_slots(from_north, neighbours[:, 3])
    along_y = jnp.concatenate([south[:, :, :, None], along_x, north[:, :, :, None]], 3)
    below = select_slots(along_y[:, :, :, :, -1], neighbours[:, 4])
    above = select_slots(along_y[:, :, :, :, 0], neighbours[:, 5])
    return jnp.concatenate([below[..., None], along_y, above[..., None]], 4)


def gradient_shells(values, neighbours):
    below = select_slots(values[:, :, :, :, -1], neighbours[:, 4])
    above = select_slots(values[:, :, :, :, 0], neighbours[:, 5])
    along_z = jnp.concatenate([below[..., None], values, above[..., None]], 4)
    from_south = shifted(along_z[:, :, :, -1], "gy", 1)
    from_north = shifted(along_z[:, :, :, 0], "gy", -1)
    south = select_slots(from_south, neighbours[:, 2])
    north = select_slots(from_north, neighbours[:, 3])
    along_y = jnp.concatenate([south[:, :, :, None], along_z, north[:, :, :, None]], 3)
    from_west = shifted(along_y[:, :, -1], "gx", 1)
    from_east = shifted(along_y[:, :, 0], "gx", -1)
    west = select_slots(from_west, neighbours[:, 0])
    east = select_slots(from_east, neighbours[:, 1])
    return jnp.concatenate([west[:, :, None], along_y, east[:, :, None]], 2)


def slab_ranges(extent):
    ranges = []
    start = 0
    while start < extent:
        width = min(4, extent - start)
        ranges.append((start, width))
        start = start + width
    return ranges


def tap_columns(source, first, width, extent, flipped):
    blocks, channels = (source.shape[0], source.shape[1])
    pieces = []
    for along_x in range(3):
        for along_y in range(3):
            for along_z in range(3):
                if flipped:
                    off_x, off_y, off_z = (2 - along_x, 2 - along_y, 2 - along_z)
                else:
                    off_x, off_y, off_z = (along_x, along_y, along_z)
                piece = source[
                    :,
                    :,
                    first + off_x : first + off_x + width,
                    off_y : off_y + extent,
                    off_z : off_z + extent,
                ]
                pieces.append(piece.reshape(blocks, channels, width * extent * extent))
    return jnp.concatenate(pieces, 1)


def forward_and_weights(padded, gradient_masked, weight):
    extent = padded.shape[2] - 2
    plane = extent * extent
    out_parts = []
    weight_total = jnp.zeros(weight.shape, jnp.float32)
    for first, width in slab_ranges(extent):
        columns = tap_columns(padded, first, width, extent, False)
        out_parts.append(
            jnp.einsum("or,brm->bom", weight, columns, preferred_element_type=jnp.float32)
        )
        grad_slab = gradient_masked[:, :, first * plane : (first + width) * plane]
        weight_total = weight_total + jnp.einsum(
            "bom,brm->or", grad_slab, columns, preferred_element_type=jnp.float32
        )
    return (jnp.concatenate(out_parts, 2), weight_total)


def spread_back(grad_padded, weight):
    channels = weight.shape[0]
    extent = grad_padded.shape[2] - 2
    turned = (
        weight.reshape(channels, 27, channels).transpose(2, 1, 0).reshape(channels, 27 * channels)
    )
    out_parts = []
    for first, width in slab_ranges(extent):
        columns = tap_columns(grad_padded, first, width, extent, True)
        out_parts.append(
            jnp.einsum("or,brm->bom", turned, columns, preferred_element_type=jnp.float32)
        )
    return jnp.concatenate(out_parts, 2)


def body(features, weight, occupancy, adjacency, cotangent):
    blocks, channels = (features.shape[2], features.shape[3])
    extent = BS
    block_shape = (blocks, channels, extent, extent, extent)
    occupied = occupancy.reshape(blocks, 1, extent**3).astype(jnp.bfloat16)
    occupied_f = occupied.astype(jnp.float32)
    neighbours = adjacency.reshape(blocks, 6)
    masked = features.reshape(blocks, channels, extent**3) * occupied
    gradient_masked = cotangent.reshape(blocks, channels, extent**3) * occupied
    padded = with_shells(masked.reshape(block_shape), neighbours)
    reduced_total, partial_value = forward_and_weights(padded, gradient_masked, weight)
    outputs = (reduced_total * occupied_f).astype(jnp.bfloat16)
    grad_padded = gradient_shells(gradient_masked.reshape(block_shape), neighbours)
    spread = spread_back(grad_padded, weight)
    feature_grad = (spread * occupied_f).astype(jnp.bfloat16)
    summed_grad = lax.psum(partial_value, ("gx", "gy"))
    slot_count = lax.axis_size("gx") * lax.axis_size("gy") * blocks * extent**3
    weight_grad = summed_grad * (1.0 / math.sqrt(slot_count))
    out_shape = (1, 1, blocks, channels, extent**3)
    return (outputs.reshape(out_shape), feature_grad.reshape(out_shape), weight_grad)


def solution(mesh):
    placed = (
        P("gx", "gy", None, None, None),
        P(),
        P("gx", "gy", None, None),
        P("gx", "gy", None, None),
        P("gx", "gy", None, None, None),
    )
    return jax.shard_map(
        body,
        mesh=mesh,
        in_specs=placed,
        out_specs=(P("gx", "gy", None, None, None), P("gx", "gy", None, None, None), P()),
        check_vma=False,
    )
```

profile of v0, /device:TPU:1, one launch (start us, length us, event | category | flops | bytes accessed | tf_op | source)
XLA Modules:
  0.0 465.4 jit_solution(3051724697896263604)
XLA Ops:
  7.2 1.5 fusion.94
  8.8 1.6 copy.26
  11.2 1.3 copy.23
  13.8 1.7 broadcast_multiply_fusion
  15.9 0.8 fusion.78
  16.7 1.3 collective-permute-start.4
  18.0 6.8 %collective-permute-start.5 = (bf16[1,96,16,18]{1,3,2,0:T(8,128)(2,1)}, bf16[1,96,16,18]{1,3,2,0:T(8,128)(2,1)}, u32[]{:S(2)}, u32[]{:S(2)}) collective-permute-start(bf16[1,96,16,18]{1,3,2,0:T(8,128)(2,1)} %get-tuple-element.163), channel_id=1, source_target_pairs={{0,1},{1,2},{2,3},{3,4},{4,5},{5,6},{6,7},{7,8},{8,9},{9,10},{10,1... | collective-permute-start | bytes 165896 | tf_op jit(solution)/shard_map/ppermute | solution.py:14
  25.4 5.1 %collective-permute-start.1 = (bf16[1,96,16,16]{1,3,2,0:T(8,128)(2,1)}, bf16[1,96,16,16]{1,3,2,0:T(8,128)(2,1)}, u32[]{:S(2)}, u32[]{:S(2)}) collective-permute-start(bf16[1,96,16,16]{1,3,2,0:T(8,128)(2,1)} %get-tuple-element.238), channel_id=1, source_target_pairs={{16,0},{32,16},{48,32},{64,48},{80,64},{96,80},{112,96},{128,112},... | collective-permute-start | bytes 147464 | tf_op jit(solution)/shard_map/ppermute | solution.py:14
  30.5 1.9 collective-permute-start
  32.4 1.6 fusion.92
  34.1 2.2 fusion.61
  36.2 0.9 bitcast_multiply_fusion
  37.2 2.3 fusion.70
  40.1 1.1 copy.32
  41.2 1.4 copy.33
  45.1 0.9 select_bitcast_fusion.5
  46.0 0.9 select_bitcast_fusion.6
  46.9 1.9 fusion.93
  49.5 1.3 collective-permute-start.3
  50.8 6.1 %collective-permute-start.2 = (bf16[1,96,18,16]{1,3,2,0:T(8,128)(2,1)}, bf16[1,96,18,16]{1,3,2,0:T(8,128)(2,1)}, u32[]{:S(2)}, u32[]{:S(2)}) collective-permute-start(bf16[1,96,18,16]{1,3,2,0:T(8,128)(2,1)} %get-tuple-element.209), channel_id=1, source_target_pairs={{0,1},{1,2},{2,3},{3,4},{4,5},{5,6},{6,7},{7,8},{8,9},{9,10},{10,1... | collective-permute-start | bytes 165896 | tf_op jit(solution)/shard_map/ppermute | solution.py:14
  56.9 0.9 broadcast_select_fusion.4
  57.9 0.8 maximum_bitcast_fusion
  58.7 2.0 maximum_maximum_fusion.2
  60.8 2.6 fusion.88
  63.3 1.8 fusion.89
  65.2 2.6 fusion.86
  67.7 1.8 fusion.87
  69.6 2.3 collective-permute-start.6
  71.9 2.6 collective-permute-start.7
  74.5 10.8 %concatenate.326 = bf16[1,2592,1024]{1,2,0:T(8,128)(2,1)} concatenate(bf16[1,96,1024]{1,2,0:T(8,128)(2,1)} %bitcast.549, bf16[1,96,1024]{1,2,0:T(8,128)(2,1)} %bitcast.548, bf16[1,96,1024]{1,2,0:T(8,128)(2,1)} %bitcast.547, bf16[1,96,1024]{1,2,0:T(8,128)(2,1)} %bitcast.463, bf16[1,96,1024]{1,2,0:T(8,128)(2,1)} %bitcast.451, bf16[1,96,1024]{1,2,0:T(8,128)(2,1)} %bitcast.460, ...), dimensions={1} | concatenate | bytes 10616832 | tf_op jit(solution)/shard_map/concatenate | solution.py:84
  85.3 5.1 %fusion.53 = f32[1,1,1,96,1024]{4,3,2,1,0:T(8,128)} fusion(bf16[96,2592]{0,1:T(8,128)(2,1)S(1)} %bitcast.396, bf16[1,2592,1024]{1,2,0:T(8,128)(2,1)} %concatenate.326), kind=kOutput, calls=%fused_computation.81 | convolution fusion | flops 509607936 | bytes 6199296 | tf_op jit(solution)/shard_map/or,brm->bom/dot_general | solution.py:114
  90.4 10.6 %concatenate.324 = bf16[1,2592,1024]{1,2,0:T(8,128)(2,1)} concatenate(bf16[1,96,1024]{1,2,0:T(8,128)(2,1)} %bitcast.537, bf16[1,96,1024]{1,2,0:T(8,128)(2,1)} %bitcast.536, bf16[1,96,1024]{1,2,0:T(8,128)(2,1)} %bitcast.535, bf16[1,96,1024]{1,2,0:T(8,128)(2,1)} %bitcast.445, bf16[1,96,1024]{1,2,0:T(8,128)(2,1)} %bitcast.441, bf16[1,96,1024]{1,2,0:T(8,128)(2,1)} %bitcast.442, ...), dimensions={1} | concatenate | bytes 10616832 | tf_op jit(solution)/shard_map/concatenate | solution.py:84
  101.0 5.2 %fusion.50 = f32[1,1,1,96,1024]{4,3,2,1,0:T(8,128)} fusion(bf16[96,2592]{0,1:T(8,128)(2,1)S(1)} %bitcast.397, bf16[1,2592,1024]{1,2,0:T(8,128)(2,1)} %concatenate.324), kind=kOutput, calls=%fused_computation.80 | convolution fusion | flops 509607936 | bytes 6199296 | tf_op jit(solution)/shard_map/or,brm->bom/dot_general | solution.py:114
  106.1 0.9 select_bitcast_fusion.3
  107.9 2.5 pad_maximum_fusion
  110.4 2.3 fusion.81
  112.8 1.9 fusion.83
  114.6 2.9 fusion.80
  117.5 2.6 fusion.82
  120.1 1.9 fusion.91
  122.0 1.8 fusion.90
  123.9 10.6 %concatenate.312 = bf16[1,2592,1024]{1,2,0:T(8,128)(2,1)} concatenate(bf16[1,96,1024]{1,2,0:T(8,128)(2,1)} %bitcast.516, bf16[1,96,1024]{1,2,0:T(8,128)(2,1)} %bitcast.594, bf16[1,96,1024]{1,2,0:T(8,128)(2,1)} %bitcast.561, bf16[1,96,1024]{1,2,0:T(8,128)(2,1)} %bitcast.515, bf16[1,96,1024]{1,2,0:T(8,128)(2,1)} %bitcast.617, bf16[1,96,1024]{1,2,0:T(8,128)(2,1)} %bitcast.560, ...), dimensions={1} | concatenate | bytes 10616832 | tf_op jit(solution)/shard_map/concatenate | solution.py:84
  134.4 5.1 %fusion.44 = f32[1,1,1,96,1024]{4,3,2,1,0:T(8,128)} fusion(bf16[96,2592]{1,0:T(8,128)(2,1)S(1)} %copy-done.1, bf16[1,2592,1024]{1,2,0:T(8,128)(2,1)} %concatenate.312), kind=kOutput, calls=%fused_computation.78 | convolution fusion | flops 509607936 | bytes 6199296 | tf_op jit(solution)/shard_map/or,brm->bom/dot_general | solution.py:95
  139.5 10.5 %concatenate.309 = bf16[1,2592,1024]{1,2,0:T(8,128)(2,1)} concatenate(bf16[1,96,1024]{1,2,0:T(8,128)(2,1)} %bitcast.495, bf16[1,96,1024]{1,2,0:T(8,128)(2,1)} %bitcast.564, bf16[1,96,1024]{1,2,0:T(8,128)(2,1)} %bitcast.531, bf16[1,96,1024]{1,2,0:T(8,128)(2,1)} %bitcast.494, bf16[1,96,1024]{1,2,0:T(8,128)(2,1)} %bitcast.615, bf16[1,96,1024]{1,2,0:T(8,128)(2,1)} %bitcast.530, ...), dimensions={1} | concatenate | bytes 10616832 | tf_op jit(solution)/shard_map/concatenate | solution.py:84
  150.1 5.1 %fusion.41 = f32[1,1,1,96,1024]{4,3,2,1,0:T(8,128)} fusion(bf16[96,2592]{1,0:T(8,128)(2,1)S(1)} %copy-done.1, bf16[1,2592,1024]{1,2,0:T(8,128)(2,1)} %concatenate.309), kind=kOutput, calls=%fused_computation.77 | convolution fusion | flops 509607936 | bytes 6199296 | tf_op jit(solution)/shard_map/or,brm->bom/dot_general | solution.py:95
  155.2 10.3 %concatenate.307 = bf16[1,2592,1024]{1,2,0:T(8,128)(2,1)} concatenate(bf16[1,96,1024]{1,2,0:T(8,128)(2,1)} %bitcast.475, bf16[1,96,1024]{1,2,0:T(8,128)(2,1)} %bitcast.522, bf16[1,96,1024]{1,2,0:T(8,128)(2,1)} %bitcast.507, bf16[1,96,1024]{1,2,0:T(8,128)(2,1)} %bitcast.474, bf16[1,96,1024]{1,2,0:T(8,128)(2,1)} %bitcast.612, bf16[1,96,1024]{1,2,0:T(8,128)(2,1)} %bitcast.506, ...), dimensions={1} | concatenate | bytes 10616832 | tf_op jit(solution)/shard_map/concatenate | solution.py:84
  165.5 5.2 %fusion.38 = f32[1,1,1,96,1024]{4,3,2,1,0:T(8,128)} fusion(bf16[96,2592]{1,0:T(8,128)(2,1)S(1)} %copy-done.1, bf16[1,2592,1024]{1,2,0:T(8,128)(2,1)} %concatenate.307), kind=kOutput, calls=%fused_computation.76 | convolution fusion | flops 509607936 | bytes 6199296 | tf_op jit(solution)/shard_map/or,brm->bom/dot_general | solution.py:95
  170.8 2.0 fusion.16
  172.7 10.6 %concatenate.305 = bf16[1,2592,1024]{1,2,0:T(8,128)(2,1)} concatenate(bf16[1,96,1024]{1,2,0:T(8,128)(2,1)} %bitcast.459, bf16[1,96,1024]{1,2,0:T(8,128)(2,1)} %bitcast.486, bf16[1,96,1024]{1,2,0:T(8,128)(2,1)} %bitcast.483, bf16[1,96,1024]{1,2,0:T(8,128)(2,1)} %bitcast.458, bf16[1,96,1024]{1,2,0:T(8,128)(2,1)} %bitcast.608, bf16[1,96,1024]{1,2,0:T(8,128)(2,1)} %bitcast.482, ...), dimensions={1} | concatenate | bytes 10616832 | tf_op jit(solution)/shard_map/concatenate | solution.py:84
  183.3 3.8 fusion.24
  187.2 3.7 fusion.27
  190.9 2.0 fusion.30
  192.9 4.4 fusion.35
  197.4 0.9 select_bitcast_fusion.1
  198.3 0.9 select_bitcast_fusion
  199.2 3.8 maximum_maximum_fusion.1
  203.1 2.4 fusion.84
  205.9 10.6 %concatenate.329 = bf16[1,2592,1024]{1,2,0:T(8,128)(2,1)} concatenate(bf16[1,96,1024]{1,2,0:T(8,128)(2,1)} %bitcast.595, bf16[1,96,1024]{1,2,0:T(8,128)(2,1)} %bitcast.596, bf16[1,96,1024]{1,2,0:T(8,128)(2,1)} %bitcast.597, bf16[1,96,1024]{1,2,0:T(8,128)(2,1)} %bitcast.598, bf16[1,96,1024]{1,2,0:T(8,128)(2,1)} %bitcast.599, bf16[1,96,1024]{1,2,0:T(8,128)(2,1)} %bitcast.600, ...), dimensions={1} | concatenate | bytes 10616832 | tf_op jit(solution)/shard_map/concatenate | solution.py:84
  216.6 4.5 fusion.56
  221.1 10.8 %concatenate.322 = bf16[1,2592,1024]{1,2,0:T(8,128)(2,1)} concatenate(bf16[1,96,1024]{1,2,0:T(8,128)(2,1)} %bitcast.420, bf16[1,96,1024]{1,2,0:T(8,128)(2,1)} %bitcast.419, bf16[1,96,1024]{1,2,0:T(8,128)(2,1)} %bitcast.418, bf16[1,96,1024]{1,2,0:T(8,128)(2,1)S(1)} %bitcast.407, bf16[1,96,1024]{1,2,0:T(8,128)(2,1)S(1)} %bitcast.403, bf16[1,96,1024]{1,2,0:T(8,128)(2,1)S(1)} %bitcast.405, ...), dimensions={1} | concatenate | bytes 10616832 | tf_op jit(solution)/shard_map/concatenate | solution.py:84
  232.0 4.5 fusion.47
  236.6 1.4 fusion.34
  238.0 218.3 %all-reduce.2.cloned.1.call-done = f32[96,2592]{1,0:T(8,128)} async-done(((f32[96,2592]{1,0:T(8,128)}), f32[96,2592]{1,0:T(8,128)}) %all-reduce.2.cloned.1.call-update) | async-done | bytes 995344 | tf_op jit(solution)/shard_map/psum | solution.py:134
  456.3 2.2 broadcast_multiply_fusion.2
  (97 shorter events, 4.6 us)
Async XLA Ops:
  7.2 4.1 copy-start.33
  7.2 449.2 %all-reduce.2.cloned.1.call-start = ((), (), s32[]{:S(2)}) async-start(), calls=%async_computation | async-start | bytes 2064384 | tf_op jit(solution)/shard_map/psum | solution.py:134
  16.7 40.2 %collective-permute-start.4 = (bf16[1,96,16,18]{1,3,2,0:T(8,128)(2,1)}, bf16[1,96,16,18]{1,3,2,0:T(8,128)(2,1)}, u32[]{:S(2)}, u32[]{:S(2)}) collective-permute-start(bf16[1,96,16,18]{1,3,2,0:T(8,128)(2,1)} %get-tuple-element.164), channel_id=1, source_target_pairs={{1,0},{2,1},{3,2},{4,3},{5,4},{6,5},{7,6},{8,7},{9,8},{10,9},{11,1... | collective-permute-start | bytes 165896 | tf_op jit(solution)/shard_map/ppermute | solution.py:14
  18.0 39.9 %collective-permute-start.5 = (bf16[1,96,16,18]{1,3,2,0:T(8,128)(2,1)}, bf16[1,96,16,18]{1,3,2,0:T(8,128)(2,1)}, u32[]{:S(2)}, u32[]{:S(2)}) collective-permute-start(bf16[1,96,16,18]{1,3,2,0:T(8,128)(2,1)} %get-tuple-element.163), channel_id=1, source_target_pairs={{0,1},{1,2},{2,3},{3,4},{4,5},{5,6},{6,7},{7,8},{8,9},{9,10},{10,1... | collective-permute-start | bytes 165896 | tf_op jit(solution)/shard_map/ppermute | solution.py:14
  25.4 19.7 %collective-permute-start.1 = (bf16[1,96,16,16]{1,3,2,0:T(8,128)(2,1)}, bf16[1,96,16,16]{1,3,2,0:T(8,128)(2,1)}, u32[]{:S(2)}, u32[]{:S(2)}) collective-permute-start(bf16[1,96,16,16]{1,3,2,0:T(8,128)(2,1)} %get-tuple-element.238), channel_id=1, source_target_pairs={{16,0},{32,16},{48,32},{64,48},{80,64},{96,80},{112,96},{128,112},... | collective-permute-start | bytes 147464 | tf_op jit(solution)/shard_map/ppermute | solution.py:14
  30.5 15.5 %collective-permute-start = (bf16[1,96,16,16]{1,3,2,0:T(8,128)(2,1)}, bf16[1,96,16,16]{1,3,2,0:T(8,128)(2,1)}, u32[]{:S(2)}, u32[]{:S(2)}) collective-permute-start(bf16[1,96,16,16]{1,3,2,0:T(8,128)(2,1)} %get-tuple-element.237), channel_id=1, source_target_pairs={{0,16},{16,32},{32,48},{48,64},{64,80},{80,96},{96,112},{112,128},... | collective-permute-start | bytes 147464 | tf_op jit(solution)/shard_map/ppermute | solution.py:14
  34.1 2.2 copy-start.2
  37.2 2.9 copy-start.1
  46.0 2.8 copy-start.4
  46.9 1.9 copy-start.6
  49.5 56.7 %collective-permute-start.3 = (bf16[1,96,18,16]{1,3,2,0:T(8,128)(2,1)}, bf16[1,96,18,16]{1,3,2,0:T(8,128)(2,1)}, u32[]{:S(2)}, u32[]{:S(2)}) collective-permute-start(bf16[1,96,18,16]{1,3,2,0:T(8,128)(2,1)} %get-tuple-element.210), channel_id=1, source_target_pairs={{1,0},{2,1},{3,2},{4,3},{5,4},{6,5},{7,6},{8,7},{9,8},{10,9},{11,1... | collective-permute-start | bytes 165896 | tf_op jit(solution)/shard_map/ppermute | solution.py:14
  50.8 56.3 %collective-permute-start.2 = (bf16[1,96,18,16]{1,3,2,0:T(8,128)(2,1)}, bf16[1,96,18,16]{1,3,2,0:T(8,128)(2,1)}, u32[]{:S(2)}, u32[]{:S(2)}) collective-permute-start(bf16[1,96,18,16]{1,3,2,0:T(8,128)(2,1)} %get-tuple-element.209), channel_id=1, source_target_pairs={{0,1},{1,2},{2,3},{3,4},{4,5},{5,6},{6,7},{7,8},{8,9},{9,10},{10,1... | collective-permute-start | bytes 165896 | tf_op jit(solution)/shard_map/ppermute | solution.py:14
  57.9 2.9 copy-start.13
  57.9 2.8 copy-start.15
  69.6 127.8 %collective-permute-start.6 = (bf16[1,96,18,18]{1,3,2,0:T(8,128)(2,1)}, bf16[1,96,18,18]{1,3,2,0:T(8,128)(2,1)}, u32[]{:S(2)}, u32[]{:S(2)}) collective-permute-start(bf16[1,96,18,18]{1,3,2,0:T(8,128)(2,1)} %get-tuple-element.155), channel_id=1, source_target_pairs={{0,16},{16,32},{32,48},{48,64},{64,80},{80,96},{96,112},{112,128},... | collective-permute-start | bytes 186632 | tf_op jit(solution)/shard_map/ppermute | solution.py:14
  71.9 126.4 %collective-permute-start.7 = (bf16[1,96,18,18]{1,3,2,0:T(8,128)(2,1)}, bf16[1,96,18,18]{1,3,2,0:T(8,128)(2,1)}, u32[]{:S(2)}, u32[]{:S(2)}) collective-permute-start(bf16[1,96,18,18]{1,3,2,0:T(8,128)(2,1)} %get-tuple-element.156), channel_id=1, source_target_pairs={{16,0},{32,16},{48,32},{64,48},{80,64},{96,80},{112,96},{128,112},... | collective-permute-start | bytes 186632 | tf_op jit(solution)/shard_map/ppermute | solution.py:14
  100.9 6.1 %copy-start.5 = (bf16[1,96,1,16,16]{1,4,3,2,0:T(8,128)(2,1)S(1)}, bf16[1,96,1,16,16]{1,4,3,2,0:T(8,128)(2,1)}, u32[]{:S(2)}) copy-start(bf16[1,96,1,16,16]{1,4,3,2,0:T(8,128)(2,1)} %copy-done.4) | copy-start | bytes 147460
  101.0 6.1 %copy-start.7 = (bf16[1,96,1,16,16]{1,4,3,2,0:T(8,128)(2,1)S(1)}, bf16[1,96,1,16,16]{1,4,3,2,0:T(8,128)(2,1)}, u32[]{:S(2)}) copy-start(bf16[1,96,1,16,16]{1,4,3,2,0:T(8,128)(2,1)} %copy-done.6) | copy-start | bytes 147460
  165.5 5.3 %copy-start = (bf16[1,2592,1024]{1,2,0:T(8,128)(2,1)S(1)}, bf16[1,2592,1024]{1,2,0:T(8,128)(2,1)}, u32[]{:S(2)}) copy-start(bf16[1,2592,1024]{1,2,0:T(8,128)(2,1)} %concatenate.307) | copy-start | bytes 15925252
  183.3 3.9 copy-start.3
  183.3 7.6 %slice-start = ((s8[5505024]{0:T(1024)(128)(4,1)}), s8[4194304]{0:T(1024)(128)(4,1)S(1)}, s32[]{:S(2)}) async-start(s8[5505024]{0:T(1024)(128)(4,1)} %bitcast.394), calls=%async_computation.1 | async-start | bytes 8388608
  187.2 3.8 slice-start.1
  192.9 6.3 %copy-start.14 = (bf16[1,96,16,1,18]{1,4,3,2,0:T(8,128)(2,1)S(1)}, bf16[1,96,16,1,18]{1,4,3,2,0:T(8,128)(2,1)}, u32[]{:S(2)}) copy-start(bf16[1,96,16,1,18]{1,4,3,2,0:T(8,128)(2,1)} %copy-done.13) | copy-start | bytes 165892
  192.9 6.3 %copy-start.16 = (bf16[1,96,16,1,18]{1,4,3,2,0:T(8,128)(2,1)S(1)}, bf16[1,96,16,1,18]{1,4,3,2,0:T(8,128)(2,1)}, u32[]{:S(2)}) copy-start(bf16[1,96,16,1,18]{1,4,3,2,0:T(8,128)(2,1)} %copy-done.15) | copy-start | bytes 165892
  203.0 2.5 copy-start.23
  203.0 2.5 copy-start.24
  203.0 2.5 copy-start.25
  203.0 2.5 copy-start.26
  203.0 2.5 copy-start.27
  203.1 2.5 copy-start.28
  203.1 2.5 copy-start.30
  203.1 2.6 copy-start.31
  203.1 2.8 copy-start.32
  216.5 4.6 copy-start.17
  216.5 4.6 copy-start.18
  216.5 4.6 copy-start.19
  216.5 4.6 copy-start.20
  216.5 4.6 copy-start.21
  216.5 4.6 copy-start.22
  216.6 4.6 copy-start.29
  231.9 4.6 copy-start.8
  231.9 4.6 copy-start.9
  231.9 4.6 copy-start.10
  232.0 4.6 copy-start.11
  232.0 4.6 copy-start.12
  232.0 4.6 copy-start.34
Sparse Core Ops, SparseCore 0:
  197.5 258.8 all-reduce.1
where the time goes:
time: 475 us; the launch traced here: 465 us
  waiting for transfers between devices  218 us (46%)
  local copies, waits for them, and re-layouts  117 us (25%)
  matrix products  50.7 us (11%)
  other arithmetic  32.8 us (7%)
  starting transfers between devices  27.4 us (6%)
  between operations  18.6 us (4%)
    psum x1, waiting for transfers between devices, body(): summed_grad = lax.psum(partial_value, ('gx', 'gy'))  218 us
    concatenate x8, local copies, waits for them, and re-layouts, tap_columns(): return jnp.concatenate(pieces, 1)  84.6 us
    ppermute x8, starting transfers between devices, shifted(): return lax.ppermute(array, axis, pairs)  27.4 us
    slice x11, local copies, waits for them, and re-layouts, tap_columns(): source[:, :, first + off_x:first + off_x + width, off_y:off_y + extent, o...  24.6 us
    dot_general x4, matrix products, forward_and_weights(): jnp.einsum('or,brm->bom', weight, columns, preferred_element_type=jnp.flo...  19.8 us
    dot_general x4, matrix products, spread_back(): jnp.einsum('or,brm->bom', turned, columns, preferred_element_type=jnp.flo...  19.3 us
    dot_general x4, matrix products, forward_and_weights(): jnp.einsum('bom,brm->or', grad_slab, columns, preferred_element_type=jnp....  11.5 us
  transfers between devices with their start and end apart: 9, of which 1 were waited for; matrix products, arithmetic and copies ran while one was open for 41% of the time, Pallas kernels for 0%

commit v1 on v0

v1 whole, which is shorter than its diff:
```python
import math

import jax
import jax.numpy as jnp
from jax import lax
from jax.experimental import pallas as pl
from jax.experimental.pallas import tpu as pltpu
from jax.sharding import PartitionSpec as P

BS = 16
PLANE = BS * BS
VOX = BS**3
C = 96
F32 = jnp.float32
BF16 = jnp.bfloat16
VMEM = pl.BlockSpec(memory_space=pltpu.VMEM)
LIMIT = pltpu.CompilerParams(vmem_limit_bytes=48 << 20)


def shifted(array, axis, by):
    size = lax.axis_size(axis)
    pairs = [(i, i + by) for i in range(size) if 0 <= i + by < size]
    return lax.ppermute(array, axis, pairs)


def swap(array, axis, mask):
    return lax.ppermute(array, axis, [(i, i ^ mask) for i in range(lax.axis_size(axis))])


def y_face(values, first):
    return jnp.concatenate(
        [values[:, x * PLANE + first : x * PLANE + first + BS] for x in range(BS)], 1
    )


def prepare_kernel(feat, cot, occ, f_out, g_out, f_south, f_north, g_south, g_north):
    occupied = occ[...].astype(BF16)
    for source, out, low, high in (
        (feat, f_out, f_south, f_north),
        (cot, g_out, g_south, g_north),
    ):
        masked = source[...] * occupied
        out[...] = masked
        low[...] = y_face(masked, 0)
        high[...] = y_face(masked, PLANE - BS)


def prepare(features, cotangent, occupancy):
    whole = jax.ShapeDtypeStruct((C, VOX), BF16)
    face = jax.ShapeDtypeStruct((C, PLANE), BF16)
    return pl.pallas_call(
        prepare_kernel,
        out_shape=(whole, whole, face, face, face, face),
        in_specs=[VMEM] * 3,
        out_specs=(VMEM,) * 6,
        compiler_params=LIMIT,
        cost_estimate=pl.CostEstimate(flops=2**20, bytes_accessed=4 << 20, transcendentals=0),
    )(features, cotangent, occupancy)


def build_shifts(centre, west, east, south, north, shifts):
    shifts[1, :, :PLANE] = west[...]
    shifts[1, :, PLANE : PLANE + VOX] = centre[...]
    shifts[1, :, PLANE + VOX :] = east[...]
    for x in range(BS + 2):
        at = slice(x * PLANE, (x + 1) * PLANE)
        plane = shifts[1, :, at]
        low = south[:, x * BS : (x + 1) * BS]
        high = north[:, x * BS : (x + 1) * BS]
        shifts[0, :, at] = jnp.concatenate([low, plane[:, : PLANE - BS]], 1)
        shifts[2, :, at] = jnp.concatenate([plane[:, BS:], high], 1)


def columns(shifts, first, width):
    pieces = []
    for a in range(3):
        for b in range(3):
            start = first + a * PLANE
            pieces.append(shifts[b, :, start : start + width])
    return jnp.concatenate(pieces, 0)


def conv_kernel(centre, west, east, south, north, mat, occ, out, shifts):
    build_shifts(centre, west, east, south, north, shifts)
    width = 1024
    z = lax.broadcasted_iota(jnp.int32, (1, width), 1) % BS
    for first in range(0, VOX, width):
        spread = jnp.dot(mat[...], columns(shifts, first, width), preferred_element_type=F32)
        low = pltpu.roll(spread[:C], 1, 1)
        high = pltpu.roll(spread[2 * C :], width - 1, 1)
        total = spread[C : 2 * C] + jnp.where(z > 0, low, 0.0) + jnp.where(z < BS - 1, high, 0.0)
        here = occ[:, first : first + width].astype(F32)
        out[:, first : first + width] = (total * here).astype(BF16)


def conv(centre, west, east, south, north, mat, occupancy):
    return pl.pallas_call(
        conv_kernel,
        out_shape=jax.ShapeDtypeStruct((C, VOX), BF16),
        in_specs=[VMEM] * 7,
        out_specs=VMEM,
        scratch_shapes=[pltpu.VMEM((3, C, VOX + 2 * PLANE), BF16)],
        compiler_params=LIMIT,
        cost_estimate=pl.CostEstimate(
            flops=2 * C * 27 * C * VOX * 2, bytes_accessed=4 << 20, transcendentals=0
        ),
    )(centre, west, east, south, north, mat, occupancy)


ROWS = 2048
LANES = 128


def weights_kernel(centre, west, east, south, north, grad, out, shifts, acc):
    build_shifts(centre, west, east, south, north, shifts)
    width = 1024
    z = lax.broadcasted_iota(jnp.int32, (1, width), 1) % BS
    for first in range(0, VOX, width):
        here = grad[:, first : first + width].astype(F32)
        up = jnp.where(z < BS - 1, pltpu.roll(here, width - 1, 1), 0.0)
        down = jnp.where(z > 0, pltpu.roll(here, 1, 1), 0.0)
        stacked = jnp.concatenate([up, here, down], 0).astype(BF16)
        part = lax.dot_general(
            stacked,
            columns(shifts, first, width),
            (((1,), (1,)), ((), ())),
            preferred_element_type=F32,
        )
        if first == 0:
            acc[:, : 9 * C] = part
            acc[:, 9 * C :] = jnp.zeros((3 * C, 7 * LANES - 9 * C), F32)
        else:
            acc[:, : 9 * C] += part
    for tile in range(7):
        out[tile * 3 * C : (tile + 1) * 3 * C, :] = acc[:, tile * LANES : (tile + 1) * LANES]
    out[7 * 3 * C :, :] = jnp.zeros((ROWS - 21 * C, LANES), F32)


def weight_partial(centre, west, east, south, north, grad):
    return pl.pallas_call(
        weights_kernel,
        out_shape=jax.ShapeDtypeStruct((ROWS, LANES), F32),
        in_specs=[VMEM] * 6,
        out_specs=VMEM,
        scratch_shapes=[
            pltpu.VMEM((3, C, VOX + 2 * PLANE), BF16),
            pltpu.VMEM((3 * C, 7 * LANES), F32),
        ],
        compiler_params=LIMIT,
        cost_estimate=pl.CostEstimate(
            flops=2 * C * 27 * C * VOX * 2, bytes_accessed=4 << 20, transcendentals=0
        ),
    )(centre, west, east, south, north, grad)


def sum_everywhere(part):
    gx = lax.axis_index("gx")
    core, chip = gx % 2, gx // 2
    low, high = part[: ROWS // 2], part[ROWS // 2 :]
    mine = jnp.where(core == 0, low, high)
    theirs = jnp.where(core == 0, high, low)
    total = mine + swap(theirs, "gx", 1)
    total = total.reshape(8, LANES, LANES)

    def slot(index):
        return lax.dynamic_index_in_dim(total, index, 0, keepdims=False)

    got = [swap(slot(chip ^ k).astype(BF16), "gx", 2 * k) for k in range(1, 8)]
    own = slot(chip)
    for piece in got:
        own = own + piece.astype(F32)
    for step in (1, 4):
        got = [swap(own, "gy", step * k) for k in (1, 2, 3)]
        own = (own + got[0]) + (got[1] + got[2])
    own = own.astype(BF16)
    got = [own] + [swap(own, "gx", 2 * k) for k in range(1, 8)]
    half = jnp.zeros((8, LANES, LANES), BF16)
    for k in range(8):
        half = lax.dynamic_update_index_in_dim(half, got[k], chip ^ k, 0)
    half = half.reshape(ROWS // 2, LANES)
    other = swap(half, "gx", 1)
    low = jnp.where(core == 0, half, other)
    high = jnp.where(core == 0, other, half)
    return jnp.concatenate([low, high], 0)


def body(features, weight, occupancy, adjacency, cotangent):
    occupancy = occupancy.reshape(1, VOX)
    near = adjacency.reshape(6) == 0
    features = features.reshape(C, VOX)
    cotangent = cotangent.reshape(C, VOX)
    f, g, f_low, f_high, g_low, g_high = prepare(features, cotangent, occupancy)

    def kept(layer, face):
        return jnp.where(near[face], layer, jnp.zeros_like(layer))

    west = kept(shifted(f[:, VOX - PLANE :], "gx", 1), 0)
    east = kept(shifted(f[:, :PLANE], "gx", -1), 1)
    edge = PLANE - BS
    send_high = jnp.concatenate([west[:, edge:], f_high, east[:, edge:]], 1)
    send_low = jnp.concatenate([west[:, :BS], f_low, east[:, :BS]], 1)
    south = kept(shifted(send_high, "gy", 1), 2)
    north = kept(shifted(send_low, "gy", -1), 3)

    part = weight_partial(f, west, east, south, north, g)
    summed = sum_everywhere(part)

    taps = weight.reshape(C, 9, 3, C)
    mat = taps.transpose(2, 0, 1, 3).reshape(3 * C, 9 * C)
    outputs = conv(f, west, east, south, north, mat, occupancy)

    g_south = kept(shifted(g_high, "gy", 1), 2)
    g_north = kept(shifted(g_low, "gy", -1), 3)
    send_high = jnp.concatenate([g_south[:, edge:], g[:, VOX - PLANE :], g_north[:, edge:]], 1)
    send_low = jnp.concatenate([g_south[:, :BS], g[:, :PLANE], g_north[:, :BS]], 1)
    g_west = kept(shifted(send_high, "gx", 1), 0)
    g_east = kept(shifted(send_low, "gx", -1), 1)
    last = PLANE + BS
    g_south = jnp.concatenate([g_west[:, :BS], g_south, g_east[:, :BS]], 1)
    g_north = jnp.concatenate([g_west[:, last:], g_north, g_east[:, last:]], 1)
    back = taps[:, ::-1, ::-1].transpose(2, 3, 1, 0).reshape(3 * C, 9 * C)
    feature_grad = conv(
        g, g_west[:, BS:last], g_east[:, BS:last], g_south, g_north, back, occupancy
    )

    slot_count = lax.axis_size("gx") * lax.axis_size("gy") * VOX
    scale = 1.0 / math.sqrt(slot_count)
    tiles = summed[: 21 * C].reshape(7, 3, C, LANES).astype(F32) * scale
    wide = tiles.transpose(2, 1, 0, 3).reshape(C, 3, 7 * LANES)[:, :, : 9 * C]
    weight_grad = wide.reshape(C, 3, 9, C).transpose(0, 2, 1, 3).reshape(C, 27 * C)
    out_shape = (1, 1, 1, C, VOX)
    return (outputs.reshape(out_shape), feature_grad.reshape(out_shape), weight_grad)


def solution(mesh):
    placed = (
        P("gx", "gy", None, None, None),
        P(),
        P("gx", "gy", None, None),
        P("gx", "gy", None, None),
        P("gx", "gy", None, None, None),
    )
    return jax.shard_map(
        body,
        mesh=mesh,
        in_specs=placed,
        out_specs=(P("gx", "gy", None, None, None), P("gx", "gy", None, None, None), P()),
        check_vma=False,
    )
```

time: 475 us -> 128 us (0.27); the launches traced: 465 us -> 127 us
  waiting for transfers between devices: 218 us -> 21.4 us
  local copies, waits for them, and re-layouts: 117 us -> 17.4 us
  matrix products: 50.7 us -> 0 us
  starting transfers between devices: 27.4 us -> 69.8 us
  other arithmetic: 32.8 us -> 6.49 us
  between operations: 18.6 us -> 1.1 us
  Pallas kernels: 0 us -> 10.8 us
    psum x1 -> x0, waiting for transfers between devices: 218 us -> none  [body(): summed_grad = lax.psum(partial_value, ('gx', 'gy'))]
    concatenate x8 -> x0, local copies, waits for them, and re-layouts: 84.6 us -> none  [tap_columns(): return jnp.concatenate(pieces, 1)]
    dot_general x12 -> x0, matrix products: 50.7 us -> none  [the longest x4 19.8 us: forward_and_weights(): jnp.einsum('or,brm->bom', weight, columns, preferred_element_type=jnp.flo...]
    ppermute x0 -> x22, starting transfers between devices: none -> 45.8 us  [swap(): lax.ppermute(array, axis, [(i, i ^ mask) for i in range(lax.axis_size(axi...]
    slice x12, local copies, waits for them, and re-layouts: 26.1 us -> 2.35 us  [the longest x1 0.64 us: body(): east = kept(shifted(f[:, :PLANE], 'gx', -1), 1)]
    ppermute x0 -> x22, waiting for transfers between devices: none -> 16.7 us  [swap(): lax.ppermute(array, axis, [(i, i ^ mask) for i in range(lax.axis_size(axi...]
    concatenate x6 -> x5, other arithmetic: 13.2 us -> 0.5 us  [the longest x1 0.12 us: body(): g_south = jnp.concatenate([g_west[:, :BS], g_south, g_east[:, :BS]], 1)]
    pallas_call x0 -> x4, Pallas kernels: none -> 10.8 us  [the longest x2 7.5 us: conv(): pl.pallas_call(conv_kernel, out_shape=jax.ShapeDtypeStruct((C, VOX), BF16...]
  transfers between devices with their start and end apart: 9 -> 30, of which waited for: 1 -> 10; matrix products, arithmetic and copies ran while one was open for 41% -> 13% of each run, Pallas kernels for 0% -> 6%
where the time goes in v1:
time: 128 us; the launch traced here: 127 us
  starting transfers between devices  69.8 us (55%)
  waiting for transfers between devices  21.4 us (17%)
  local copies, waits for them, and re-layouts  17.4 us (14%)
  Pallas kernels  10.8 us (8%)
  other arithmetic  6.49 us (5%)
    ppermute x22, starting transfers between devices, swap(): lax.ppermute(array, axis, [(i, i ^ mask) for i in range(lax.axis_size(axi...  45.8 us
    ppermute x8, starting transfers between devices, shifted(): return lax.ppermute(array, axis, pairs)  23.9 us
    ppermute x22, waiting for transfers between devices, swap(): lax.ppermute(array, axis, [(i, i ^ mask) for i in range(lax.axis_size(axi...  16.7 us
    pallas_call x2, Pallas kernels, conv(): pl.pallas_call(conv_kernel, out_shape=jax.ShapeDtypeStruct((C, VOX), BF16...  7.5 us
    select_n x8, other arithmetic, kept(): return jnp.where(near[face], layer, jnp.zeros_like(layer))  5.6 us
    unnamed x14, local copies, waits for them, and re-layouts  4.72 us
    ppermute x8, waiting for transfers between devices, shifted(): return lax.ppermute(array, axis, pairs)  4.68 us
    reshape x2, local copies, waits for them, and re-layouts, body(): back = taps[:, ::-1, ::-1].transpose(2, 3, 1, 0).reshape(3 * C, 9 * C)  4.42 us
  transfers between devices with their start and end apart: 30, of which 10 were waited for; matrix products, arithmetic and copies ran while one was open for 13% of the time, Pallas kernels for 6%

profile of v1, /device:TPU:1, one launch (start us, length us, event | category | flops | bytes accessed | tf_op | source)
XLA Modules:
  0.0 127.0 jit_solution(1973358524611069591)
XLA Ops:
  0.7 1.1 copy-done
  1.8 1.1 copy-done.1
  2.9 0.7 copy-done.2
  3.6 0.5 shard_map.76
  4.2 6.1 %collective-permute-start.4 = (bf16[96,256]{1,0:T(8,128)(2,1)S(1)}, bf16[96,256]{1,0:T(8,128)(2,1)}, u32[]{:S(2)}, u32[]{:S(2)}) collective-permute-start(bf16[96,256]{1,0:T(8,128)(2,1)S(1)} %get-tuple-element.13), channel_id=1, source_target_pairs={{0,1},{1,2},{2,3},{3,4},{4,5},{5,6},{6,7},{7,8},{8,9},{9,10},{10,1... | collective-permute-start | bytes 147464 | tf_op jit(solution)/shard_map/ppermute | solution.py:23
  10.3 1.3 %collective-permute-start.5 = (bf16[96,256]{1,0:T(8,128)(2,1)S(1)}, bf16[96,256]{1,0:T(8,128)(2,1)}, u32[]{:S(2)}, u32[]{:S(2)}) collective-permute-start(bf16[96,256]{1,0:T(8,128)(2,1)S(1)} %get-tuple-element.14), channel_id=1, source_target_pairs={{1,0},{2,1},{3,2},{4,3},{5,4},{6,5},{7,6},{8,7},{9,8},{10,9},{11,1... | collective-permute-start | bytes 147464 | tf_op jit(solution)/shard_map/ppermute | solution.py:23
  11.6 0.6 fusion.14
  12.2 2.9 %collective-permute-start.1 = (bf16[96,256]{1,0:T(8,128)(2,1)}, bf16[96,256]{1,0:T(8,128)(2,1)}, u32[]{:S(2)}, u32[]{:S(2)}) collective-permute-start(bf16[96,256]{1,0:T(8,128)(2,1)} %get-tuple-element.22), channel_id=1, source_target_pairs={{16,0},{32,16},{48,32},{64,48},{80,64},{96,80},{112,96},{128,112},... | collective-permute-start | bytes 147464 | tf_op jit(solution)/shard_map/ppermute | solution.py:23
  15.1 2.7 %collective-permute-start = (bf16[96,256]{1,0:T(8,128)(2,1)}, bf16[96,256]{1,0:T(8,128)(2,1)S(1)}, u32[]{:S(2)}, u32[]{:S(2)}) collective-permute-start(bf16[96,256]{1,0:T(8,128)(2,1)} %get-tuple-element.23), channel_id=1, source_target_pairs={{0,16},{16,32},{32,48},{48,64},{64,80},{80,96},{96,112},{112,128},... | collective-permute-start | bytes 147464 | tf_op jit(solution)/shard_map/ppermute | solution.py:23
  17.8 0.3 copy.10
  18.2 0.9 reverse_bitcast_fusion
  19.1 0.6 fusion.21
  19.7 2.5 %copy.20 = bf16[3,96,9,96]{3,2,1,0:T(8,128)(2,1)} copy(bf16[3,96,9,96]{3,1,0,2:T(8,128)(2,1)} %reverse_bitcast_fusion) | data formatting | bytes 995328 | tf_op jit(solution)/shard_map/reshape | solution.py:221
  22.2 1.9 %reshape.81.mat = bf16[288,864]{1,0:T(8,128)(2,1)S(1)} reshape(bf16[3,96,9,96]{3,2,1,0:T(8,128)(2,1)} %copy.20) | data formatting | bytes 995328 | tf_op jit(solution)/shard_map/reshape | solution.py:221
  24.1 2.0 %copy.19 = bf16[3,96,9,96]{3,2,1,0:T(8,128)(2,1)} copy(bf16[3,96,9,96]{1,3,0,2:T(8,128)(2,1)S(1)} %bitcast.79) | data formatting | bytes 995328 | tf_op jit(solution)/shard_map/reshape | solution.py:209
  26.1 1.9 %reshape.80.mat = bf16[288,864]{1,0:T(8,128)(2,1)S(1)} reshape(bf16[3,96,9,96]{3,2,1,0:T(8,128)(2,1)} %copy.19) | data formatting | bytes 995328 | tf_op jit(solution)/shard_map/reshape | solution.py:209
  28.1 0.6 broadcast_select_fusion.7
  28.9 0.6 broadcast_select_fusion.6
  29.5 1.4 %broadcast_select_fusion.8.east = bf16[96,256]{1,0:T(8,128)(2,1)S(1)} fusion(bf16[96,256]{1,0:T(8,128)(2,1)} %collective-permute-done.1, pred[]{:T(512)} %bitcast.4), kind=kLoop, calls=%fused_computation.36 | loop fusion | flops 24576 | bytes 98305 | tf_op jit(solution)/shard_map/jit(_where)/select_n | solution.py:195
  31.0 0.6 broadcast_select_fusion.9.west
  31.8 5.0 %collective-permute-start.2 = (bf16[96,288]{1,0:T(8,128)(2,1)S(1)}, bf16[96,288]{1,0:T(8,128)(2,1)S(1)}, u32[]{:S(2)}, u32[]{:S(2)}) collective-permute-start(bf16[96,288]{1,0:T(8,128)(2,1)S(1)} %pad_maximum_fusion.1), channel_id=1, source_target_pairs={{0,1},{1,2},{2,3},{3,4},{4,5},{5,6},{6,7},{7,8},{8,9},{9,10},{10,1... | collective-permute-start | bytes 165896 | tf_op jit(solution)/shard_map/ppermute | solution.py:23
  36.9 1.3 %collective-permute-start.3 = (bf16[96,288]{1,0:T(8,128)(2,1)S(1)}, bf16[96,288]{1,0:T(8,128)(2,1)S(1)}, u32[]{:S(2)}, u32[]{:S(2)}) collective-permute-start(bf16[96,288]{1,0:T(8,128)(2,1)S(1)} %pad_maximum_fusion.2), channel_id=1, source_target_pairs={{1,0},{2,1},{3,2},{4,3},{5,4},{6,5},{7,6},{8,7},{9,8},{10,9},{11,1... | collective-permute-start | bytes 165896 | tf_op jit(solution)/shard_map/ppermute | solution.py:23
  38.2 0.6 broadcast_select_fusion.5.south
  38.9 4.7 %collective-permute-done.3 = bf16[96,288]{1,0:T(8,128)(2,1)S(1)} collective-permute-done((bf16[96,288]{1,0:T(8,128)(2,1)S(1)}, bf16[96,288]{1,0:T(8,128)(2,1)S(1)}, u32[]{:S(2)}, u32[]{:S(2)}) %collective-permute-start.3) | collective-permute-done | bytes 55328 | tf_op jit(solution)/shard_map/ppermute | solution.py:23
  43.5 0.6 broadcast_select_fusion.4.north
  44.1 2.8 %shard_map.79 = f32[2048,128]{1,0:T(8,128)S(1)} custom-call(bf16[96,4096]{1,0:T(8,128)(2,1)S(1)} %get-tuple-element.9.centre, bf16[96,256]{1,0:T(8,128)(2,1)S(1)} %broadcast_select_fusion.9.west, bf16[96,256]{1,0:T(8,128)(2,1)S(1)} %broadcast_select_fusion.8.east, bf16[96,288]{1,0:T(8,128)(2,1)S(1)} %broadcast_select_fusion.5.south, ...), custom_call_target="tpu_custom_call" | custom-call | flops 4076863488 | bytes 4194304 | tf_op jit(solution)/shard_map/pallas_call | solution.py:140
  47.0 2.0 %collective-permute-start.8 = (f32[1024,128]{1,0:T(8,128)S(1)}, f32[1024,128]{1,0:T(8,128)S(1)}, u32[]{:S(2)}, u32[]{:S(2)}) collective-permute-start(f32[1024,128]{1,0:T(8,128)S(1)} %slice_select_fusion), channel_id=1, source_target_pairs={{0,16},{16,0},{32,48},{48,32},{64,80},{80,64},{96,112},{112,96},{1... | collective-permute-start | bytes 1572872 | tf_op jit(solution)/shard_map/ppermute | solution.py:27
  49.0 2.8 %collective-permute-start.6 = (bf16[96,288]{1,0:T(8,128)(2,1)S(1)}, bf16[96,288]{1,0:T(8,128)(2,1)S(1)}, u32[]{:S(2)}, u32[]{:S(2)}) collective-permute-start(bf16[96,288]{1,0:T(8,128)(2,1)S(1)} %pad_maximum_fusion.3), channel_id=1, source_target_pairs={{0,16},{16,32},{32,48},{48,64},{64,80},{80,96},{96,112},{112,128},... | collective-permute-start | bytes 165896 | tf_op jit(solution)/shard_map/ppermute | solution.py:23
  52.0 1.9 %collective-permute-start.7 = (bf16[96,288]{1,0:T(8,128)(2,1)S(1)}, bf16[96,288]{1,0:T(8,128)(2,1)S(1)}, u32[]{:S(2)}, u32[]{:S(2)}) collective-permute-start(bf16[96,288]{1,0:T(8,128)(2,1)S(1)} %pad_maximum_fusion.4), channel_id=1, source_target_pairs={{16,0},{32,16},{48,32},{64,48},{80,64},{96,80},{112,96},{128,112},... | collective-permute-start | bytes 165896 | tf_op jit(solution)/shard_map/ppermute | solution.py:23
  53.9 3.8 %shard_map.77 = bf16[96,4096]{1,0:T(8,128)(2,1)} custom-call(bf16[96,4096]{1,0:T(8,128)(2,1)S(1)} %get-tuple-element.9.centre, bf16[96,256]{1,0:T(8,128)(2,1)S(1)} %broadcast_select_fusion.9.west, bf16[96,256]{1,0:T(8,128)(2,1)S(1)} %broadcast_select_fusion.8.east, bf16[96,288]{1,0:T(8,128)(2,1)S(1)} %broadcast_select_fusion.5.south, ...), custom_call_target="tpu_custom_call" | custom-call | flops 4076863488 | bytes 4194304 | tf_op jit(solution)/shard_map/pallas_call | solution.py:97
  57.8 1.9 %collective-permute-start.9 = (bf16[128,128]{1,0:T(8,128)(2,1)S(1)}, bf16[128,128]{1,0:T(8,128)(2,1)S(1)}, u32[]{:S(2)}, u32[]{:S(2)}) collective-permute-start(bf16[128,128]{1,0:T(8,128)(2,1)S(1)} %get-tuple-element.26), channel_id=1, source_target_pairs={{0,32},{16,48},{32,0},{48,16},{64,96},{80,112},{96,64},{112,80},{1... | collective-permute-start | bytes 98312 | tf_op jit(solution)/shard_map/ppermute | solution.py:27
  59.8 2.2 %collective-permute-start.15 = (bf16[128,128]{1,0:T(8,128)(2,1)S(1)}, bf16[128,128]{1,0:T(8,128)(2,1)S(1)}, u32[]{:S(2)}, u32[]{:S(2)}) collective-permute-start(bf16[128,128]{1,0:T(8,128)(2,1)S(1)} %get-tuple-element.27), channel_id=1, source_target_pairs={{0,224},{16,240},{32,192},{48,208},{64,160},{80,176},{96,128},{112... | collective-permute-start | bytes 98312 | tf_op jit(solution)/shard_map/ppermute | solution.py:27
  62.0 0.6 broadcast_select_fusion.3
  62.6 0.4 collective-permute-start.14
  63.0 2.7 %collective-permute-start.13 = (bf16[128,128]{1,0:T(8,128)(2,1)S(1)}, bf16[128,128]{1,0:T(8,128)(2,1)S(1)}, u32[]{:S(2)}, u32[]{:S(2)}) collective-permute-start(bf16[128,128]{1,0:T(8,128)(2,1)S(1)} %get-tuple-element.29), channel_id=1, source_target_pairs={{0,160},{16,176},{32,128},{48,144},{64,224},{80,240},{96,192},{112... | collective-permute-start | bytes 98312 | tf_op jit(solution)/shard_map/ppermute | solution.py:27
  65.7 1.3 %collective-permute-start.12 = (bf16[128,128]{1,0:T(8,128)(2,1)S(1)}, bf16[128,128]{1,0:T(8,128)(2,1)S(1)}, u32[]{:S(2)}, u32[]{:S(2)}) collective-permute-start(bf16[128,128]{1,0:T(8,128)(2,1)S(1)} %get-tuple-element.30), channel_id=1, source_target_pairs={{0,128},{16,144},{32,160},{48,176},{64,192},{80,208},{96,224},{112... | collective-permute-start | bytes 98312 | tf_op jit(solution)/shard_map/ppermute | solution.py:27
  67.0 0.2 collective-permute-start.11
  67.2 1.1 collective-permute-start.10
  68.3 0.6 broadcast_select_fusion.2
  69.0 1.1 collective-permute-done.12
  70.1 0.9 collective-permute-done.11
  71.0 6.2 %collective-permute-start.18 = (f32[128,128]{1,0:T(8,128)S(1)}, f32[128,128]{1,0:T(8,128)S(1)}, u32[]{:S(2)}, u32[]{:S(2)}) collective-permute-start(f32[128,128]{1,0:T(8,128)S(1)} %fusion.5), channel_id=1, source_target_pairs={{0,3},{1,2},{2,1},{3,0},{4,7},{5,6},{6,5},{7,4},{8,11},{9,10},{10,... | collective-permute-start | bytes 196616 | tf_op jit(solution)/shard_map/ppermute | solution.py:27
  77.2 0.4 collective-permute-start.16
  77.6 1.2 collective-permute-done.18
  78.8 1.5 %collective-permute-done.17 = f32[128,128]{1,0:T(8,128)S(1)} collective-permute-done((f32[128,128]{1,0:T(8,128)S(1)}, f32[128,128]{1,0:T(8,128)S(1)}, u32[]{:S(2)}, u32[]{:S(2)}) %collective-permute-start.17) | collective-permute-done | bytes 65568 | tf_op jit(solution)/shard_map/ppermute | solution.py:27
  80.3 1.8 %collective-permute-done.16 = f32[128,128]{1,0:T(8,128)S(1)} collective-permute-done((f32[128,128]{1,0:T(8,128)S(1)}, f32[128,128]{1,0:T(8,128)S(1)}, u32[]{:S(2)}, u32[]{:S(2)}) %collective-permute-start.16) | collective-permute-done | bytes 65568 | tf_op jit(solution)/shard_map/ppermute | solution.py:27
  82.1 4.8 %collective-permute-start.21 = (f32[128,128]{1,0:T(8,128)S(1)}, f32[128,128]{1,0:T(8,128)S(1)}, u32[]{:S(2)}, u32[]{:S(2)}) collective-permute-start(f32[128,128]{1,0:T(8,128)S(1)} %add_add_fusion), channel_id=1, source_target_pairs={{0,12},{1,13},{2,14},{3,15},{4,8},{5,9},{6,10},{7,11},{8,4},{9,5},... | collective-permute-start | bytes 196616 | tf_op jit(solution)/shard_map/ppermute | solution.py:27
  86.9 5.1 %collective-permute-start.20 = (f32[128,128]{1,0:T(8,128)S(1)}, f32[128,128]{1,0:T(8,128)S(1)}, u32[]{:S(2)}, u32[]{:S(2)}) collective-permute-start(f32[128,128]{1,0:T(8,128)S(1)} %add_add_fusion), channel_id=1, source_target_pairs={{0,8},{1,9},{2,10},{3,11},{4,12},{5,13},{6,14},{7,15},{8,0},{9,1},... | collective-permute-start | bytes 196616 | tf_op jit(solution)/shard_map/ppermute | solution.py:27
  92.1 2.0 %collective-permute-done.20 = f32[128,128]{1,0:T(8,128)S(1)} collective-permute-done((f32[128,128]{1,0:T(8,128)S(1)}, f32[128,128]{1,0:T(8,128)S(1)}, u32[]{:S(2)}, u32[]{:S(2)}) %collective-permute-start.20) | collective-permute-done | bytes 65568 | tf_op jit(solution)/shard_map/ppermute | solution.py:27
  94.0 3.4 %collective-permute-done.19 = f32[128,128]{1,0:T(8,128)S(1)} collective-permute-done((f32[128,128]{1,0:T(8,128)S(1)}, f32[128,128]{1,0:T(8,128)S(1)}, u32[]{:S(2)}, u32[]{:S(2)}) %collective-permute-start.19) | collective-permute-done | bytes 65568 | tf_op jit(solution)/shard_map/ppermute | solution.py:27
  97.5 0.3 collective-permute-start.22
  98.0 1.7 %collective-permute-start.27 = (bf16[128,128]{1,0:T(8,128)(2,1)S(1)}, bf16[128,128]{1,0:T(8,128)(2,1)S(1)}, u32[]{:S(2)}, u32[]{:S(2)}) collective-permute-start(bf16[128,128]{1,0:T(8,128)(2,1)S(1)} %get-tuple-element.19), channel_id=1, source_target_pairs={{0,192},{16,208},{32,224},{48,240},{64,128},{80,144},{96,160},{112... | collective-permute-start | bytes 98312 | tf_op jit(solution)/shard_map/ppermute | solution.py:27
  99.8 1.7 %collective-permute-start.26 = (bf16[128,128]{1,0:T(8,128)(2,1)S(1)}, bf16[128,128]{1,0:T(8,128)(2,1)S(1)}, u32[]{:S(2)}, u32[]{:S(2)}) collective-permute-start(bf16[128,128]{1,0:T(8,128)(2,1)S(1)} %get-tuple-element.19), channel_id=1, source_target_pairs={{0,160},{16,176},{32,128},{48,144},{64,224},{80,240},{96,192},{112... | collective-permute-start | bytes 98312 | tf_op jit(solution)/shard_map/ppermute | solution.py:27
  101.5 2.4 %collective-permute-start.25 = (bf16[128,128]{1,0:T(8,128)(2,1)S(1)}, bf16[128,128]{1,0:T(8,128)(2,1)S(1)}, u32[]{:S(2)}, u32[]{:S(2)}) collective-permute-start(bf16[128,128]{1,0:T(8,128)(2,1)S(1)} %get-tuple-element.19), channel_id=1, source_target_pairs={{0,128},{16,144},{32,160},{48,176},{64,192},{80,208},{96,224},{112... | collective-permute-start | bytes 98312 | tf_op jit(solution)/shard_map/ppermute | solution.py:27
  103.9 1.2 collective-permute-start.23
  105.1 1.8 %collective-permute-done.23 = bf16[128,128]{1,0:T(8,128)(2,1)S(1)} collective-permute-done((bf16[128,128]{1,0:T(8,128)(2,1)S(1)}, bf16[128,128]{1,0:T(8,128)(2,1)S(1)}, u32[]{:S(2)}, u32[]{:S(2)}) %collective-permute-start.23) | collective-permute-done | bytes 32800 | tf_op jit(solution)/shard_map/ppermute | solution.py:27
  107.0 1.7 %collective-permute-start.28 = (bf16[128,128]{1,0:T(8,128)(2,1)S(1)}, bf16[128,128]{1,0:T(8,128)(2,1)S(1)}, u32[]{:S(2)}, u32[]{:S(2)}) collective-permute-start(bf16[128,128]{1,0:T(8,128)(2,1)S(1)} %get-tuple-element.19), channel_id=1, source_target_pairs={{0,224},{16,240},{32,192},{48,208},{64,160},{80,176},{96,128},{112... | collective-permute-start | bytes 98312 | tf_op jit(solution)/shard_map/ppermute | solution.py:27
  108.8 3.0 %collective-permute-done.28 = bf16[128,128]{1,0:T(8,128)(2,1)S(1)} collective-permute-done((bf16[128,128]{1,0:T(8,128)(2,1)S(1)}, bf16[128,128]{1,0:T(8,128)(2,1)S(1)}, u32[]{:S(2)}, u32[]{:S(2)}) %collective-permute-start.28) | collective-permute-done | bytes 32800 | tf_op jit(solution)/shard_map/ppermute | solution.py:27
  111.9 8.5 %collective-permute-start.29 = (bf16[1024,128]{1,0:T(8,128)(2,1)S(1)}, bf16[1024,128]{1,0:T(8,128)(2,1)S(1)}, u32[]{:S(2)}, u32[]{:S(2)}) collective-permute-start(bf16[1024,128]{1,0:T(8,128)(2,1)S(1)} %bitcast.87), channel_id=1, source_target_pairs={{0,16},{16,0},{32,48},{48,32},{64,80},{80,64},{96,112},{112,96},{1... | collective-permute-start | bytes 786440 | tf_op jit(solution)/shard_map/ppermute | solution.py:27
  120.4 3.7 %shard_map.78 = bf16[96,4096]{1,0:T(8,128)(2,1)} custom-call(bf16[96,4096]{1,0:T(8,128)(2,1)S(1)} %get-tuple-element.12.centre.grad, bf16[96,256]{1,0:T(8,128)(2,1)S(1)} %slice.118.west, bf16[96,256]{1,0:T(8,128)(2,1)S(1)} %slice.121.east, bf16[96,288]{1,0:T(8,128)(2,1)S(1)} %get-tuple-element.49.south, bf16[96,288]{1,0:T(8,128)(2,1)S(1)} %get-tuple-element.50.north, ...), custom_call_target="tpu_custom_call" | custom-call | flops 4076863488 | bytes 4194304 | tf_op jit(solution)/shard_map/pallas_call | solution.py:97
  124.3 0.6 copy.24
  124.9 0.2 reshape.77
  125.1 0.4 copy.16
  125.6 1.4 %copy.18 = f32[96,2592]{1,0:T(8,128)} copy(f32[96,2592]{0,1:T(8,128)S(1)} %bitcast.81) | data formatting | bytes 1990656
  (64 shorter events, 1.9 us)
Async XLA Ops:
  0.6 17.2 %copy-start.5 = (s32[1,1,1,6]{3,2,1,0:T(1,128)S(1)}, s32[1,1,1,6]{3,2,1,0:T(1,128)}, u32[]{:S(2)}) copy-start(s32[1,1,1,6]{3,2,1,0:T(1,128)} %param.8) | copy-start | bytes 76
  0.6 1.1 copy-start
  1.8 1.1 copy-start.1
  2.9 0.7 copy-start.2
  3.6 14.2 %copy-start.4 = (bf16[96,2592]{1,0:T(8,128)(2,1)S(1)}, bf16[96,2592]{1,0:T(8,128)(2,1)}, u32[]{:S(2)}) copy-start(bf16[96,2592]{1,0:T(8,128)(2,1)} %param.6) | copy-start | bytes 1492996
  4.2 24.0 %collective-permute-start.4 = (bf16[96,256]{1,0:T(8,128)(2,1)S(1)}, bf16[96,256]{1,0:T(8,128)(2,1)}, u32[]{:S(2)}, u32[]{:S(2)}) collective-permute-start(bf16[96,256]{1,0:T(8,128)(2,1)S(1)} %get-tuple-element.13), channel_id=1, source_target_pairs={{0,1},{1,2},{2,3},{3,4},{4,5},{5,6},{6,7},{7,8},{8,9},{9,10},{10,1... | collective-permute-start | bytes 147464 | tf_op jit(solution)/shard_map/ppermute | solution.py:23
  10.3 18.6 %collective-permute-start.5 = (bf16[96,256]{1,0:T(8,128)(2,1)S(1)}, bf16[96,256]{1,0:T(8,128)(2,1)}, u32[]{:S(2)}, u32[]{:S(2)}) collective-permute-start(bf16[96,256]{1,0:T(8,128)(2,1)S(1)} %get-tuple-element.14), channel_id=1, source_target_pairs={{1,0},{2,1},{3,2},{4,3},{5,4},{6,5},{7,6},{8,7},{9,8},{10,9},{11,1... | collective-permute-start | bytes 147464 | tf_op jit(solution)/shard_map/ppermute | solution.py:23
  12.2 17.3 %collective-permute-start.1 = (bf16[96,256]{1,0:T(8,128)(2,1)}, bf16[96,256]{1,0:T(8,128)(2,1)}, u32[]{:S(2)}, u32[]{:S(2)}) collective-permute-start(bf16[96,256]{1,0:T(8,128)(2,1)} %get-tuple-element.22), channel_id=1, source_target_pairs={{16,0},{32,16},{48,32},{64,48},{80,64},{96,80},{112,96},{128,112},... | collective-permute-start | bytes 147464 | tf_op jit(solution)/shard_map/ppermute | solution.py:23
  15.1 16.0 %collective-permute-start = (bf16[96,256]{1,0:T(8,128)(2,1)}, bf16[96,256]{1,0:T(8,128)(2,1)S(1)}, u32[]{:S(2)}, u32[]{:S(2)}) collective-permute-start(bf16[96,256]{1,0:T(8,128)(2,1)} %get-tuple-element.23), channel_id=1, source_target_pairs={{0,16},{16,32},{32,48},{48,64},{64,80},{80,96},{96,112},{112,128},... | collective-permute-start | bytes 147464 | tf_op jit(solution)/shard_map/ppermute | solution.py:23
  31.8 6.4 %collective-permute-start.2 = (bf16[96,288]{1,0:T(8,128)(2,1)S(1)}, bf16[96,288]{1,0:T(8,128)(2,1)S(1)}, u32[]{:S(2)}, u32[]{:S(2)}) collective-permute-start(bf16[96,288]{1,0:T(8,128)(2,1)S(1)} %pad_maximum_fusion.1), channel_id=1, source_target_pairs={{0,1},{1,2},{2,3},{3,4},{4,5},{5,6},{6,7},{7,8},{8,9},{9,10},{10,1... | collective-permute-start | bytes 165896 | tf_op jit(solution)/shard_map/ppermute | solution.py:23
  36.9 6.6 %collective-permute-start.3 = (bf16[96,288]{1,0:T(8,128)(2,1)S(1)}, bf16[96,288]{1,0:T(8,128)(2,1)S(1)}, u32[]{:S(2)}, u32[]{:S(2)}) collective-permute-start(bf16[96,288]{1,0:T(8,128)(2,1)S(1)} %pad_maximum_fusion.2), channel_id=1, source_target_pairs={{1,0},{2,1},{3,2},{4,3},{5,4},{6,5},{7,6},{8,7},{9,8},{10,9},{11,1... | collective-permute-start | bytes 165896 | tf_op jit(solution)/shard_map/ppermute | solution.py:23
  46.9 7.0 %copy-start.3 = (s32[1,1,1,4096]{3,2,1,0:T(1,128)S(1)}, s32[1,1,1,4096]{3,2,1,0:T(1,128)}, u32[]{:S(2)}) copy-start(s32[1,1,1,4096]{3,2,1,0:T(1,128)} %param.7) | copy-start | bytes 49156
  47.0 10.7 %collective-permute-start.8 = (f32[1024,128]{1,0:T(8,128)S(1)}, f32[1024,128]{1,0:T(8,128)S(1)}, u32[]{:S(2)}, u32[]{:S(2)}) collective-permute-start(f32[1024,128]{1,0:T(8,128)S(1)} %slice_select_fusion), channel_id=1, source_target_pairs={{0,16},{16,0},{32,48},{48,32},{64,80},{80,64},{96,112},{112,96},{1... | collective-permute-start | bytes 1572872 | tf_op jit(solution)/shard_map/ppermute | solution.py:27
  49.0 12.9 %collective-permute-start.6 = (bf16[96,288]{1,0:T(8,128)(2,1)S(1)}, bf16[96,288]{1,0:T(8,128)(2,1)S(1)}, u32[]{:S(2)}, u32[]{:S(2)}) collective-permute-start(bf16[96,288]{1,0:T(8,128)(2,1)S(1)} %pad_maximum_fusion.3), channel_id=1, source_target_pairs={{0,16},{16,32},{32,48},{48,64},{64,80},{80,96},{96,112},{112,128},... | collective-permute-start | bytes 165896 | tf_op jit(solution)/shard_map/ppermute | solution.py:23
  52.0 13.7 %collective-permute-start.7 = (bf16[96,288]{1,0:T(8,128)(2,1)S(1)}, bf16[96,288]{1,0:T(8,128)(2,1)S(1)}, u32[]{:S(2)}, u32[]{:S(2)}) collective-permute-start(bf16[96,288]{1,0:T(8,128)(2,1)S(1)} %pad_maximum_fusion.4), channel_id=1, source_target_pairs={{16,0},{32,16},{48,32},{64,48},{80,64},{96,80},{112,96},{128,112},... | collective-permute-start | bytes 165896 | tf_op jit(solution)/shard_map/ppermute | solution.py:23
  57.8 9.2 %collective-permute-start.9 = (bf16[128,128]{1,0:T(8,128)(2,1)S(1)}, bf16[128,128]{1,0:T(8,128)(2,1)S(1)}, u32[]{:S(2)}, u32[]{:S(2)}) collective-permute-start(bf16[128,128]{1,0:T(8,128)(2,1)S(1)} %get-tuple-element.26), channel_id=1, source_target_pairs={{0,32},{16,48},{32,0},{48,16},{64,96},{80,112},{96,64},{112,80},{1... | collective-permute-start | bytes 98312 | tf_op jit(solution)/shard_map/ppermute | solution.py:27
  59.8 7.4 %collective-permute-start.15 = (bf16[128,128]{1,0:T(8,128)(2,1)S(1)}, bf16[128,128]{1,0:T(8,128)(2,1)S(1)}, u32[]{:S(2)}, u32[]{:S(2)}) collective-permute-start(bf16[128,128]{1,0:T(8,128)(2,1)S(1)} %get-tuple-element.27), channel_id=1, source_target_pairs={{0,224},{16,240},{32,192},{48,208},{64,160},{80,176},{96,128},{112... | collective-permute-start | bytes 98312 | tf_op jit(solution)/shard_map/ppermute | solution.py:27
  62.6 6.4 %collective-permute-start.14 = (bf16[128,128]{1,0:T(8,128)(2,1)S(1)}, bf16[128,128]{1,0:T(8,128)(2,1)S(1)}, u32[]{:S(2)}, u32[]{:S(2)}) collective-permute-start(bf16[128,128]{1,0:T(8,128)(2,1)S(1)} %get-tuple-element.28), channel_id=1, source_target_pairs={{0,192},{16,208},{32,224},{48,240},{64,128},{80,144},{96,160},{112... | collective-permute-start | bytes 98312 | tf_op jit(solution)/shard_map/ppermute | solution.py:27
  63.0 6.0 %collective-permute-start.13 = (bf16[128,128]{1,0:T(8,128)(2,1)S(1)}, bf16[128,128]{1,0:T(8,128)(2,1)S(1)}, u32[]{:S(2)}, u32[]{:S(2)}) collective-permute-start(bf16[128,128]{1,0:T(8,128)(2,1)S(1)} %get-tuple-element.29), channel_id=1, source_target_pairs={{0,160},{16,176},{32,128},{48,144},{64,224},{80,240},{96,192},{112... | collective-permute-start | bytes 98312 | tf_op jit(solution)/shard_map/ppermute | solution.py:27
  65.7 4.4 %collective-permute-start.12 = (bf16[128,128]{1,0:T(8,128)(2,1)S(1)}, bf16[128,128]{1,0:T(8,128)(2,1)S(1)}, u32[]{:S(2)}, u32[]{:S(2)}) collective-permute-start(bf16[128,128]{1,0:T(8,128)(2,1)S(1)} %get-tuple-element.30), channel_id=1, source_target_pairs={{0,128},{16,144},{32,160},{48,176},{64,192},{80,208},{96,224},{112... | collective-permute-start | bytes 98312 | tf_op jit(solution)/shard_map/ppermute | solution.py:27
  67.0 4.0 %collective-permute-start.11 = (bf16[128,128]{1,0:T(8,128)(2,1)S(1)}, bf16[128,128]{1,0:T(8,128)(2,1)S(1)}, u32[]{:S(2)}, u32[]{:S(2)}) collective-permute-start(bf16[128,128]{1,0:T(8,128)(2,1)S(1)} %get-tuple-element.31), channel_id=1, source_target_pairs={{0,96},{16,112},{32,64},{48,80},{64,32},{80,48},{96,0},{112,16},{1... | collective-permute-start | bytes 98312 | tf_op jit(solution)/shard_map/ppermute | solution.py:27
  67.2 3.8 %collective-permute-start.10 = (bf16[128,128]{1,0:T(8,128)(2,1)S(1)}, bf16[128,128]{1,0:T(8,128)(2,1)S(1)}, u32[]{:S(2)}, u32[]{:S(2)}) collective-permute-start(bf16[128,128]{1,0:T(8,128)(2,1)S(1)} %get-tuple-element.32), channel_id=1, source_target_pairs={{0,64},{16,80},{32,96},{48,112},{64,0},{80,16},{96,32},{112,48},{1... | collective-permute-start | bytes 98312 | tf_op jit(solution)/shard_map/ppermute | solution.py:27
  71.0 7.8 %collective-permute-start.18 = (f32[128,128]{1,0:T(8,128)S(1)}, f32[128,128]{1,0:T(8,128)S(1)}, u32[]{:S(2)}, u32[]{:S(2)}) collective-permute-start(f32[128,128]{1,0:T(8,128)S(1)} %fusion.5), channel_id=1, source_target_pairs={{0,3},{1,2},{2,1},{3,0},{4,7},{5,6},{6,5},{7,4},{8,11},{9,10},{10,... | collective-permute-start | bytes 196616 | tf_op jit(solution)/shard_map/ppermute | solution.py:27
  77.2 3.1 %collective-permute-start.17 = (f32[128,128]{1,0:T(8,128)S(1)}, f32[128,128]{1,0:T(8,128)S(1)}, u32[]{:S(2)}, u32[]{:S(2)}) collective-permute-start(f32[128,128]{1,0:T(8,128)S(1)} %fusion.5), channel_id=1, source_target_pairs={{0,2},{1,3},{2,0},{3,1},{4,6},{5,7},{6,4},{7,5},{8,10},{9,11},{10,... | collective-permute-start | bytes 196616 | tf_op jit(solution)/shard_map/ppermute | solution.py:27
  77.2 4.9 %collective-permute-start.16 = (f32[128,128]{1,0:T(8,128)S(1)}, f32[128,128]{1,0:T(8,128)S(1)}, u32[]{:S(2)}, u32[]{:S(2)}) collective-permute-start(f32[128,128]{1,0:T(8,128)S(1)} %fusion.5), channel_id=1, source_target_pairs={{0,1},{1,0},{2,3},{3,2},{4,5},{5,4},{6,7},{7,6},{8,9},{9,8},{10,11... | collective-permute-start | bytes 196616 | tf_op jit(solution)/shard_map/ppermute | solution.py:27
  82.1 9.9 %collective-permute-start.21 = (f32[128,128]{1,0:T(8,128)S(1)}, f32[128,128]{1,0:T(8,128)S(1)}, u32[]{:S(2)}, u32[]{:S(2)}) collective-permute-start(f32[128,128]{1,0:T(8,128)S(1)} %add_add_fusion), channel_id=1, source_target_pairs={{0,12},{1,13},{2,14},{3,15},{4,8},{5,9},{6,10},{7,11},{8,4},{9,5},... | collective-permute-start | bytes 196616 | tf_op jit(solution)/shard_map/ppermute | solution.py:27
  86.9 7.1 %collective-permute-start.20 = (f32[128,128]{1,0:T(8,128)S(1)}, f32[128,128]{1,0:T(8,128)S(1)}, u32[]{:S(2)}, u32[]{:S(2)}) collective-permute-start(f32[128,128]{1,0:T(8,128)S(1)} %add_add_fusion), channel_id=1, source_target_pairs={{0,8},{1,9},{2,10},{3,11},{4,12},{5,13},{6,14},{7,15},{8,0},{9,1},... | collective-permute-start | bytes 196616 | tf_op jit(solution)/shard_map/ppermute | solution.py:27
  92.0 5.4 %collective-permute-start.19 = (f32[128,128]{1,0:T(8,128)S(1)}, f32[128,128]{1,0:T(8,128)S(1)}, u32[]{:S(2)}, u32[]{:S(2)}) collective-permute-start(f32[128,128]{1,0:T(8,128)S(1)} %add_add_fusion), channel_id=1, source_target_pairs={{0,4},{1,5},{2,6},{3,7},{4,0},{5,1},{6,2},{7,3},{8,12},{9,13},{10,... | collective-permute-start | bytes 196616 | tf_op jit(solution)/shard_map/ppermute | solution.py:27
  97.5 6.5 %collective-permute-start.22 = (bf16[128,128]{1,0:T(8,128)(2,1)S(1)}, bf16[128,128]{1,0:T(8,128)(2,1)S(1)}, u32[]{:S(2)}, u32[]{:S(2)}) collective-permute-start(bf16[128,128]{1,0:T(8,128)(2,1)S(1)} %get-tuple-element.19), channel_id=1, source_target_pairs={{0,32},{16,48},{32,0},{48,16},{64,96},{80,112},{96,64},{112,80},{1... | collective-permute-start | bytes 98312 | tf_op jit(solution)/shard_map/ppermute | solution.py:27
  98.0 10.7 %collective-permute-start.27 = (bf16[128,128]{1,0:T(8,128)(2,1)S(1)}, bf16[128,128]{1,0:T(8,128)(2,1)S(1)}, u32[]{:S(2)}, u32[]{:S(2)}) collective-permute-start(bf16[128,128]{1,0:T(8,128)(2,1)S(1)} %get-tuple-element.19), channel_id=1, source_target_pairs={{0,192},{16,208},{32,224},{48,240},{64,128},{80,144},{96,160},{112... | collective-permute-start | bytes 98312 | tf_op jit(solution)/shard_map/ppermute | solution.py:27
  99.8 9.0 %collective-permute-start.26 = (bf16[128,128]{1,0:T(8,128)(2,1)S(1)}, bf16[128,128]{1,0:T(8,128)(2,1)S(1)}, u32[]{:S(2)}, u32[]{:S(2)}) collective-permute-start(bf16[128,128]{1,0:T(8,128)(2,1)S(1)} %get-tuple-element.19), channel_id=1, source_target_pairs={{0,160},{16,176},{32,128},{48,144},{64,224},{80,240},{96,192},{112... | collective-permute-start | bytes 98312 | tf_op jit(solution)/shard_map/ppermute | solution.py:27
  101.5 7.3 %collective-permute-start.25 = (bf16[128,128]{1,0:T(8,128)(2,1)S(1)}, bf16[128,128]{1,0:T(8,128)(2,1)S(1)}, u32[]{:S(2)}, u32[]{:S(2)}) collective-permute-start(bf16[128,128]{1,0:T(8,128)(2,1)S(1)} %get-tuple-element.19), channel_id=1, source_target_pairs={{0,128},{16,144},{32,160},{48,176},{64,192},{80,208},{96,224},{112... | collective-permute-start | bytes 98312 | tf_op jit(solution)/shard_map/ppermute | solution.py:27
  103.9 4.8 %collective-permute-start.24 = (bf16[128,128]{1,0:T(8,128)(2,1)S(1)}, bf16[128,128]{1,0:T(8,128)(2,1)S(1)}, u32[]{:S(2)}, u32[]{:S(2)}) collective-permute-start(bf16[128,128]{1,0:T(8,128)(2,1)S(1)} %get-tuple-element.19), channel_id=1, source_target_pairs={{0,96},{16,112},{32,64},{48,80},{64,32},{80,48},{96,0},{112,16},{1... | collective-permute-start | bytes 98312 | tf_op jit(solution)/shard_map/ppermute | solution.py:27
  103.9 3.1 %collective-permute-start.23 = (bf16[128,128]{1,0:T(8,128)(2,1)S(1)}, bf16[128,128]{1,0:T(8,128)(2,1)S(1)}, u32[]{:S(2)}, u32[]{:S(2)}) collective-permute-start(bf16[128,128]{1,0:T(8,128)(2,1)S(1)} %get-tuple-element.19), channel_id=1, source_target_pairs={{0,64},{16,80},{32,96},{48,112},{64,0},{80,16},{96,32},{112,48},{1... | collective-permute-start | bytes 98312 | tf_op jit(solution)/shard_map/ppermute | solution.py:27
  107.0 4.9 %collective-permute-start.28 = (bf16[128,128]{1,0:T(8,128)(2,1)S(1)}, bf16[128,128]{1,0:T(8,128)(2,1)S(1)}, u32[]{:S(2)}, u32[]{:S(2)}) collective-permute-start(bf16[128,128]{1,0:T(8,128)(2,1)S(1)} %get-tuple-element.19), channel_id=1, source_target_pairs={{0,224},{16,240},{32,192},{48,208},{64,160},{80,176},{96,128},{112... | collective-permute-start | bytes 98312 | tf_op jit(solution)/shard_map/ppermute | solution.py:27
  111.9 12.2 %collective-permute-start.29 = (bf16[1024,128]{1,0:T(8,128)(2,1)S(1)}, bf16[1024,128]{1,0:T(8,128)(2,1)S(1)}, u32[]{:S(2)}, u32[]{:S(2)}) collective-permute-start(bf16[1024,128]{1,0:T(8,128)(2,1)S(1)} %bitcast.87), channel_id=1, source_target_pairs={{0,16},{16,0},{32,48},{48,32},{64,80},{80,64},{96,112},{112,96},{1... | collective-permute-start | bytes 786440 | tf_op jit(solution)/shard_map/ppermute | solution.py:27

commit v2 on v1

v2 whole, which is shorter than its diff:
```python
import math

import jax
import jax.numpy as jnp
from jax import lax
from jax.experimental import pallas as pl
from jax.experimental.pallas import tpu as pltpu
from jax.sharding import PartitionSpec as P

BS = 16
PLANE = BS * BS
VOX = BS**3
C = 96
F32 = jnp.float32
BF16 = jnp.bfloat16
ROWS = 2048
HALF = ROWS // 2
LANES = 128
PIECES = 6
VMEM = pl.BlockSpec(memory_space=pltpu.VMEM)
SMEM = pl.BlockSpec(memory_space=pltpu.SMEM)
HBM = pl.BlockSpec(memory_space=pltpu.HBM)
LIMIT = pltpu.CompilerParams(vmem_limit_bytes=40 << 20)


def cost(flops, moved):
    return pl.CostEstimate(flops=flops, bytes_accessed=moved, transcendentals=0)


def shifted(array, axis, by):
    size = lax.axis_size(axis)
    pairs = [(i, i + by) for i in range(size) if 0 <= i + by < size]
    return lax.ppermute(array, axis, pairs)


def swap(array, axis, mask):
    return lax.ppermute(array, axis, [(i, i ^ mask) for i in range(lax.axis_size(axis))])


def start_all(sources, targets, sems):
    copies = [
        pltpu.make_async_copy(source, target, sems.at[i])
        for i, (source, target) in enumerate(zip(sources, targets))
    ]
    for copy in copies:
        copy.start()
    return copies


def kept(layer, flag):
    return jnp.where(flag == 0, layer, jnp.zeros_like(layer))


def y_face(values, first):
    return jnp.concatenate(
        [values[:, x * PLANE + first : x * PLANE + first + BS] for x in range(BS)], 1
    )


def prepare_kernel(
    facts, feat, cot, occ, f_out, g_out, mask, x_low, x_high, y_low, y_high, f_in, g_in, occ_in, sems
):
    rows = C // PIECES
    cuts = [slice(i * rows, (i + 1) * rows) for i in range(PIECES)]
    copies = start_all(
        [occ] + [feat.at[c] for c in cuts] + [cot.at[c] for c in cuts],
        [occ_in] + [f_in.at[c] for c in cuts] + [g_in.at[c] for c in cuts],
        sems,
    )
    copies[0].wait()
    occupied = occ_in[...].astype(BF16)
    mask[...] = occ_in[...].astype(F32)
    last, edge = VOX - PLANE, PLANE - BS
    for part, source, out in ((0, f_in, f_out), (1, g_in, g_out)):
        for copy in copies[1 + part * PIECES : 1 + (part + 1) * PIECES]:
            copy.wait()
        masked = source[...] * occupied
        out[...] = masked
        to = slice(part * C, (part + 1) * C)
        low, high = masked[:, :PLANE], masked[:, last:]
        for message, plane in ((x_low, low), (x_high, high)):
            message[to, :PLANE] = plane
            edges = [kept(plane[:, :BS], facts[2]), kept(plane[:, edge:], facts[3])]
            message[to, PLANE:] = jnp.concatenate(edges, 1)
        y_low[to, :PLANE] = y_face(masked, 0)
        edges = [kept(low[:, :BS], facts[0]), kept(high[:, :BS], facts[1])]
        y_low[to, PLANE:] = jnp.concatenate(edges, 1)
        y_high[to] = y_face(masked, edge)


def prepare(facts, features, cotangent, occupancy):
    whole = jax.ShapeDtypeStruct((C, VOX), BF16)
    face = jax.ShapeDtypeStruct((2 * C, PLANE + 2 * BS), BF16)
    return pl.pallas_call(
        prepare_kernel,
        out_shape=(
            whole,
            whole,
            jax.ShapeDtypeStruct((1, VOX), F32),
            face,
            face,
            face,
            jax.ShapeDtypeStruct((2 * C, PLANE), BF16),
        ),
        in_specs=[SMEM, HBM, HBM, HBM],
        out_specs=(VMEM,) * 7,
        scratch_shapes=[
            pltpu.VMEM((C, VOX), BF16),
            pltpu.VMEM((C, VOX), BF16),
            pltpu.VMEM((1, VOX), jnp.int32),
            pltpu.SemaphoreType.DMA((1 + 2 * PIECES,)),
        ],
        compiler_params=LIMIT,
        cost_estimate=cost(2**20, 3 << 20),
    )(facts, *[pltpu.with_memory_space_constraint(x, pltpu.HBM) for x in (features, cotangent, occupancy)])


def matrices_kernel(weight, mat, back, held, sems):
    start_all([weight], [held], sems)[0].wait()
    for ab in range(9):
        for c in range(3):
            k = ab * 3 + c
            block = held[:, k * C : (k + 1) * C]
            mat[c * C : (c + 1) * C, ab * C : (ab + 1) * C] = block
            turned = block.astype(F32).T.astype(BF16)
            back[(2 - c) * C : (3 - c) * C, (8 - ab) * C : (9 - ab) * C] = turned


def matrices(weight):
    shape = jax.ShapeDtypeStruct((3 * C, 9 * C), BF16)
    return pl.pallas_call(
        matrices_kernel,
        out_shape=(shape, shape),
        in_specs=[HBM],
        out_specs=(VMEM, VMEM),
        scratch_shapes=[pltpu.VMEM((C, 27 * C), BF16), pltpu.SemaphoreType.DMA((1,))],
        compiler_params=LIMIT,
        cost_estimate=cost(2**28, 6 << 20),
    )(pltpu.with_memory_space_constraint(weight, pltpu.HBM))


def build_shifts(centre, west, east, south, north, shifts):
    shifts[1, :, :PLANE] = west
    shifts[1, :, PLANE : PLANE + VOX] = centre[...]
    shifts[1, :, PLANE + VOX :] = east
    for x in range(BS + 2):
        at = slice(x * PLANE, (x + 1) * PLANE)
        plane = shifts[1, :, at]
        shifts[0, :, at] = jnp.concatenate([south(x), plane[:, : PLANE - BS]], 1)
        shifts[2, :, at] = jnp.concatenate([plane[:, BS:], north(x)], 1)


def columns(shifts, first, width):
    pieces = []
    for a in range(3):
        for b in range(3):
            start = first + a * PLANE
            pieces.append(shifts[b, :, start : start + width])
    return jnp.concatenate(pieces, 0)


def conv_kernel(part, facts, centre, halo, from_south, from_north, mat, mask, out, south, north, shifts, sems):
    for copy in start_all([from_south, from_north], [south, north], sems):
        copy.wait()
    rows = slice(part * C, (part + 1) * C)
    if part == 0:
        pairs = [kept(south[rows, PLANE:], facts[2]), kept(north[rows], facts[3])]
    else:
        pairs = [south[rows, PLANE:], north[rows]]
    ends = [[pair[:, :BS], pair[:, BS:]] for pair in pairs]
    if part == 1:
        ends = [[kept(low, facts[0]), kept(high, facts[1])] for low, high in ends]
    faces = [kept(south[rows, :PLANE], facts[2]), halo[3 * part + 2]]

    def strip(side):
        def row(x):
            if x == 0:
                return ends[side][0]
            if x == BS + 1:
                return ends[side][1]
            return faces[side][:, (x - 1) * BS : x * BS]

        return row

    build_shifts(centre, halo[3 * part], halo[3 * part + 1], strip(0), strip(1), shifts)
    width = 1024
    z = lax.broadcasted_iota(jnp.int32, (1, width), 1) % BS
    for first in range(0, VOX, width):
        spread = jnp.dot(mat[...], columns(shifts, first, width), preferred_element_type=F32)
        low = pltpu.roll(spread[:C], 1, 1)
        high = pltpu.roll(spread[2 * C :], width - 1, 1)
        total = spread[C : 2 * C] + jnp.where(z > 0, low, 0.0) + jnp.where(z < BS - 1, high, 0.0)
        out[:, first : first + width] = (total * mask[:, first : first + width]).astype(BF16)


def conv(part, facts, centre, halo, from_south, from_north, mat, mask):
    def kernel(*refs):
        conv_kernel(part, *refs)

    return pl.pallas_call(
        kernel,
        out_shape=jax.ShapeDtypeStruct((C, VOX), BF16),
        in_specs=[SMEM, VMEM, VMEM, HBM, HBM, VMEM, VMEM],
        out_specs=VMEM,
        scratch_shapes=[
            pltpu.VMEM((2 * C, PLANE + 2 * BS), BF16),
            pltpu.VMEM((2 * C, 2 * BS), BF16),
            pltpu.VMEM((3, C, VOX + 2 * PLANE), BF16),
            pltpu.SemaphoreType.DMA((2,)),
        ],
        compiler_params=LIMIT,
        cost_estimate=cost(2 * C * 27 * C * VOX * 2, 4 << 20),
        name="conv_back" if part else "conv_out",
    )(facts, centre, halo, from_south, from_north, mat, mask)


def z_stack(values):
    wide = values.astype(F32)
    width = values.shape[1]
    z = lax.broadcasted_iota(jnp.int32, (1, width), 1) % BS
    up = jnp.where(z < BS - 1, pltpu.roll(wide, width - 1, 1), 0.0)
    down = jnp.where(z > 0, pltpu.roll(wide, 1, 1), 0.0)
    return jnp.concatenate([up, wide, down], 0).astype(BF16)


def over_voxels(left, right):
    return lax.dot_general(left, right, (((1,), (1,)), ((), ())), preferred_element_type=F32)


def inner_kernel(f, g, acc, shifts):
    nothing = jnp.zeros((C, PLANE), BF16)

    def row(x):
        return nothing[:, :BS]

    build_shifts(f, nothing, nothing, row, row, shifts)
    width = 1024
    for first in range(0, VOX, width):
        part = over_voxels(
            z_stack(g[:, first : first + width]), columns(shifts, first, width)
        )
        if first == 0:
            acc[:, : 9 * C] = part
            acc[:, 9 * C :] = jnp.zeros((3 * C, 7 * LANES - 9 * C), F32)
        else:
            acc[:, : 9 * C] += part


def inner_partial(f, g):
    return pl.pallas_call(
        inner_kernel,
        out_shape=jax.ShapeDtypeStruct((3 * C, 7 * LANES), F32),
        in_specs=[VMEM, VMEM],
        out_specs=VMEM,
        scratch_shapes=[pltpu.VMEM((3, C, VOX + 2 * PLANE), BF16)],
        compiler_params=LIMIT,
        cost_estimate=cost(2 * C * 27 * C * VOX * 2, 4 << 20),
    )(f, g)


def weights_kernel(
    facts,
    f,
    g,
    inner,
    y_high,
    from_west,
    from_east,
    from_north,
    mine,
    theirs,
    halo,
    to_north,
    to_south,
    x_in,
    y_in,
    acc,
    flat,
    sems,
):
    copies = start_all(
        [from_west, from_east, from_north],
        [x_in.at[0], x_in.at[1], y_in],
        sems,
    )
    acc[...] = inner[...]
    for copy in copies:
        copy.wait()
    edge, last = PLANE - BS, VOX - PLANE
    for part in range(2):
        rows = slice(part * C, (part + 1) * C)
        for side in range(2):
            halo[3 * part + side] = kept(x_in[side, rows, :PLANE], facts[side])
        halo[3 * part + 2] = kept(y_in[rows, :PLANE], facts[3])
    west, east, north, g_north = halo[0], halo[1], halo[2], halo[5]
    at_low, at_high = slice(PLANE, PLANE + BS), slice(PLANE + BS, PLANE + 2 * BS)
    to_north[:, :PLANE] = y_high[...]
    to_north[:C, PLANE:] = jnp.concatenate([west[:, edge:], east[:, edge:]], 1)
    to_south[:C] = jnp.concatenate([west[:, :BS], east[:, :BS]], 1)
    to_north[C:, PLANE:] = jnp.concatenate([x_in[0, C:, at_high], x_in[1, C:, at_high]], 1)
    to_south[C:] = jnp.concatenate([x_in[0, C:, at_low], x_in[1, C:, at_low]], 1)

    def add(ab, left, right):
        acc[:, ab * C : (ab + 1) * C] += over_voxels(left, right)

    gap = jnp.zeros((C, BS), BF16)
    for a, plane, at in ((0, west, 0), (2, east, last)):
        left = z_stack(g[:, at : at + PLANE])
        moved = [
            jnp.concatenate([gap, plane[:, :edge]], 1),
            plane,
            jnp.concatenate([plane[:, BS:], gap], 1),
        ]
        part = over_voxels(left, jnp.concatenate(moved, 0))
        acc[:, 3 * a * C : 3 * (a + 1) * C] += part
    left = z_stack(y_high[C:])
    moved = [jnp.concatenate([gap, north[:, :edge]], 1), north, jnp.concatenate([north[:, BS:], gap], 1)]
    part = over_voxels(left, jnp.concatenate(moved, 0))
    for a in range(3):
        ab = 3 * a + 2
        acc[:, ab * C : (ab + 1) * C] += part[:, a * C : (a + 1) * C]
    left = z_stack(g_north)
    top = y_high[:C]
    moved = [
        jnp.concatenate([west[:, edge:], top[:, :edge]], 1),
        top,
        jnp.concatenate([top[:, BS:], east[:, edge:]], 1),
    ]
    part = over_voxels(left, jnp.concatenate(moved, 0))
    for a in range(3):
        ab = 3 * a
        acc[:, ab * C : (ab + 1) * C] += part[:, a * C : (a + 1) * C]
    for ab, g_edge, f_edge in (
        (2, x_in[1, C:, at_high], y_in[:C, at_high]),
        (8, x_in[0, C:, at_high], y_in[:C, at_low]),
    ):
        add(ab, z_stack(widen(g_edge)), widen(f_edge))
    for tile in range(7):
        flat[tile * 3 * C : (tile + 1) * 3 * C] = acc[:, tile * LANES : (tile + 1) * LANES]
    flat[21 * C :] = jnp.zeros((ROWS - 21 * C, LANES), F32)
    core = facts[6]
    mine[...] = flat[pl.ds(pl.multiple_of(core * HALF, HALF), HALF)]
    theirs[...] = flat[pl.ds(pl.multiple_of((1 - core) * HALF, HALF), HALF)]


def widen(values):
    return jnp.concatenate([values, jnp.zeros((C, LANES - BS), values.dtype)], 1)


def weight_partial(facts, f, g, inner, y_high, from_west, from_east, from_north):
    half = jax.ShapeDtypeStruct((HALF, LANES), F32)
    face = jax.ShapeDtypeStruct((2 * C, PLANE + 2 * BS), BF16)
    relay = jax.ShapeDtypeStruct((2 * C, 2 * BS), BF16)
    return pl.pallas_call(
        weights_kernel,
        out_shape=(half, half, jax.ShapeDtypeStruct((6, C, PLANE), BF16), face, relay),
        in_specs=[SMEM, VMEM, VMEM, VMEM, VMEM, HBM, HBM, HBM],
        out_specs=(VMEM,) * 5,
        scratch_shapes=[
            pltpu.VMEM((2, 2 * C, PLANE + 2 * BS), BF16),
            pltpu.VMEM((2 * C, PLANE + 2 * BS), BF16),
            pltpu.VMEM((3 * C, 7 * LANES), F32),
            pltpu.VMEM((ROWS, LANES), F32),
            pltpu.SemaphoreType.DMA((3,)),
        ],
        compiler_params=LIMIT,
        cost_estimate=cost(2**28, 4 << 20),
    )(facts, f, g, inner, y_high, from_west, from_east, from_north)


def core_groups():
    return [list(range(core, lax.axis_size("gx"), 2)) for core in range(2)]


def scatter_sum(total):
    total = total.reshape(-1, LANES, LANES)
    got = lax.all_to_all(total.astype(BF16), "gx", 0, 0, axis_index_groups=core_groups())
    return got.astype(F32).sum(0)


def gather_sum(own):
    parts = lax.axis_size("gx") // 2
    own = jnp.broadcast_to(own.astype(BF16)[None], (parts, LANES, LANES))
    got = lax.all_to_all(own, "gx", 0, 0, axis_index_groups=core_groups())
    return got.reshape(HALF, LANES)


def make_result(facts, half, other, scale):
    def kernel(facts, half, other, out, flat):
        core = facts[6]
        flat[pl.ds(pl.multiple_of(core * HALF, HALF), HALF)] = half[...].astype(F32)
        flat[pl.ds(pl.multiple_of((1 - core) * HALF, HALF), HALF)] = other[...].astype(F32)
        wide = []
        for c in range(3):
            tiles = [flat[(t * 3 + c) * C : (t * 3 + c + 1) * C] * scale for t in range(7)]
            wide.append(jnp.concatenate(tiles, 1))
        blocks = [wide[c][:, ab * C : (ab + 1) * C] for ab in range(9) for c in range(3)]
        out[...] = jnp.concatenate(blocks, 1)

    return pl.pallas_call(
        kernel,
        out_shape=jax.ShapeDtypeStruct((C, 27 * C), F32),
        in_specs=[SMEM, VMEM, VMEM],
        out_specs=VMEM,
        scratch_shapes=[pltpu.VMEM((ROWS, LANES), F32)],
        compiler_params=LIMIT,
        cost_estimate=cost(2**20, 2 << 20),
    )(facts, half, other)


def body(features, weight, occupancy, adjacency, cotangent):
    occupancy = occupancy.reshape(1, VOX)
    core = lax.axis_index("gx") % 2
    facts = jnp.concatenate([adjacency.reshape(6), jnp.full((2,), core, jnp.int32)])
    features = features.reshape(C, VOX)
    cotangent = cotangent.reshape(C, VOX)
    f, g, mask, x_low, x_high, y_low, y_high = prepare(facts, features, cotangent, occupancy)
    from_north = shifted(y_low, "gy", -1)
    from_west = shifted(x_high, "gx", 1)
    from_east = shifted(x_low, "gx", -1)
    inner = inner_partial(f, g)
    mine, theirs, halo, to_north, to_south = weight_partial(
        facts, f, g, inner, y_high, from_west, from_east, from_north
    )
    got, weight = lax.optimization_barrier((swap(theirs, "gx", 1), weight))
    own = scatter_sum(mine + got)
    mat, back = matrices(weight)
    own, mat, back, to_north = lax.optimization_barrier((own, mat, back, to_north))
    from_south = shifted(to_north, "gy", 1)
    step = 1
    while step < lax.axis_size("gy"):
        own = own + swap(own, "gy", step)
        if step == 1:
            own, to_south = lax.optimization_barrier((own, to_south))
            corner_north = shifted(to_south, "gy", -1)
        step = 2 * step
    outputs = conv(0, facts, f, halo, from_south, corner_north, mat, mask)
    own, outputs = lax.optimization_barrier((own, outputs))
    half = gather_sum(own)
    feature_grad = conv(1, facts, g, halo, from_south, corner_north, back, mask)
    half, feature_grad = lax.optimization_barrier((half, feature_grad))

    slot_count = lax.axis_size("gx") * lax.axis_size("gy") * VOX
    weight_grad = make_result(facts, half, swap(half, "gx", 1), 1.0 / math.sqrt(slot_count))
    out_shape = (1, 1, 1, C, VOX)
    return (outputs.reshape(out_shape), feature_grad.reshape(out_shape), weight_grad)


def solution(mesh):
    placed = (
        P("gx", "gy", None, None, None),
        P(),
        P("gx", "gy", None, None),
        P("gx", "gy", None, None),
        P("gx", "gy", None, None, None),
    )
    return jax.shard_map(
        body,
        mesh=mesh,
        in_specs=placed,
        out_specs=(P("gx", "gy", None, None, None), P("gx", "gy", None, None, None), P()),
        check_vma=False,
    )
```

time: 128 us -> 84.9 us (0.66)
  starting transfers between devices: 69.8 us -> 43.3 us
  local copies, waits for them, and re-layouts: 17.4 us -> 1.39 us
  Pallas kernels: 10.8 us -> 22.7 us
  waiting for transfers between devices: 21.4 us -> 14.4 us
  other arithmetic: 6.49 us -> 1.79 us
    ppermute x22 -> x6, starting transfers between devices: 45.8 us -> 20.4 us  [swap(): lax.ppermute(array, axis, [(i, i ^ mask) for i in range(lax.axis_size(axi...]
    pallas_call x4 -> x7, Pallas kernels: 10.8 us -> 22.7 us  [the longest x2 9.19 us: conv(): pl.pallas_call(kernel, out_shape=jax.ShapeDtypeStruct((C, VOX), BF16), in...]
    ppermute x22 -> x6, waiting for transfers between devices: 16.7 us -> 5.17 us  [swap(): lax.ppermute(array, axis, [(i, i ^ mask) for i in range(lax.axis_size(axi...]
    ppermute x8 -> x5, starting transfers between devices: 23.9 us -> 13.9 us  [shifted(): return lax.ppermute(array, axis, pairs)]
    all_to_all x0 -> x2, starting transfers between devices: none -> 9.06 us  [the longest x1 5.64 us: scatter_sum(): lax.all_to_all(total.astype(BF16), 'gx', 0, 0, axis_index_groups=core_gro...]
    reshape x5 -> x0, local copies, waits for them, and re-layouts: 8.58 us -> none  [the longest x2 4.42 us: body(): back = taps[:, ::-1, ::-1].transpose(2, 3, 1, 0).reshape(3 * C, 9 * C)]
    select_n x10 -> x0, other arithmetic: 5.74 us -> none  [the longest x8 5.6 us: kept(): return jnp.where(near[face], layer, jnp.zeros_like(layer))]
    all_to_all x0 -> x2, waiting for transfers between devices: none -> 4.34 us  [the longest x1 2.88 us: scatter_sum(): lax.all_to_all(total.astype(BF16), 'gx', 0, 0, axis_index_groups=core_gro...]
  transfers between devices with their start and end apart: 30 -> 13, of which waited for: 10 -> 8; matrix products, arithmetic and copies ran while one was open for 13% -> 0% of each run, Pallas kernels for 6% -> 19%
where the time goes in v2:
time: 84.9 us; the launch traced here: 84.4 us
  starting transfers between devices  43.3 us (51%)
  Pallas kernels  22.7 us (27%)
  waiting for transfers between devices  14.4 us (17%)
  other arithmetic  1.79 us (2%)
  local copies, waits for them, and re-layouts  1.39 us (2%)
    ppermute x6, starting transfers between devices, swap(): lax.ppermute(array, axis, [(i, i ^ mask) for i in range(lax.axis_size(axi...  20.4 us
    ppermute x5, starting transfers between devices, shifted(): return lax.ppermute(array, axis, pairs)  13.9 us
    pallas_call x2, Pallas kernels, conv(): pl.pallas_call(kernel, out_shape=jax.ShapeDtypeStruct((C, VOX), BF16), in...  9.19 us
    all_to_all x1, starting transfers between devices, scatter_sum(): lax.all_to_all(total.astype(BF16), 'gx', 0, 0, axis_index_groups=core_gro...  5.64 us
    ppermute x6, waiting for transfers between devices, swap(): lax.ppermute(array, axis, [(i, i ^ mask) for i in range(lax.axis_size(axi...  5.17 us
    ppermute x5, waiting for transfers between devices, shifted(): return lax.ppermute(array, axis, pairs)  4.87 us
    pallas_call x1, Pallas kernels, matrices(): pl.pallas_call(matrices_kernel, out_shape=(shape, shape), in_specs=[HBM],...  3.92 us
    all_to_all x1, starting transfers between devices, gather_sum(): got = lax.all_to_all(own, 'gx', 0, 0, axis_index_groups=core_groups())  3.41 us
  transfers between devices with their start and end apart: 13, of which 8 were waited for; matrix products, arithmetic and copies ran while one was open for 0% of the time, Pallas kernels for 19%

profile of v2, /device:TPU:1, one launch (start us, length us, event | category | flops | bytes accessed | tf_op | source)
XLA Modules:
  0.0 84.4 jit_solution(6984466877017233837)
XLA Ops:
  0.6 0.0 copy-start
  0.7 0.6 copy-done
  1.3 2.6 %shard_map.76 = (bf16[96,4096]{1,0:T(8,128)(2,1)S(1)}, bf16[96,4096]{1,0:T(8,128)(2,1)S(1)}, f32[1,4096]{1,0:T(1,128)S(1)}, bf16[192,288]{1,0:T(8,128)(2,1)S(1)}...) custom-call(s32[8]{0:T(128)S(1)} %concatenate.3.facts.refs_0_, ...), custom_call_target="tpu_custom_call" | custom-call | flops 1048576 | bytes 3145728 | tf_op jit(solution)/shard_map/pallas_call | solution.py:94
  3.9 4.5 %collective-permute-start = (bf16[192,288]{1,0:T(8,128)(2,1)S(1)}, bf16[192,288]{1,0:T(8,128)(2,1)S(1)}, u32[]{:S(2)}, u32[]{:S(2)}) collective-permute-start(bf16[192,288]{1,0:T(8,128)(2,1)S(1)} %get-tuple-element.32), channel_id=1, source_target_pairs={{0,16},{16,32},{32,48},{48,64},{64,80},{80,96},{96,112},{112,128},... | collective-permute-start | bytes 331784 | tf_op jit(solution)/shard_map/ppermute | solution.py:33
  8.4 1.9 %collective-permute-start.1 = (bf16[192,288]{1,0:T(8,128)(2,1)S(1)}, bf16[192,288]{1,0:T(8,128)(2,1)S(1)}, u32[]{:S(2)}, u32[]{:S(2)}) collective-permute-start(bf16[192,288]{1,0:T(8,128)(2,1)S(1)} %get-tuple-element.33), channel_id=1, source_target_pairs={{16,0},{32,16},{48,32},{64,48},{80,64},{96,80},{112,96},{128,112},... | collective-permute-start | bytes 331784 | tf_op jit(solution)/shard_map/ppermute | solution.py:33
  10.3 1.3 %collective-permute-start.2 = (bf16[192,288]{1,0:T(8,128)(2,1)S(1)}, bf16[192,288]{1,0:T(8,128)(2,1)S(1)}, u32[]{:S(2)}, u32[]{:S(2)}) collective-permute-start(bf16[192,288]{1,0:T(8,128)(2,1)S(1)} %get-tuple-element.34), channel_id=1, source_target_pairs={{1,0},{2,1},{3,2},{4,3},{5,4},{6,5},{7,6},{8,7},{9,8},{10,9},{11,1... | collective-permute-start | bytes 331784 | tf_op jit(solution)/shard_map/ppermute | solution.py:33
  11.6 2.8 %shard_map.77.inner = f32[288,896]{1,0:T(8,128)S(1)} custom-call(bf16[96,4096]{1,0:T(8,128)(2,1)S(1)} %get-tuple-element.29.f.refs_1_, bf16[96,4096]{1,0:T(8,128)(2,1)S(1)} %get-tuple-element.30.g.refs_1_), custom_call_target="tpu_custom_call" | custom-call | flops 4076863488 | bytes 4194304 | tf_op jit(solution)/shard_map/pallas_call | solution.py:250
  14.4 0.0 collective-permute-done.from_west
  14.4 0.4 collective-permute-done.1.from_east
  14.9 4.4 %collective-permute-done.2.from_north = bf16[192,288]{1,0:T(8,128)(2,1)S(1)} collective-permute-done((bf16[192,288]{1,0:T(8,128)(2,1)S(1)}, bf16[192,288]{1,0:T(8,128)(2,1)S(1)}, u32[]{:S(2)}, u32[]{:S(2)}) %collective-permute-start.2) | collective-permute-done | bytes 110624 | tf_op jit(solution)/shard_map/ppermute | solution.py:33
  19.3 2.3 %shard_map.78 = (f32[1024,128]{1,0:T(8,128)S(1)}, f32[1024,128]{1,0:T(8,128)S(1)}, bf16[6,96,256]{2,1,0:T(8,128)(2,1)S(1)}, bf16[192,288]{1,0:T(8,128)(2,1)S(1)}, bf16[192,32]{1,0:T(8,128)(2,1)S(1)}) custom-call(s32[8]{0:T(128)S(1)} %concatenate.3.facts.refs_0_, bf16[96,4096]{1,0:T(8,128)(2,1)S(1)} %get-tuple-element.29.f.refs_1_, ...), custom_call_target="tpu_custom_call" | custom-call | flops 268435456 | bytes 4194304 | tf_op jit(solution)/shard_map/pallas_call | solution.py:354
  21.6 0.5 collective-permute-start.3
  22.1 1.5 %collective-permute-done.3 = f32[1024,128]{1,0:T(8,128)S(1)} collective-permute-done((f32[1024,128]{1,0:T(8,128)S(1)}, f32[1024,128]{1,0:T(8,128)S(1)}, u32[]{:S(2)}, u32[]{:S(2)}) %collective-permute-start.3) | collective-permute-done | bytes 524320 | tf_op jit(solution)/shard_map/ppermute | solution.py:37
  23.6 0.8 add_convert_fusion
  24.4 5.6 %all-to-all-start = ((bf16[8,128,128]{2,1,0:T(8,128)(2,1)}), bf16[8,128,128]{2,1,0:T(8,128)(2,1)}, u32[]{:S(2)}, u32[]{:S(2)}) async-start(bf16[8,128,128]{2,1,0:T(8,128)(2,1)} %bitcast.4), calls=%async_computation | async-start | bytes 524288 | tf_op jit(solution)/shard_map/all_to_all | solution.py:377
  30.0 3.9 %shard_map.79 = (bf16[288,864]{1,0:T(8,128)(2,1)S(1)}, bf16[288,864]{1,0:T(8,128)(2,1)S(1)}) custom-call(bf16[96,2592]{1,0:T(8,128)(2,1)} %weight), custom_call_target="tpu_custom_call" | custom-call | flops 268435456 | bytes 6291456 | tf_op jit(solution)/shard_map/pallas_call | solution.py:131
  33.9 2.9 %all-to-all-done = bf16[8,128,128]{2,1,0:T(8,128)(2,1)} async-done(((bf16[8,128,128]{2,1,0:T(8,128)(2,1)}), bf16[8,128,128]{2,1,0:T(8,128)(2,1)}, u32[]{:S(2)}, u32[]{:S(2)}) %all-to-all-start) | async-done | bytes 262176 | tf_op jit(solution)/shard_map/all_to_all | solution.py:377
  36.8 1.0 %convert_reduce_fusion = f32[128,128]{1,0:T(8,128)S(1)} fusion(bf16[8,128,128]{2,1,0:T(8,128)(2,1)} %all-to-all-done), kind=kLoop, calls=%fused_computation | loop fusion | flops 245760 | bytes 327680 | tf_op jit(solution)/shard_map/reduce_sum | solution.py:378
  37.8 3.3 %collective-permute-start.4 = (f32[128,128]{1,0:T(8,128)S(1)}, f32[128,128]{1,0:T(8,128)S(1)}, u32[]{:S(2)}, u32[]{:S(2)}) collective-permute-start(f32[128,128]{1,0:T(8,128)S(1)} %convert_reduce_fusion), channel_id=1, source_target_pairs={{0,1},{1,0},{2,3},{3,2},{4,5},{5,4},{6,7},{7,6},{8,9},{9,8},{10,11... | collective-permute-start | bytes 196616 | tf_op jit(solution)/shard_map/ppermute | solution.py:37
  41.1 1.7 %collective-permute-done.4 = f32[128,128]{1,0:T(8,128)S(1)} collective-permute-done((f32[128,128]{1,0:T(8,128)S(1)}, f32[128,128]{1,0:T(8,128)S(1)}, u32[]{:S(2)}, u32[]{:S(2)}) %collective-permute-start.4) | collective-permute-done | bytes 65568 | tf_op jit(solution)/shard_map/ppermute | solution.py:37
  42.7 1.7 %collective-permute-start.5 = (f32[128,128]{1,0:T(8,128)S(1)}, f32[128,128]{1,0:T(8,128)S(1)}, u32[]{:S(2)}, u32[]{:S(2)}) collective-permute-start(f32[128,128]{1,0:T(8,128)S(1)} %add.23), channel_id=1, source_target_pairs={{0,2},{1,3},{2,0},{3,1},{4,6},{5,7},{6,4},{7,5},{8,10},{9,11},{10,... | collective-permute-start | bytes 196616 | tf_op jit(solution)/shard_map/ppermute | solution.py:37
  44.5 4.9 %collective-permute-start.8 = (bf16[192,288]{1,0:T(8,128)(2,1)S(1)}, bf16[192,288]{1,0:T(8,128)(2,1)S(1)}, u32[]{:S(2)}, u32[]{:S(2)}) collective-permute-start(bf16[192,288]{1,0:T(8,128)(2,1)S(1)} %get-tuple-element.46), channel_id=1, source_target_pairs={{0,1},{1,2},{2,3},{3,4},{4,5},{5,6},{6,7},{7,8},{8,9},{9,10},{10,1... | collective-permute-start | bytes 331784 | tf_op jit(solution)/shard_map/ppermute | solution.py:33
  49.3 0.0 collective-permute-done.5
  49.4 4.3 %collective-permute-start.6 = (f32[128,128]{1,0:T(8,128)S(1)}, f32[128,128]{1,0:T(8,128)S(1)}, u32[]{:S(2)}, u32[]{:S(2)}) collective-permute-start(f32[128,128]{1,0:T(8,128)S(1)} %add.24), channel_id=1, source_target_pairs={{0,4},{1,5},{2,6},{3,7},{4,0},{5,1},{6,2},{7,3},{8,12},{9,13},{10,... | collective-permute-start | bytes 196616 | tf_op jit(solution)/shard_map/ppermute | solution.py:37
  53.7 1.3 %collective-permute-start.9 = (bf16[192,32]{1,0:T(8,128)(2,1)S(1)}, bf16[192,32]{1,0:T(8,128)(2,1)S(1)}, u32[]{:S(2)}, u32[]{:S(2)}) collective-permute-start(bf16[192,32]{1,0:T(8,128)(2,1)S(1)} %get-tuple-element.47), channel_id=1, source_target_pairs={{1,0},{2,1},{3,2},{4,3},{5,4},{6,5},{7,6},{8,7},{9,8},{10,9},{11,1... | collective-permute-start | bytes 36872 | tf_op jit(solution)/shard_map/ppermute | solution.py:33
  54.9 0.8 collective-permute-done.6
  55.8 4.7 %collective-permute-start.7 = (f32[128,128]{1,0:T(8,128)S(1)}, f32[128,128]{1,0:T(8,128)S(1)}, u32[]{:S(2)}, u32[]{:S(2)}) collective-permute-start(f32[128,128]{1,0:T(8,128)S(1)} %add.25), channel_id=1, source_target_pairs={{0,8},{1,9},{2,10},{3,11},{4,12},{5,13},{6,14},{7,15},{8,0},{9,1},... | collective-permute-start | bytes 196616 | tf_op jit(solution)/shard_map/ppermute | solution.py:37
  60.5 0.0 collective-permute-done.9.refs_4_
  60.5 0.0 collective-permute-done.8.refs_3_
  60.5 4.6 %conv_out.1 = bf16[96,4096]{1,0:T(8,128)(2,1)} custom-call(s32[8]{0:T(128)S(1)} %concatenate.3.facts.refs_0_, bf16[96,4096]{1,0:T(8,128)(2,1)S(1)} %get-tuple-element.29.f.refs_1_, bf16[6,96,256]{2,1,0:T(8,128)(2,1)S(1)} %get-tuple-element.45.refs_2_, bf16[192,288]{1,0:T(8,128)(2,1)S(1)} %collective-permute-done.8.refs_3_, ...), custom_call_target="tpu_custom_call" | custom-call | flops 4076863488 | bytes 4194304 | tf_op jit(solution)/shard_map/conv_out/pallas_call | solution.py:200
  65.1 0.0 collective-permute-done.7
  65.1 0.7 broadcast_in_dim.2
  65.8 3.4 %all-to-all-start.1 = ((bf16[8,128,128]{2,1,0:T(8,128)(2,1)}), bf16[8,128,128]{2,1,0:T(8,128)(2,1)S(1)}, u32[]{:S(2)}, u32[]{:S(2)}) async-start(bf16[8,128,128]{2,1,0:T(8,128)(2,1)} %broadcast_in_dim.2), calls=%async_computation.1 | async-start | bytes 524288 | tf_op jit(solution)/shard_map/all_to_all | solution.py:384
  69.2 4.6 %conv_back.1 = bf16[96,4096]{1,0:T(8,128)(2,1)} custom-call(s32[8]{0:T(128)S(1)} %concatenate.3.facts.refs_0_, bf16[96,4096]{1,0:T(8,128)(2,1)S(1)} %get-tuple-element.30.g.refs_1_, bf16[6,96,256]{2,1,0:T(8,128)(2,1)S(1)} %get-tuple-element.45.refs_2_, bf16[192,288]{1,0:T(8,128)(2,1)S(1)} %collective-permute-done.8.refs_3_, ...), custom_call_target="tpu_custom_call" | custom-call | flops 4076863488 | bytes 4194304 | tf_op jit(solution)/shard_map/conv_back/pallas_call | solution.py:200
  73.9 1.5 %all-to-all-done.1 = bf16[8,128,128]{2,1,0:T(8,128)(2,1)S(1)} async-done(((bf16[8,128,128]{2,1,0:T(8,128)(2,1)}), bf16[8,128,128]{2,1,0:T(8,128)(2,1)S(1)}, u32[]{:S(2)}, u32[]{:S(2)}) %all-to-all-start.1) | async-done | bytes 262176 | tf_op jit(solution)/shard_map/all_to_all | solution.py:384
  75.3 5.9 %collective-permute-start.10 = (bf16[1024,128]{1,0:T(8,128)(2,1)S(1)}, bf16[1024,128]{1,0:T(8,128)(2,1)S(1)}, u32[]{:S(2)}, u32[]{:S(2)}) collective-permute-start(bf16[1024,128]{1,0:T(8,128)(2,1)S(1)} %bitcast.8), channel_id=1, source_target_pairs={{0,16},{16,0},{32,48},{48,32},{64,80},{80,64},{96,112},{112,96},{1... | collective-permute-start | bytes 786440 | tf_op jit(solution)/shard_map/ppermute | solution.py:37
  81.2 1.2 %collective-permute-done.10.other = bf16[1024,128]{1,0:T(8,128)(2,1)S(1)} collective-permute-done((bf16[1024,128]{1,0:T(8,128)(2,1)S(1)}, bf16[1024,128]{1,0:T(8,128)(2,1)S(1)}, u32[]{:S(2)}, u32[]{:S(2)}) %collective-permute-start.10) | collective-permute-done | bytes 262176 | tf_op jit(solution)/shard_map/ppermute | solution.py:37
  82.4 2.0 %shard_map.80 = f32[96,2592]{1,0:T(8,128)} custom-call(s32[8]{0:T(128)S(1)} %concatenate.3.facts.refs_0_, bf16[1024,128]{1,0:T(8,128)(2,1)S(1)} %bitcast.9, bf16[1024,128]{1,0:T(8,128)(2,1)S(1)} %collective-permute-done.10.other), custom_call_target="tpu_custom_call" | custom-call | flops 1048576 | bytes 2097152 | tf_op jit(solution)/shard_map/pallas_call | solution.py:400
  (5 shorter events, 0.0 us)
Async XLA Ops:
  0.6 0.7 copy-start
  3.9 10.5 %collective-permute-start = (bf16[192,288]{1,0:T(8,128)(2,1)S(1)}, bf16[192,288]{1,0:T(8,128)(2,1)S(1)}, u32[]{:S(2)}, u32[]{:S(2)}) collective-permute-start(bf16[192,288]{1,0:T(8,128)(2,1)S(1)} %get-tuple-element.32), channel_id=1, source_target_pairs={{0,16},{16,32},{32,48},{48,64},{64,80},{80,96},{96,112},{112,128},... | collective-permute-start | bytes 331784 | tf_op jit(solution)/shard_map/ppermute | solution.py:33
  8.4 6.5 %collective-permute-start.1 = (bf16[192,288]{1,0:T(8,128)(2,1)S(1)}, bf16[192,288]{1,0:T(8,128)(2,1)S(1)}, u32[]{:S(2)}, u32[]{:S(2)}) collective-permute-start(bf16[192,288]{1,0:T(8,128)(2,1)S(1)} %get-tuple-element.33), channel_id=1, source_target_pairs={{16,0},{32,16},{48,32},{64,48},{80,64},{96,80},{112,96},{128,112},... | collective-permute-start | bytes 331784 | tf_op jit(solution)/shard_map/ppermute | solution.py:33
  10.3 9.0 %collective-permute-start.2 = (bf16[192,288]{1,0:T(8,128)(2,1)S(1)}, bf16[192,288]{1,0:T(8,128)(2,1)S(1)}, u32[]{:S(2)}, u32[]{:S(2)}) collective-permute-start(bf16[192,288]{1,0:T(8,128)(2,1)S(1)} %get-tuple-element.34), channel_id=1, source_target_pairs={{1,0},{2,1},{3,2},{4,3},{5,4},{6,5},{7,6},{8,7},{9,8},{10,9},{11,1... | collective-permute-start | bytes 331784 | tf_op jit(solution)/shard_map/ppermute | solution.py:33
  21.6 2.0 %collective-permute-start.3 = (f32[1024,128]{1,0:T(8,128)S(1)}, f32[1024,128]{1,0:T(8,128)S(1)}, u32[]{:S(2)}, u32[]{:S(2)}) collective-permute-start(f32[1024,128]{1,0:T(8,128)S(1)} %get-tuple-element.36), channel_id=1, source_target_pairs={{0,16},{16,0},{32,48},{48,32},{64,80},{80,64},{96,112},{112,96},{1... | collective-permute-start | bytes 1572872 | tf_op jit(solution)/shard_map/ppermute | solution.py:37
  24.4 12.5 %all-to-all-start = ((bf16[8,128,128]{2,1,0:T(8,128)(2,1)}), bf16[8,128,128]{2,1,0:T(8,128)(2,1)}, u32[]{:S(2)}, u32[]{:S(2)}) async-start(bf16[8,128,128]{2,1,0:T(8,128)(2,1)} %bitcast.4), calls=%async_computation | async-start | bytes 524288 | tf_op jit(solution)/shard_map/all_to_all | solution.py:377
  37.8 4.9 %collective-permute-start.4 = (f32[128,128]{1,0:T(8,128)S(1)}, f32[128,128]{1,0:T(8,128)S(1)}, u32[]{:S(2)}, u32[]{:S(2)}) collective-permute-start(f32[128,128]{1,0:T(8,128)S(1)} %convert_reduce_fusion), channel_id=1, source_target_pairs={{0,1},{1,0},{2,3},{3,2},{4,5},{5,4},{6,7},{7,6},{8,9},{9,8},{10,11... | collective-permute-start | bytes 196616 | tf_op jit(solution)/shard_map/ppermute | solution.py:37
  42.7 6.6 %collective-permute-start.5 = (f32[128,128]{1,0:T(8,128)S(1)}, f32[128,128]{1,0:T(8,128)S(1)}, u32[]{:S(2)}, u32[]{:S(2)}) collective-permute-start(f32[128,128]{1,0:T(8,128)S(1)} %add.23), channel_id=1, source_target_pairs={{0,2},{1,3},{2,0},{3,1},{4,6},{5,7},{6,4},{7,5},{8,10},{9,11},{10,... | collective-permute-start | bytes 196616 | tf_op jit(solution)/shard_map/ppermute | solution.py:37
  44.5 16.0 %collective-permute-start.8 = (bf16[192,288]{1,0:T(8,128)(2,1)S(1)}, bf16[192,288]{1,0:T(8,128)(2,1)S(1)}, u32[]{:S(2)}, u32[]{:S(2)}) collective-permute-start(bf16[192,288]{1,0:T(8,128)(2,1)S(1)} %get-tuple-element.46), channel_id=1, source_target_pairs={{0,1},{1,2},{2,3},{3,4},{4,5},{5,6},{6,7},{7,8},{8,9},{9,10},{10,1... | collective-permute-start | bytes 331784 | tf_op jit(solution)/shard_map/ppermute | solution.py:33
  49.4 6.4 %collective-permute-start.6 = (f32[128,128]{1,0:T(8,128)S(1)}, f32[128,128]{1,0:T(8,128)S(1)}, u32[]{:S(2)}, u32[]{:S(2)}) collective-permute-start(f32[128,128]{1,0:T(8,128)S(1)} %add.24), channel_id=1, source_target_pairs={{0,4},{1,5},{2,6},{3,7},{4,0},{5,1},{6,2},{7,3},{8,12},{9,13},{10,... | collective-permute-start | bytes 196616 | tf_op jit(solution)/shard_map/ppermute | solution.py:37
  53.7 6.8 %collective-permute-start.9 = (bf16[192,32]{1,0:T(8,128)(2,1)S(1)}, bf16[192,32]{1,0:T(8,128)(2,1)S(1)}, u32[]{:S(2)}, u32[]{:S(2)}) collective-permute-start(bf16[192,32]{1,0:T(8,128)(2,1)S(1)} %get-tuple-element.47), channel_id=1, source_target_pairs={{1,0},{2,1},{3,2},{4,3},{5,4},{6,5},{7,6},{8,7},{9,8},{10,9},{11,1... | collective-permute-start | bytes 36872 | tf_op jit(solution)/shard_map/ppermute | solution.py:33
  55.8 9.3 %collective-permute-start.7 = (f32[128,128]{1,0:T(8,128)S(1)}, f32[128,128]{1,0:T(8,128)S(1)}, u32[]{:S(2)}, u32[]{:S(2)}) collective-permute-start(f32[128,128]{1,0:T(8,128)S(1)} %add.25), channel_id=1, source_target_pairs={{0,8},{1,9},{2,10},{3,11},{4,12},{5,13},{6,14},{7,15},{8,0},{9,1},... | collective-permute-start | bytes 196616 | tf_op jit(solution)/shard_map/ppermute | solution.py:37
  65.8 9.5 %all-to-all-start.1 = ((bf16[8,128,128]{2,1,0:T(8,128)(2,1)}), bf16[8,128,128]{2,1,0:T(8,128)(2,1)S(1)}, u32[]{:S(2)}, u32[]{:S(2)}) async-start(bf16[8,128,128]{2,1,0:T(8,128)(2,1)} %broadcast_in_dim.2), calls=%async_computation.1 | async-start | bytes 524288 | tf_op jit(solution)/shard_map/all_to_all | solution.py:384
  75.3 7.1 %collective-permute-start.10 = (bf16[1024,128]{1,0:T(8,128)(2,1)S(1)}, bf16[1024,128]{1,0:T(8,128)(2,1)S(1)}, u32[]{:S(2)}, u32[]{:S(2)}) collective-permute-start(bf16[1024,128]{1,0:T(8,128)(2,1)S(1)} %bitcast.8), channel_id=1, source_target_pairs={{0,16},{16,0},{32,48},{48,32},{64,80},{80,64},{96,112},{112,96},{1... | collective-permute-start | bytes 786440 | tf_op jit(solution)/shard_map/ppermute | solution.py:37

commit v3 on v2

--- a/solution.py
+++ b/solution.py
@@ -57,85 +57,121 @@
     )
 
 
+def pack_message(message, faces, *edges):
+    message[: 2 * C, :] = faces
+    gap = jnp.zeros((BS, PLANE - 2 * C), BF16)
+    for k, each in enumerate(edges):
+        pieces = [each[i * BS : (i + 1) * BS] for i in range(C // BS)]
+        first = 2 * C + k * BS
+        message[first : first + BS, :] = jnp.concatenate(pieces + [gap], 1)
+
+
+def unpack_edges(message, k=0):
+    rows = message[2 * C + k * BS : 2 * C + (k + 1) * BS, :]
+    return jnp.concatenate([rows[:, 2 * BS * i : 2 * BS * (i + 1)] for i in range(C // BS)], 0)
+
+
+MESSAGE = (2 * C + BS, PLANE)
+RELAY = (2 * C + 2 * BS, PLANE)
+
+
 def prepare_kernel(
-    facts, feat, cot, occ, f_out, g_out, mask, x_low, x_high, y_low, y_high, f_in, g_in, occ_in, sems
+    links, feat, cot, occ, f_out, g_out, mask, y_low, x_edges, f_in, g_in, occ_in, facts, sems
 ):
     rows = C // PIECES
     cuts = [slice(i * rows, (i + 1) * rows) for i in range(PIECES)]
     copies = start_all(
-        [occ] + [feat.at[c] for c in cuts] + [cot.at[c] for c in cuts],
-        [occ_in] + [f_in.at[c] for c in cuts] + [g_in.at[c] for c in cuts],
+        [occ, links] + [feat.at[c] for c in cuts] + [cot.at[c] for c in cuts],
+        [occ_in, facts] + [f_in.at[c] for c in cuts] + [g_in.at[c] for c in cuts],
         sems,
     )
     copies[0].wait()
+    copies[1].wait()
     occupied = occ_in[...].astype(BF16)
     mask[...] = occ_in[...].astype(F32)
-    last, edge = VOX - PLANE, PLANE - BS
     for part, source, out in ((0, f_in, f_out), (1, g_in, g_out)):
-        for copy in copies[1 + part * PIECES : 1 + (part + 1) * PIECES]:
+        for copy in copies[2 + part * PIECES : 2 + (part + 1) * PIECES]:
             copy.wait()
-        masked = source[...] * occupied
-        out[...] = masked
-        to = slice(part * C, (part + 1) * C)
-        low, high = masked[:, :PLANE], masked[:, last:]
-        for message, plane in ((x_low, low), (x_high, high)):
-            message[to, :PLANE] = plane
-            edges = [kept(plane[:, :BS], facts[2]), kept(plane[:, edge:], facts[3])]
-            message[to, PLANE:] = jnp.concatenate(edges, 1)
-        y_low[to, :PLANE] = y_face(masked, 0)
-        edges = [kept(low[:, :BS], facts[0]), kept(high[:, :BS], facts[1])]
-        y_low[to, PLANE:] = jnp.concatenate(edges, 1)
-        y_high[to] = y_face(masked, edge)
+        out[...] = source[...] * occupied
+    faces = jnp.concatenate([y_face(f_out, 0), y_face(g_out, 0)], 0)
+    last = VOX - PLANE
+    edges = [kept(f_out[:, :BS], facts[0, 0]), kept(f_out[:, last : last + BS], facts[0, 1])]
+    pack_message(y_low, faces, jnp.concatenate(edges, 1))
+    for side, first in ((0, 0), (1, last)):
+        low = kept(g_out[:, first : first + BS], facts[0, 2])
+        high = kept(g_out[:, first + PLANE - BS : first + PLANE], facts[0, 3])
+        x_edges[side] = jnp.concatenate([low, high], 1)
 
 
 def prepare(facts, features, cotangent, occupancy):
     whole = jax.ShapeDtypeStruct((C, VOX), BF16)
-    face = jax.ShapeDtypeStruct((2 * C, PLANE + 2 * BS), BF16)
+    inputs = [pltpu.with_memory_space_constraint(x, pltpu.HBM) for x in (facts, features, cotangent, occupancy)]
     return pl.pallas_call(
         prepare_kernel,
         out_shape=(
             whole,
             whole,
             jax.ShapeDtypeStruct((1, VOX), F32),
-            face,
-            face,
-            face,
-            jax.ShapeDtypeStruct((2 * C, PLANE), BF16),
+            jax.ShapeDtypeStruct(MESSAGE, BF16),
+            jax.ShapeDtypeStruct((2, C, 2 * BS), BF16),
         ),
-        in_specs=[SMEM, HBM, HBM, HBM],
-        out_specs=(VMEM,) * 7,
+        in_specs=[HBM] * 4,
+        out_specs=(VMEM,) * 5,
         scratch_shapes=[
             pltpu.VMEM((C, VOX), BF16),
             pltpu.VMEM((C, VOX), BF16),
             pltpu.VMEM((1, VOX), jnp.int32),
-            pltpu.SemaphoreType.DMA((1 + 2 * PIECES,)),
+            pltpu.SMEM((1, 6), jnp.int32),
+            pltpu.SemaphoreType.DMA((2 + 2 * PIECES,)),
         ],
         compiler_params=LIMIT,
         cost_estimate=cost(2**20, 3 << 20),
-    )(facts, *[pltpu.with_memory_space_constraint(x, pltpu.HBM) for x in (features, cotangent, occupancy)])
-
-
-def matrices_kernel(weight, mat, back, held, sems):
-    start_all([weight], [held], sems)[0].wait()
-    for ab in range(9):
-        for c in range(3):
-            k = ab * 3 + c
-            block = held[:, k * C : (k + 1) * C]
-            mat[c * C : (c + 1) * C, ab * C : (ab + 1) * C] = block
-            turned = block.astype(F32).T.astype(BF16)
-            back[(2 - c) * C : (3 - c) * C, (8 - ab) * C : (9 - ab) * C] = turned
-
-
-def matrices(weight):
-    shape = jax.ShapeDtypeStruct((3 * C, 9 * C), BF16)
-    return pl.pallas_call(
-        matrices_kernel,
-        out_shape=(shape, shape),
+    )(*inputs)
+
+
+def faces_kernel(f, g, x_edges, x_low, x_high, y_high):
+    edge = PLANE - BS
+    for side, message, first in ((0, x_low, 0), (1, x_high, VOX - PLANE)):
+        at = slice(first, first + PLANE)
+        pack_message(message, jnp.concatenate([f[:, at], g[:, at]], 0), x_edges[side])
+    y_high[:C] = y_face(f, edge)
+    y_high[C:] = y_face(g, edge)
+
+
+def other_faces(f, g, x_edges):
+    message = jax.ShapeDtypeStruct(MESSAGE, BF16)
+    return pl.pallas_call(
+        faces_kernel,
+        out_shape=(message, message, jax.ShapeDtypeStruct((2 * C, PLANE), BF16)),
+        in_specs=[VMEM] * 3,
+        out_specs=(VMEM,) * 3,
+        compiler_params=LIMIT,
+        cost_estimate=cost(2**20, 1 << 20),
+    )(f, g, x_edges)
+
+
+def matrix(back, weight):
+    def kernel(weight, mat, held, sems):
+        start_all([weight], [held], sems)[0].wait()
+        for ab in range(9):
+            for c in range(3):
+                k = ab * 3 + c
+                block = held[:, k * C : (k + 1) * C]
+                if back:
+                    turned = block.astype(F32).T.astype(BF16)
+                    mat[(2 - c) * C : (3 - c) * C, (8 - ab) * C : (9 - ab) * C] = turned
+                else:
+                    mat[c * C : (c + 1) * C, ab * C : (ab + 1) * C] = block
+
+    return pl.pallas_call(
+        kernel,
+        out_shape=jax.ShapeDtypeStruct((3 * C, 9 * C), BF16),
         in_specs=[HBM],
-        out_specs=(VMEM, VMEM),
+        out_specs=VMEM,
         scratch_shapes=[pltpu.VMEM((C, 27 * C), BF16), pltpu.SemaphoreType.DMA((1,))],
         compiler_params=LIMIT,
         cost_estimate=cost(2**28, 6 << 20),
+        name="matrix_back" if back else "matrix_out",
     )(pltpu.with_memory_space_constraint(weight, pltpu.HBM))
 
 
@@ -164,13 +200,13 @@
         copy.wait()
     rows = slice(part * C, (part + 1) * C)
     if part == 0:
-        pairs = [kept(south[rows, PLANE:], facts[2]), kept(north[rows], facts[3])]
+        pairs = [kept(unpack_edges(south), facts[0, 2]), kept(north[rows], facts[0, 3])]
     else:
-        pairs = [south[rows, PLANE:], north[rows]]
+        pairs = [unpack_edges(south, 1), north[rows]]
     ends = [[pair[:, :BS], pair[:, BS:]] for pair in pairs]
     if part == 1:
-        ends = [[kept(low, facts[0]), kept(high, facts[1])] for low, high in ends]
-    faces = [kept(south[rows, :PLANE], facts[2]), halo[3 * part + 2]]
+        ends = [[kept(low, facts[0, 0]), kept(high, facts[0, 1])] for low, high in ends]
+    faces = [kept(south[rows], facts[0, 2]), halo[3 * part + 2]]
 
     def strip(side):
         def row(x):
@@ -203,7 +239,7 @@
         in_specs=[SMEM, VMEM, VMEM, HBM, HBM, VMEM, VMEM],
         out_specs=VMEM,
         scratch_shapes=[
-            pltpu.VMEM((2 * C, PLANE + 2 * BS), BF16),
+            pltpu.VMEM(RELAY, BF16),
             pltpu.VMEM((2 * C, 2 * BS), BF16),
             pltpu.VMEM((3, C, VOX + 2 * PLANE), BF16),
             pltpu.SemaphoreType.DMA((2,)),
@@ -260,6 +296,7 @@
 
 def weights_kernel(
     facts,
+    place,
     f,
     g,
     inner,
@@ -290,15 +327,18 @@
     for part in range(2):
         rows = slice(part * C, (part + 1) * C)
         for side in range(2):
-            halo[3 * part + side] = kept(x_in[side, rows, :PLANE], facts[side])
-        halo[3 * part + 2] = kept(y_in[rows, :PLANE], facts[3])
+            halo[3 * part + side] = kept(x_in[side, rows], facts[0, side])
+        halo[3 * part + 2] = kept(y_in[rows], facts[0, 3])
     west, east, north, g_north = halo[0], halo[1], halo[2], halo[5]
-    at_low, at_high = slice(PLANE, PLANE + BS), slice(PLANE + BS, PLANE + 2 * BS)
-    to_north[:, :PLANE] = y_high[...]
-    to_north[:C, PLANE:] = jnp.concatenate([west[:, edge:], east[:, edge:]], 1)
+    on_west, on_east, on_north = [unpack_edges(m) for m in (x_in.at[0], x_in.at[1], y_in)]
+    pack_message(
+        to_north,
+        y_high[...],
+        jnp.concatenate([west[:, edge:], east[:, edge:]], 1),
+        jnp.concatenate([on_west[:, BS:], on_east[:, BS:]], 1),
+    )
     to_south[:C] = jnp.concatenate([west[:, :BS], east[:, :BS]], 1)
-    to_north[C:, PLANE:] = jnp.concatenate([x_in[0, C:, at_high], x_in[1, C:, at_high]], 1)
-    to_south[C:] = jnp.concatenate([x_in[0, C:, at_low], x_in[1, C:, at_low]], 1)
+    to_south[C:] = jnp.concatenate([on_west[:, :BS], on_east[:, :BS]], 1)
 
     def add(ab, left, right):
         acc[:, ab * C : (ab + 1) * C] += over_voxels(left, right)
@@ -331,14 +371,14 @@
         ab = 3 * a
         acc[:, ab * C : (ab + 1) * C] += part[:, a * C : (a + 1) * C]
     for ab, g_edge, f_edge in (
-        (2, x_in[1, C:, at_high], y_in[:C, at_high]),
-        (8, x_in[0, C:, at_high], y_in[:C, at_low]),
+        (2, on_east[:, BS:], on_north[:, BS:]),
+        (8, on_west[:, BS:], on_north[:, :BS]),
     ):
         add(ab, z_stack(widen(g_edge)), widen(f_edge))
     for tile in range(7):
         flat[tile * 3 * C : (tile + 1) * 3 * C] = acc[:, tile * LANES : (tile + 1) * LANES]
     flat[21 * C :] = jnp.zeros((ROWS - 21 * C, LANES), F32)
-    core = facts[6]
+    core = place[0]
     mine[...] = flat[pl.ds(pl.multiple_of(core * HALF, HALF), HALF)]
     theirs[...] = flat[pl.ds(pl.multiple_of((1 - core) * HALF, HALF), HALF)]
 
@@ -347,25 +387,25 @@
     return jnp.concatenate([values, jnp.zeros((C, LANES - BS), values.dtype)], 1)
 
 
-def weight_partial(facts, f, g, inner, y_high, from_west, from_east, from_north):
+def weight_partial(facts, place, f, g, inner, y_high, from_west, from_east, from_north):
     half = jax.ShapeDtypeStruct((HALF, LANES), F32)
-    face = jax.ShapeDtypeStruct((2 * C, PLANE + 2 * BS), BF16)
+    face = jax.ShapeDtypeStruct(RELAY, BF16)
     relay = jax.ShapeDtypeStruct((2 * C, 2 * BS), BF16)
     return pl.pallas_call(
         weights_kernel,
         out_shape=(half, half, jax.ShapeDtypeStruct((6, C, PLANE), BF16), face, relay),
-        in_specs=[SMEM, VMEM, VMEM, VMEM, VMEM, HBM, HBM, HBM],
+        in_specs=[SMEM, SMEM, VMEM, VMEM, VMEM, VMEM, HBM, HBM, HBM],
         out_specs=(VMEM,) * 5,
         scratch_shapes=[
-            pltpu.VMEM((2, 2 * C, PLANE + 2 * BS), BF16),
-            pltpu.VMEM((2 * C, PLANE + 2 * BS), BF16),
+            pltpu.VMEM((2, *MESSAGE), BF16),
+            pltpu.VMEM(MESSAGE, BF16),
             pltpu.VMEM((3 * C, 7 * LANES), F32),
             pltpu.VMEM((ROWS, LANES), F32),
             pltpu.SemaphoreType.DMA((3,)),
         ],
         compiler_params=LIMIT,
         cost_estimate=cost(2**28, 4 << 20),
-    )(facts, f, g, inner, y_high, from_west, from_east, from_north)
+    )(facts, place, f, g, inner, y_high, from_west, from_east, from_north)
 
 
 def core_groups():
@@ -385,9 +425,9 @@
     return got.reshape(HALF, LANES)
 
 
-def make_result(facts, half, other, scale):
-    def kernel(facts, half, other, out, flat):
-        core = facts[6]
+def make_result(place, half, other, scale):
+    def kernel(place, half, other, out, flat):
+        core = place[0]
         flat[pl.ds(pl.multiple_of(core * HALF, HALF), HALF)] = half[...].astype(F32)
         flat[pl.ds(pl.multiple_of((1 - core) * HALF, HALF), HALF)] = other[...].astype(F32)
         wide = []
@@ -405,26 +445,27 @@
         scratch_shapes=[pltpu.VMEM((ROWS, LANES), F32)],
         compiler_params=LIMIT,
         cost_estimate=cost(2**20, 2 << 20),
-    )(facts, half, other)
+    )(place, half, other)
 
 
 def body(features, weight, occupancy, adjacency, cotangent):
     occupancy = occupancy.reshape(1, VOX)
-    core = lax.axis_index("gx") % 2
-    facts = jnp.concatenate([adjacency.reshape(6), jnp.full((2,), core, jnp.int32)])
+    place = jnp.full((1,), lax.axis_index("gx") % 2, jnp.int32)
+    facts = adjacency.reshape(1, 6)
     features = features.reshape(C, VOX)
     cotangent = cotangent.reshape(C, VOX)
-    f, g, mask, x_low, x_high, y_low, y_high = prepare(facts, features, cotangent, occupancy)
+    f, g, mask, y_low, x_edges = prepare(facts, features, cotangent, occupancy)
     from_north = shifted(y_low, "gy", -1)
+    x_low, x_high, y_high = other_faces(f, g, x_edges)
     from_west = shifted(x_high, "gx", 1)
     from_east = shifted(x_low, "gx", -1)
     inner = inner_partial(f, g)
     mine, theirs, halo, to_north, to_south = weight_partial(
-        facts, f, g, inner, y_high, from_west, from_east, from_north
+        facts, place, f, g, inner, y_high, from_west, from_east, from_north
     )
     got, weight = lax.optimization_barrier((swap(theirs, "gx", 1), weight))
     own = scatter_sum(mine + got)
-    mat, back = matrices(weight)
+    mat, back = matrix(False, weight), matrix(True, weight)
     own, mat, back, to_north = lax.optimization_barrier((own, mat, back, to_north))
     from_south = shifted(to_north, "gy", 1)
     step = 1
@@ -441,7 +482,7 @@
     half, feature_grad = lax.optimization_barrier((half, feature_grad))
 
     slot_count = lax.axis_size("gx") * lax.axis_size("gy") * VOX
-    weight_grad = make_result(facts, half, swap(half, "gx", 1), 1.0 / math.sqrt(slot_count))
+    weight_grad = make_result(place, half, swap(half, "gx", 1), 1.0 / math.sqrt(slot_count))
     out_shape = (1, 1, 1, C, VOX)
     return (outputs.reshape(out_shape), feature_grad.reshape(out_shape), weight_grad)
 

time: 84.9 us -> 81.3 us (0.958)
  waiting for transfers between devices: 14.4 us -> 10.4 us
  starting transfers between devices: 43.3 us -> 44.7 us
  other arithmetic: 1.79 us -> 0.83 us
    ppermute x5, waiting for transfers between devices: 4.87 us -> 1.4 us  [shifted(): return lax.ppermute(array, axis, pairs)]
    ppermute x6, starting transfers between devices: 20.4 us -> 23.8 us  [swap(): lax.ppermute(array, axis, [(i, i ^ mask) for i in range(lax.axis_size(axi...]
    ppermute x5, starting transfers between devices: 13.9 us -> 11.6 us  [shifted(): return lax.ppermute(array, axis, pairs)]
    pallas_call x1 -> x3, Pallas kernels: 3.92 us -> 5.36 us  [the longest x2 5.1 us: matrix(): pl.pallas_call(kernel, out_shape=jax.ShapeDtypeStruct((3 * C, 9 * C), BF1...]
    all_to_all x1, waiting for transfers between devices: 2.88 us -> 1.84 us  [scatter_sum(): lax.all_to_all(total.astype(BF16), 'gx', 0, 0, axis_index_groups=core_gro...]
    reduce_sum x1, other arithmetic: 0.99 us -> 0.04 us  [scatter_sum(): return got.astype(F32).sum(0)]
  transfers between devices with their start and end apart: 13 -> 13, of which waited for: 8 -> 7; matrix products, arithmetic and copies ran while one was open for 0% -> 0% of each run, Pallas kernels for 19% -> 21%
where the time goes in v3:
time: 81.3 us; the launch traced here: 80.8 us
  starting transfers between devices  44.7 us (55%)
  Pallas kernels  22.6 us (28%)
  waiting for transfers between devices  10.4 us (13%)
  local copies, waits for them, and re-layouts  1.39 us (2%)
  other arithmetic  0.83 us (1%)
  between operations  0.82 us (1%)
    ppermute x6, starting transfers between devices, swap(): lax.ppermute(array, axis, [(i, i ^ mask) for i in range(lax.axis_size(axi...  23.8 us
    ppermute x5, starting transfers between devices, shifted(): return lax.ppermute(array, axis, pairs)  11.6 us
    pallas_call x2, Pallas kernels, conv(): pl.pallas_call(kernel, out_shape=jax.ShapeDtypeStruct((C, VOX), BF16), in...  9.08 us
    ppermute x6, waiting for transfers between devices, swap(): lax.ppermute(array, axis, [(i, i ^ mask) for i in range(lax.axis_size(axi...  5.79 us
    all_to_all x1, starting transfers between devices, scatter_sum(): lax.all_to_all(total.astype(BF16), 'gx', 0, 0, axis_index_groups=core_gro...  5.71 us
    pallas_call x2, Pallas kernels, matrix(): pl.pallas_call(kernel, out_shape=jax.ShapeDtypeStruct((3 * C, 9 * C), BF1...  5.1 us
    all_to_all x1, starting transfers between devices, gather_sum(): got = lax.all_to_all(own, 'gx', 0, 0, axis_index_groups=core_groups())  3.59 us
    pallas_call x1, Pallas kernels, inner_partial(): pl.pallas_call(inner_kernel, out_shape=jax.ShapeDtypeStruct((3 * C, 7 * L...  2.73 us
  transfers between devices with their start and end apart: 13, of which 7 were waited for; matrix products, arithmetic and copies ran while one was open for 0% of the time, Pallas kernels for 21%

profile of v3, /device:TPU:1, one launch (start us, length us, event | category | flops | bytes accessed | tf_op | source)
XLA Modules:
  0.0 80.8 jit_solution(10118508125141707262)
XLA Ops:
  0.6 1.9 %shard_map.76 = (bf16[96,4096]{1,0:T(8,128)(2,1)S(1)}, bf16[96,4096]{1,0:T(8,128)(2,1)S(1)}, f32[1,4096]{1,0:T(1,128)S(1)}, bf16[208,256]{1,0:T(8,128)(2,1)S(1)}, bf16[2,96,32]{2,1,0:T(8,128)(2,1)S(1)}) custom-call(s32[1,6]{1,0:T(1,128)} %bitcast.11, bf16[96,4096]{1,0:T(8,128)(2,1)} %bitcast.15, bf16[96,4096]{1,0:T(8,128)(2,1)} %bitcast.16, s32[1,4096]{1,0:T(1,128)} %bitcast.17), custom_call_target="tpu_custom_call" | custom-call | flops 1048576 | bytes 3145728 | tf_op jit(solution)/shard_map/pallas_call | solution.py:109
  2.5 1.3 %collective-permute-start.2 = (bf16[208,256]{1,0:T(8,128)(2,1)S(1)}, bf16[208,256]{1,0:T(8,128)(2,1)S(1)}, u32[]{:S(2)}, u32[]{:S(2)}) collective-permute-start(bf16[208,256]{1,0:T(8,128)(2,1)S(1)} %get-tuple-element.34), channel_id=1, source_target_pairs={{1,0},{2,1},{3,2},{4,3},{5,4},{6,5},{7,6},{8,7},{9,8},{10,9},{11,1... | collective-permute-start | bytes 319496 | tf_op jit(solution)/shard_map/ppermute | solution.py:33
  3.8 0.3 shard_map.78
  4.1 4.5 %collective-permute-start = (bf16[208,256]{1,0:T(8,128)(2,1)S(1)}, bf16[208,256]{1,0:T(8,128)(2,1)S(1)}, u32[]{:S(2)}, u32[]{:S(2)}) collective-permute-start(bf16[208,256]{1,0:T(8,128)(2,1)S(1)} %get-tuple-element.32), channel_id=1, source_target_pairs={{0,16},{16,32},{32,48},{48,64},{64,80},{80,96},{96,112},{112,128},... | collective-permute-start | bytes 319496 | tf_op jit(solution)/shard_map/ppermute | solution.py:33
  8.6 1.9 %collective-permute-start.1 = (bf16[208,256]{1,0:T(8,128)(2,1)S(1)}, bf16[208,256]{1,0:T(8,128)(2,1)S(1)}, u32[]{:S(2)}, u32[]{:S(2)}) collective-permute-start(bf16[208,256]{1,0:T(8,128)(2,1)S(1)} %get-tuple-element.33), channel_id=1, source_target_pairs={{16,0},{32,16},{48,32},{64,48},{80,64},{96,80},{112,96},{128,112},... | collective-permute-start | bytes 319496 | tf_op jit(solution)/shard_map/ppermute | solution.py:33
  10.6 2.7 %shard_map.77.inner = f32[288,896]{1,0:T(8,128)S(1)} custom-call(bf16[96,4096]{1,0:T(8,128)(2,1)S(1)} %get-tuple-element.28.f.refs_1_, bf16[96,4096]{1,0:T(8,128)(2,1)S(1)} %get-tuple-element.29.g.refs_1_), custom_call_target="tpu_custom_call" | custom-call | flops 4076863488 | bytes 4194304 | tf_op jit(solution)/shard_map/pallas_call | solution.py:286
  13.3 0.0 collective-permute-done.2.from_north
  13.3 0.0 collective-permute-done.from_west
  13.3 1.4 %collective-permute-done.1.from_east = bf16[208,256]{1,0:T(8,128)(2,1)S(1)} collective-permute-done((bf16[208,256]{1,0:T(8,128)(2,1)S(1)}, bf16[208,256]{1,0:T(8,128)(2,1)S(1)}, u32[]{:S(2)}, u32[]{:S(2)}) %collective-permute-start.1) | collective-permute-done | bytes 106528 | tf_op jit(solution)/shard_map/ppermute | solution.py:33
  14.7 0.0 copy-start
  14.7 0.7 copy-done
  15.4 2.1 %shard_map.79 = (f32[1024,128]{1,0:T(8,128)S(1)}, f32[1024,128]{1,0:T(8,128)S(1)}, bf16[6,96,256]{2,1,0:T(8,128)(2,1)S(1)}, bf16[224,256]{1,0:T(8,128)(2,1)S(1)}, bf16[192,32]{1,0:T(8,128)(2,1)S(1)}) custom-call(s32[1,6]{1,0:T(1,128)S(1)} %bitcast.12, s32[1]{0:T(128)} %bitcast.1.place, bf16[96,4096]{1,0:T(8,128)(2,1)S(1)} %get-tuple-element.28.f.refs_1_, ...), custom_call_target="tpu_custom_call" | custom-call | flops 268435456 | bytes 4194304 | tf_op jit(solution)/shard_map/pallas_call | solution.py:394
  17.5 0.1 collective-permute-start.3
  17.6 1.9 %collective-permute-done.3 = f32[1024,128]{1,0:T(8,128)S(1)} collective-permute-done((f32[1024,128]{1,0:T(8,128)S(1)}, f32[1024,128]{1,0:T(8,128)S(1)}, u32[]{:S(2)}, u32[]{:S(2)}) %collective-permute-start.3) | collective-permute-done | bytes 524320 | tf_op jit(solution)/shard_map/ppermute | solution.py:37
  19.5 0.8 add_convert_fusion
  20.3 5.7 %all-to-all-start = ((bf16[8,128,128]{2,1,0:T(8,128)(2,1)}), bf16[8,128,128]{2,1,0:T(8,128)(2,1)S(1)}, u32[]{:S(2)}, u32[]{:S(2)}) async-start(bf16[8,128,128]{2,1,0:T(8,128)(2,1)} %bitcast.5), calls=%async_computation | async-start | bytes 524288 | tf_op jit(solution)/shard_map/all_to_all | solution.py:417
  26.0 3.8 %matrix_back.1.refs_5_ = bf16[288,864]{1,0:T(8,128)(2,1)S(1)} custom-call(bf16[96,2592]{1,0:T(8,128)(2,1)} %weight.1), custom_call_target="tpu_custom_call" | custom-call | flops 268435456 | bytes 6291456 | tf_op jit(solution)/shard_map/matrix_back/pallas_call | solution.py:166
  29.7 1.3 %matrix_out.1.refs_5_ = bf16[288,864]{1,0:T(8,128)(2,1)S(1)} custom-call(bf16[96,2592]{1,0:T(8,128)(2,1)} %weight.1), custom_call_target="tpu_custom_call" | custom-call | flops 268435456 | bytes 6291456 | tf_op jit(solution)/shard_map/matrix_out/pallas_call | solution.py:166
  31.1 1.8 %all-to-all-done = bf16[8,128,128]{2,1,0:T(8,128)(2,1)S(1)} async-done(((bf16[8,128,128]{2,1,0:T(8,128)(2,1)}), bf16[8,128,128]{2,1,0:T(8,128)(2,1)S(1)}, u32[]{:S(2)}, u32[]{:S(2)}) %all-to-all-start) | async-done | bytes 262176 | tf_op jit(solution)/shard_map/all_to_all | solution.py:417
  33.0 3.9 %collective-permute-start.4 = (f32[128,128]{1,0:T(8,128)S(1)}, f32[128,128]{1,0:T(8,128)S(1)}, u32[]{:S(2)}, u32[]{:S(2)}) collective-permute-start(f32[128,128]{1,0:T(8,128)S(1)} %convert_reduce_fusion), channel_id=1, source_target_pairs={{0,1},{1,0},{2,3},{3,2},{4,5},{5,4},{6,7},{7,6},{8,9},{9,8},{10,11... | collective-permute-start | bytes 196616 | tf_op jit(solution)/shard_map/ppermute | solution.py:37
  36.9 1.7 %collective-permute-done.4 = f32[128,128]{1,0:T(8,128)S(1)} collective-permute-done((f32[128,128]{1,0:T(8,128)S(1)}, f32[128,128]{1,0:T(8,128)S(1)}, u32[]{:S(2)}, u32[]{:S(2)}) %collective-permute-start.4) | collective-permute-done | bytes 65568 | tf_op jit(solution)/shard_map/ppermute | solution.py:37
  38.6 4.0 %collective-permute-start.5 = (f32[128,128]{1,0:T(8,128)S(1)}, f32[128,128]{1,0:T(8,128)S(1)}, u32[]{:S(2)}, u32[]{:S(2)}) collective-permute-start(f32[128,128]{1,0:T(8,128)S(1)} %add.21), channel_id=1, source_target_pairs={{0,2},{1,3},{2,0},{3,1},{4,6},{5,7},{6,4},{7,5},{8,10},{9,11},{10,... | collective-permute-start | bytes 196616 | tf_op jit(solution)/shard_map/ppermute | solution.py:37
  42.6 2.6 %collective-permute-start.8 = (bf16[224,256]{1,0:T(8,128)(2,1)S(1)}, bf16[224,256]{1,0:T(8,128)(2,1)S(1)}, u32[]{:S(2)}, u32[]{:S(2)}) collective-permute-start(bf16[224,256]{1,0:T(8,128)(2,1)S(1)} %get-tuple-element.44), channel_id=1, source_target_pairs={{0,1},{1,2},{2,3},{3,4},{4,5},{5,6},{6,7},{7,8},{8,9},{9,10},{10,1... | collective-permute-start | bytes 344072 | tf_op jit(solution)/shard_map/ppermute | solution.py:33
  45.2 0.0 collective-permute-done.5
  45.2 3.1 %collective-permute-start.6 = (f32[128,128]{1,0:T(8,128)S(1)}, f32[128,128]{1,0:T(8,128)S(1)}, u32[]{:S(2)}, u32[]{:S(2)}) collective-permute-start(f32[128,128]{1,0:T(8,128)S(1)} %add.22), channel_id=1, source_target_pairs={{0,4},{1,5},{2,6},{3,7},{4,0},{5,1},{6,2},{7,3},{8,12},{9,13},{10,... | collective-permute-start | bytes 196616 | tf_op jit(solution)/shard_map/ppermute | solution.py:37
  48.3 1.3 %collective-permute-start.9 = (bf16[192,32]{1,0:T(8,128)(2,1)S(1)}, bf16[192,32]{1,0:T(8,128)(2,1)S(1)}, u32[]{:S(2)}, u32[]{:S(2)}) collective-permute-start(bf16[192,32]{1,0:T(8,128)(2,1)S(1)} %get-tuple-element.45), channel_id=1, source_target_pairs={{1,0},{2,1},{3,2},{4,3},{5,4},{6,5},{7,6},{8,7},{9,8},{10,9},{11,1... | collective-permute-start | bytes 36872 | tf_op jit(solution)/shard_map/ppermute | solution.py:33
  49.6 1.1 %collective-permute-done.6 = f32[128,128]{1,0:T(8,128)S(1)} collective-permute-done((f32[128,128]{1,0:T(8,128)S(1)}, f32[128,128]{1,0:T(8,128)S(1)}, u32[]{:S(2)}, u32[]{:S(2)}) %collective-permute-start.6) | collective-permute-done | bytes 65568 | tf_op jit(solution)/shard_map/ppermute | solution.py:37
  50.7 8.0 %collective-permute-start.7 = (f32[128,128]{1,0:T(8,128)S(1)}, f32[128,128]{1,0:T(8,128)S(1)}, u32[]{:S(2)}, u32[]{:S(2)}) collective-permute-start(f32[128,128]{1,0:T(8,128)S(1)} %add.23), channel_id=1, source_target_pairs={{0,8},{1,9},{2,10},{3,11},{4,12},{5,13},{6,14},{7,15},{8,0},{9,1},... | collective-permute-start | bytes 196616 | tf_op jit(solution)/shard_map/ppermute | solution.py:37
  58.7 0.0 collective-permute-done.9.refs_4_
  58.7 0.0 collective-permute-done.8.refs_3_
  58.7 4.6 %conv_out.1 = bf16[96,4096]{1,0:T(8,128)(2,1)} custom-call(s32[1,6]{1,0:T(1,128)S(1)} %bitcast.13, bf16[96,4096]{1,0:T(8,128)(2,1)S(1)} %get-tuple-element.28.f.refs_1_, bf16[6,96,256]{2,1,0:T(8,128)(2,1)S(1)} %get-tuple-element.43.refs_2_, bf16[224,256]{1,0:T(8,128)(2,1)S(1)} %collective-permute-done.8.refs_3_, ...), custom_call_target="tpu_custom_call" | custom-call | flops 4076863488 | bytes 4194304 | tf_op jit(solution)/shard_map/conv_out/pallas_call | solution.py:236
  63.3 0.0 collective-permute-done.7
  63.3 0.7 broadcast_in_dim.10
  64.0 3.6 %all-to-all-start.1 = ((bf16[8,128,128]{2,1,0:T(8,128)(2,1)}), bf16[8,128,128]{2,1,0:T(8,128)(2,1)S(1)}, u32[]{:S(2)}, u32[]{:S(2)}) async-start(bf16[8,128,128]{2,1,0:T(8,128)(2,1)} %broadcast_in_dim.10), calls=%async_computation.1 | async-start | bytes 524288 | tf_op jit(solution)/shard_map/all_to_all | solution.py:424
  67.6 4.5 %conv_back.1 = bf16[96,4096]{1,0:T(8,128)(2,1)} custom-call(s32[1,6]{1,0:T(1,128)S(1)} %bitcast.14, bf16[96,4096]{1,0:T(8,128)(2,1)S(1)} %get-tuple-element.29.g.refs_1_, bf16[6,96,256]{2,1,0:T(8,128)(2,1)S(1)} %get-tuple-element.43.refs_2_, bf16[224,256]{1,0:T(8,128)(2,1)S(1)} %collective-permute-done.8.refs_3_, ...), custom_call_target="tpu_custom_call" | custom-call | flops 4076863488 | bytes 4194304 | tf_op jit(solution)/shard_map/conv_back/pallas_call | solution.py:236
  72.1 1.4 %all-to-all-done.1 = bf16[8,128,128]{2,1,0:T(8,128)(2,1)S(1)} async-done(((bf16[8,128,128]{2,1,0:T(8,128)(2,1)}), bf16[8,128,128]{2,1,0:T(8,128)(2,1)S(1)}, u32[]{:S(2)}, u32[]{:S(2)}) %all-to-all-start.1) | async-done | bytes 262176 | tf_op jit(solution)/shard_map/all_to_all | solution.py:424
  73.5 4.7 %collective-permute-start.10 = (bf16[1024,128]{1,0:T(8,128)(2,1)S(1)}, bf16[1024,128]{1,0:T(8,128)(2,1)S(1)}, u32[]{:S(2)}, u32[]{:S(2)}) collective-permute-start(bf16[1024,128]{1,0:T(8,128)(2,1)S(1)} %bitcast.9), channel_id=1, source_target_pairs={{0,16},{16,0},{32,48},{48,32},{64,80},{80,64},{96,112},{112,96},{1... | collective-permute-start | bytes 786440 | tf_op jit(solution)/shard_map/ppermute | solution.py:37
  78.2 1.2 %collective-permute-done.10.other = bf16[1024,128]{1,0:T(8,128)(2,1)S(1)} collective-permute-done((bf16[1024,128]{1,0:T(8,128)(2,1)S(1)}, bf16[1024,128]{1,0:T(8,128)(2,1)S(1)}, u32[]{:S(2)}, u32[]{:S(2)}) %collective-permute-start.10) | collective-permute-done | bytes 262176 | tf_op jit(solution)/shard_map/ppermute | solution.py:37
  79.4 1.4 %shard_map.80 = f32[96,2592]{1,0:T(8,128)} custom-call(s32[1]{0:T(128)} %bitcast.1.place, bf16[1024,128]{1,0:T(8,128)(2,1)S(1)} %bitcast.10, bf16[1024,128]{1,0:T(8,128)(2,1)S(1)} %collective-permute-done.10.other), custom_call_target="tpu_custom_call" | custom-call | flops 1048576 | bytes 2097152 | tf_op jit(solution)/shard_map/pallas_call | solution.py:440
  (5 shorter events, 0.1 us)
Async XLA Ops:
  2.5 10.8 %collective-permute-start.2 = (bf16[208,256]{1,0:T(8,128)(2,1)S(1)}, bf16[208,256]{1,0:T(8,128)(2,1)S(1)}, u32[]{:S(2)}, u32[]{:S(2)}) collective-permute-start(bf16[208,256]{1,0:T(8,128)(2,1)S(1)} %get-tuple-element.34), channel_id=1, source_target_pairs={{1,0},{2,1},{3,2},{4,3},{5,4},{6,5},{7,6},{8,7},{9,8},{10,9},{11,1... | collective-permute-start | bytes 319496 | tf_op jit(solution)/shard_map/ppermute | solution.py:33
  4.1 9.2 %collective-permute-start = (bf16[208,256]{1,0:T(8,128)(2,1)S(1)}, bf16[208,256]{1,0:T(8,128)(2,1)S(1)}, u32[]{:S(2)}, u32[]{:S(2)}) collective-permute-start(bf16[208,256]{1,0:T(8,128)(2,1)S(1)} %get-tuple-element.32), channel_id=1, source_target_pairs={{0,16},{16,32},{32,48},{48,64},{64,80},{80,96},{96,112},{112,128},... | collective-permute-start | bytes 319496 | tf_op jit(solution)/shard_map/ppermute | solution.py:33
  8.6 6.1 %collective-permute-start.1 = (bf16[208,256]{1,0:T(8,128)(2,1)S(1)}, bf16[208,256]{1,0:T(8,128)(2,1)S(1)}, u32[]{:S(2)}, u32[]{:S(2)}) collective-permute-start(bf16[208,256]{1,0:T(8,128)(2,1)S(1)} %get-tuple-element.33), channel_id=1, source_target_pairs={{16,0},{32,16},{48,32},{64,48},{80,64},{96,80},{112,96},{128,112},... | collective-permute-start | bytes 319496 | tf_op jit(solution)/shard_map/ppermute | solution.py:33
  14.7 0.7 copy-start
  17.5 2.0 %collective-permute-start.3 = (f32[1024,128]{1,0:T(8,128)S(1)}, f32[1024,128]{1,0:T(8,128)S(1)}, u32[]{:S(2)}, u32[]{:S(2)}) collective-permute-start(f32[1024,128]{1,0:T(8,128)S(1)} %get-tuple-element.36), channel_id=1, source_target_pairs={{0,16},{16,0},{32,48},{48,32},{64,80},{80,64},{96,112},{112,96},{1... | collective-permute-start | bytes 1572872 | tf_op jit(solution)/shard_map/ppermute | solution.py:37
  20.3 12.7 %all-to-all-start = ((bf16[8,128,128]{2,1,0:T(8,128)(2,1)}), bf16[8,128,128]{2,1,0:T(8,128)(2,1)S(1)}, u32[]{:S(2)}, u32[]{:S(2)}) async-start(bf16[8,128,128]{2,1,0:T(8,128)(2,1)} %bitcast.5), calls=%async_computation | async-start | bytes 524288 | tf_op jit(solution)/shard_map/all_to_all | solution.py:417
  33.0 5.6 %collective-permute-start.4 = (f32[128,128]{1,0:T(8,128)S(1)}, f32[128,128]{1,0:T(8,128)S(1)}, u32[]{:S(2)}, u32[]{:S(2)}) collective-permute-start(f32[128,128]{1,0:T(8,128)S(1)} %convert_reduce_fusion), channel_id=1, source_target_pairs={{0,1},{1,0},{2,3},{3,2},{4,5},{5,4},{6,7},{7,6},{8,9},{9,8},{10,11... | collective-permute-start | bytes 196616 | tf_op jit(solution)/shard_map/ppermute | solution.py:37
  38.6 6.6 %collective-permute-start.5 = (f32[128,128]{1,0:T(8,128)S(1)}, f32[128,128]{1,0:T(8,128)S(1)}, u32[]{:S(2)}, u32[]{:S(2)}) collective-permute-start(f32[128,128]{1,0:T(8,128)S(1)} %add.21), channel_id=1, source_target_pairs={{0,2},{1,3},{2,0},{3,1},{4,6},{5,7},{6,4},{7,5},{8,10},{9,11},{10,... | collective-permute-start | bytes 196616 | tf_op jit(solution)/shard_map/ppermute | solution.py:37
  42.6 16.1 %collective-permute-start.8 = (bf16[224,256]{1,0:T(8,128)(2,1)S(1)}, bf16[224,256]{1,0:T(8,128)(2,1)S(1)}, u32[]{:S(2)}, u32[]{:S(2)}) collective-permute-start(bf16[224,256]{1,0:T(8,128)(2,1)S(1)} %get-tuple-element.44), channel_id=1, source_target_pairs={{0,1},{1,2},{2,3},{3,4},{4,5},{5,6},{6,7},{7,8},{8,9},{9,10},{10,1... | collective-permute-start | bytes 344072 | tf_op jit(solution)/shard_map/ppermute | solution.py:33
  45.2 5.4 %collective-permute-start.6 = (f32[128,128]{1,0:T(8,128)S(1)}, f32[128,128]{1,0:T(8,128)S(1)}, u32[]{:S(2)}, u32[]{:S(2)}) collective-permute-start(f32[128,128]{1,0:T(8,128)S(1)} %add.22), channel_id=1, source_target_pairs={{0,4},{1,5},{2,6},{3,7},{4,0},{5,1},{6,2},{7,3},{8,12},{9,13},{10,... | collective-permute-start | bytes 196616 | tf_op jit(solution)/shard_map/ppermute | solution.py:37
  48.3 10.4 %collective-permute-start.9 = (bf16[192,32]{1,0:T(8,128)(2,1)S(1)}, bf16[192,32]{1,0:T(8,128)(2,1)S(1)}, u32[]{:S(2)}, u32[]{:S(2)}) collective-permute-start(bf16[192,32]{1,0:T(8,128)(2,1)S(1)} %get-tuple-element.45), channel_id=1, source_target_pairs={{1,0},{2,1},{3,2},{4,3},{5,4},{6,5},{7,6},{8,7},{9,8},{10,9},{11,1... | collective-permute-start | bytes 36872 | tf_op jit(solution)/shard_map/ppermute | solution.py:33
  50.7 12.6 %collective-permute-start.7 = (f32[128,128]{1,0:T(8,128)S(1)}, f32[128,128]{1,0:T(8,128)S(1)}, u32[]{:S(2)}, u32[]{:S(2)}) collective-permute-start(f32[128,128]{1,0:T(8,128)S(1)} %add.23), channel_id=1, source_target_pairs={{0,8},{1,9},{2,10},{3,11},{4,12},{5,13},{6,14},{7,15},{8,0},{9,1},... | collective-permute-start | bytes 196616 | tf_op jit(solution)/shard_map/ppermute | solution.py:37
  64.0 9.5 %all-to-all-start.1 = ((bf16[8,128,128]{2,1,0:T(8,128)(2,1)}), bf16[8,128,128]{2,1,0:T(8,128)(2,1)S(1)}, u32[]{:S(2)}, u32[]{:S(2)}) async-start(bf16[8,128,128]{2,1,0:T(8,128)(2,1)} %broadcast_in_dim.10), calls=%async_computation.1 | async-start | bytes 524288 | tf_op jit(solution)/shard_map/all_to_all | solution.py:424
  73.5 5.8 %collective-permute-start.10 = (bf16[1024,128]{1,0:T(8,128)(2,1)S(1)}, bf16[1024,128]{1,0:T(8,128)(2,1)S(1)}, u32[]{:S(2)}, u32[]{:S(2)}) collective-permute-start(bf16[1024,128]{1,0:T(8,128)(2,1)S(1)} %bitcast.9), channel_id=1, source_target_pairs={{0,16},{16,0},{32,48},{48,32},{64,80},{80,64},{96,112},{112,96},{1... | collective-permute-start | bytes 786440 | tf_op jit(solution)/shard_map/ppermute | solution.py:37

commit v4 on v3

--- a/solution.py
+++ b/solution.py
@@ -312,7 +312,6 @@
     x_in,
     y_in,
     acc,
-    flat,
     sems,
 ):
     copies = start_all(
@@ -375,12 +374,24 @@
         (8, on_west[:, BS:], on_north[:, :BS]),
     ):
         add(ab, z_stack(widen(g_edge)), widen(f_edge))
-    for tile in range(7):
-        flat[tile * 3 * C : (tile + 1) * 3 * C] = acc[:, tile * LANES : (tile + 1) * LANES]
-    flat[21 * C :] = jnp.zeros((ROWS - 21 * C, LANES), F32)
-    core = place[0]
-    mine[...] = flat[pl.ds(pl.multiple_of(core * HALF, HALF), HALF)]
-    theirs[...] = flat[pl.ds(pl.multiple_of((1 - core) * HALF, HALF), HALF)]
+
+    def spread(halves):
+        for tile in range(7):
+            start = tile * 3 * C
+            for h in range(2):
+                low, high = max(start, h * HALF), min(start + 3 * C, (h + 1) * HALF)
+                if low < high:
+                    rows = acc[low - start : high - start, tile * LANES : (tile + 1) * LANES]
+                    halves[h][low - h * HALF : high - h * HALF, :] = rows
+        halves[1][21 * C - HALF :, :] = jnp.zeros((ROWS - 21 * C, LANES), F32)
+
+    @pl.when(place[0] == 0)
+    def _():
+        spread((mine, theirs))
+
+    @pl.when(place[0] == 1)
+    def _():
+        spread((theirs, mine))
 
 
 def widen(values):
@@ -400,7 +411,6 @@
             pltpu.VMEM((2, *MESSAGE), BF16),
             pltpu.VMEM(MESSAGE, BF16),
             pltpu.VMEM((3 * C, 7 * LANES), F32),
-            pltpu.VMEM((ROWS, LANES), F32),
             pltpu.SemaphoreType.DMA((3,)),
         ],
         compiler_params=LIMIT,

time: 81.3 us -> 81.4 us (level)
  no operation moved by 1% of the time
where the time goes in v4:
time: 81.4 us; the launch traced here: 80.9 us
  starting transfers between devices  44.7 us (55%)
  Pallas kernels  22.5 us (28%)
  waiting for transfers between devices  10.6 us (13%)
  local copies, waits for them, and re-layouts  1.39 us (2%)
  other arithmetic  0.83 us (1%)
  between operations  0.82 us (1%)
    ppermute x6, starting transfers between devices, swap(): lax.ppermute(array, axis, [(i, i ^ mask) for i in range(lax.axis_size(axi...  23.8 us
    ppermute x5, starting transfers between devices, shifted(): return lax.ppermute(array, axis, pairs)  11.6 us
    pallas_call x2, Pallas kernels, conv(): pl.pallas_call(kernel, out_shape=jax.ShapeDtypeStruct((C, VOX), BF16), in...  9.07 us
    ppermute x6, waiting for transfers between devices, swap(): lax.ppermute(array, axis, [(i, i ^ mask) for i in range(lax.axis_size(axi...  5.79 us
    all_to_all x1, starting transfers between devices, scatter_sum(): lax.all_to_all(total.astype(BF16), 'gx', 0, 0, axis_index_groups=core_gro...  5.7 us
    pallas_call x2, Pallas kernels, matrix(): pl.pallas_call(kernel, out_shape=jax.ShapeDtypeStruct((3 * C, 9 * C), BF1...  5.1 us
    all_to_all x1, starting transfers between devices, gather_sum(): got = lax.all_to_all(own, 'gx', 0, 0, axis_index_groups=core_groups())  3.59 us
    pallas_call x1, Pallas kernels, inner_partial(): pl.pallas_call(inner_kernel, out_shape=jax.ShapeDtypeStruct((3 * C, 7 * L...  2.73 us
  transfers between devices with their start and end apart: 13, of which 7 were waited for; matrix products, arithmetic and copies ran while one was open for 0% of the time, Pallas kernels for 21%

profile of v4, /device:TPU:1, one launch (start us, length us, event | category | flops | bytes accessed | tf_op | source)
XLA Modules:
  0.0 80.9 jit_solution(1640737604207290745)
XLA Ops:
  0.6 1.9 %shard_map.76 = (bf16[96,4096]{1,0:T(8,128)(2,1)S(1)}, bf16[96,4096]{1,0:T(8,128)(2,1)S(1)}, f32[1,4096]{1,0:T(1,128)S(1)}, bf16[208,256]{1,0:T(8,128)(2,1)S(1)}, bf16[2,96,32]{2,1,0:T(8,128)(2,1)S(1)}) custom-call(s32[1,6]{1,0:T(1,128)} %bitcast.11, bf16[96,4096]{1,0:T(8,128)(2,1)} %bitcast.15, bf16[96,4096]{1,0:T(8,128)(2,1)} %bitcast.16, s32[1,4096]{1,0:T(1,128)} %bitcast.17), custom_call_target="tpu_custom_call" | custom-call | flops 1048576 | bytes 3145728 | tf_op jit(solution)/shard_map/pallas_call | solution.py:109
  2.5 1.3 %collective-permute-start.2 = (bf16[208,256]{1,0:T(8,128)(2,1)S(1)}, bf16[208,256]{1,0:T(8,128)(2,1)S(1)}, u32[]{:S(2)}, u32[]{:S(2)}) collective-permute-start(bf16[208,256]{1,0:T(8,128)(2,1)S(1)} %get-tuple-element.34), channel_id=1, source_target_pairs={{1,0},{2,1},{3,2},{4,3},{5,4},{6,5},{7,6},{8,7},{9,8},{10,9},{11,1... | collective-permute-start | bytes 319496 | tf_op jit(solution)/shard_map/ppermute | solution.py:33
  3.8 0.3 shard_map.78
  4.1 4.5 %collective-permute-start = (bf16[208,256]{1,0:T(8,128)(2,1)S(1)}, bf16[208,256]{1,0:T(8,128)(2,1)S(1)}, u32[]{:S(2)}, u32[]{:S(2)}) collective-permute-start(bf16[208,256]{1,0:T(8,128)(2,1)S(1)} %get-tuple-element.32), channel_id=1, source_target_pairs={{0,16},{16,32},{32,48},{48,64},{64,80},{80,96},{96,112},{112,128},... | collective-permute-start | bytes 319496 | tf_op jit(solution)/shard_map/ppermute | solution.py:33
  8.6 1.9 %collective-permute-start.1 = (bf16[208,256]{1,0:T(8,128)(2,1)S(1)}, bf16[208,256]{1,0:T(8,128)(2,1)S(1)}, u32[]{:S(2)}, u32[]{:S(2)}) collective-permute-start(bf16[208,256]{1,0:T(8,128)(2,1)S(1)} %get-tuple-element.33), channel_id=1, source_target_pairs={{16,0},{32,16},{48,32},{64,48},{80,64},{96,80},{112,96},{128,112},... | collective-permute-start | bytes 319496 | tf_op jit(solution)/shard_map/ppermute | solution.py:33
  10.6 2.7 %shard_map.77.inner = f32[288,896]{1,0:T(8,128)S(1)} custom-call(bf16[96,4096]{1,0:T(8,128)(2,1)S(1)} %get-tuple-element.28.f.refs_1_, bf16[96,4096]{1,0:T(8,128)(2,1)S(1)} %get-tuple-element.29.g.refs_1_), custom_call_target="tpu_custom_call" | custom-call | flops 4076863488 | bytes 4194304 | tf_op jit(solution)/shard_map/pallas_call | solution.py:286
  13.3 0.0 collective-permute-done.2.from_north
  13.3 0.0 collective-permute-done.from_west
  13.3 1.4 %collective-permute-done.1.from_east = bf16[208,256]{1,0:T(8,128)(2,1)S(1)} collective-permute-done((bf16[208,256]{1,0:T(8,128)(2,1)S(1)}, bf16[208,256]{1,0:T(8,128)(2,1)S(1)}, u32[]{:S(2)}, u32[]{:S(2)}) %collective-permute-start.1) | collective-permute-done | bytes 106528 | tf_op jit(solution)/shard_map/ppermute | solution.py:33
  14.7 0.0 copy-start
  14.7 0.7 copy-done
  15.4 2.1 %shard_map.79 = (f32[1024,128]{1,0:T(8,128)S(1)}, f32[1024,128]{1,0:T(8,128)S(1)}, bf16[6,96,256]{2,1,0:T(8,128)(2,1)S(1)}, bf16[224,256]{1,0:T(8,128)(2,1)S(1)}, bf16[192,32]{1,0:T(8,128)(2,1)S(1)}) custom-call(s32[1,6]{1,0:T(1,128)S(1)} %bitcast.12, s32[1]{0:T(128)} %bitcast.1.place, bf16[96,4096]{1,0:T(8,128)(2,1)S(1)} %get-tuple-element.28.f.refs_1_, ...), custom_call_target="tpu_custom_call" | custom-call | flops 268435456 | bytes 4194304 | tf_op jit(solution)/shard_map/pallas_call | solution.py:405
  17.4 0.1 collective-permute-start.3
  17.5 1.9 %collective-permute-done.3 = f32[1024,128]{1,0:T(8,128)S(1)} collective-permute-done((f32[1024,128]{1,0:T(8,128)S(1)}, f32[1024,128]{1,0:T(8,128)S(1)}, u32[]{:S(2)}, u32[]{:S(2)}) %collective-permute-start.3) | collective-permute-done | bytes 524320 | tf_op jit(solution)/shard_map/ppermute | solution.py:37
  19.4 0.8 add_convert_fusion
  20.2 5.7 %all-to-all-start = ((bf16[8,128,128]{2,1,0:T(8,128)(2,1)}), bf16[8,128,128]{2,1,0:T(8,128)(2,1)S(1)}, u32[]{:S(2)}, u32[]{:S(2)}) async-start(bf16[8,128,128]{2,1,0:T(8,128)(2,1)} %bitcast.5), calls=%async_computation | async-start | bytes 524288 | tf_op jit(solution)/shard_map/all_to_all | solution.py:427
  25.9 3.8 %matrix_back.1.refs_5_ = bf16[288,864]{1,0:T(8,128)(2,1)S(1)} custom-call(bf16[96,2592]{1,0:T(8,128)(2,1)} %weight.1), custom_call_target="tpu_custom_call" | custom-call | flops 268435456 | bytes 6291456 | tf_op jit(solution)/shard_map/matrix_back/pallas_call | solution.py:166
  29.7 1.3 %matrix_out.1.refs_5_ = bf16[288,864]{1,0:T(8,128)(2,1)S(1)} custom-call(bf16[96,2592]{1,0:T(8,128)(2,1)} %weight.1), custom_call_target="tpu_custom_call" | custom-call | flops 268435456 | bytes 6291456 | tf_op jit(solution)/shard_map/matrix_out/pallas_call | solution.py:166
  31.0 1.8 %all-to-all-done = bf16[8,128,128]{2,1,0:T(8,128)(2,1)S(1)} async-done(((bf16[8,128,128]{2,1,0:T(8,128)(2,1)}), bf16[8,128,128]{2,1,0:T(8,128)(2,1)S(1)}, u32[]{:S(2)}, u32[]{:S(2)}) %all-to-all-start) | async-done | bytes 262176 | tf_op jit(solution)/shard_map/all_to_all | solution.py:427
  32.9 4.0 %collective-permute-start.4 = (f32[128,128]{1,0:T(8,128)S(1)}, f32[128,128]{1,0:T(8,128)S(1)}, u32[]{:S(2)}, u32[]{:S(2)}) collective-permute-start(f32[128,128]{1,0:T(8,128)S(1)} %convert_reduce_fusion), channel_id=1, source_target_pairs={{0,1},{1,0},{2,3},{3,2},{4,5},{5,4},{6,7},{7,6},{8,9},{9,8},{10,11... | collective-permute-start | bytes 196616 | tf_op jit(solution)/shard_map/ppermute | solution.py:37
  36.8 1.7 %collective-permute-done.4 = f32[128,128]{1,0:T(8,128)S(1)} collective-permute-done((f32[128,128]{1,0:T(8,128)S(1)}, f32[128,128]{1,0:T(8,128)S(1)}, u32[]{:S(2)}, u32[]{:S(2)}) %collective-permute-start.4) | collective-permute-done | bytes 65568 | tf_op jit(solution)/shard_map/ppermute | solution.py:37
  38.5 4.0 %collective-permute-start.5 = (f32[128,128]{1,0:T(8,128)S(1)}, f32[128,128]{1,0:T(8,128)S(1)}, u32[]{:S(2)}, u32[]{:S(2)}) collective-permute-start(f32[128,128]{1,0:T(8,128)S(1)} %add.21), channel_id=1, source_target_pairs={{0,2},{1,3},{2,0},{3,1},{4,6},{5,7},{6,4},{7,5},{8,10},{9,11},{10,... | collective-permute-start | bytes 196616 | tf_op jit(solution)/shard_map/ppermute | solution.py:37
  42.5 2.6 %collective-permute-start.8 = (bf16[224,256]{1,0:T(8,128)(2,1)S(1)}, bf16[224,256]{1,0:T(8,128)(2,1)S(1)}, u32[]{:S(2)}, u32[]{:S(2)}) collective-permute-start(bf16[224,256]{1,0:T(8,128)(2,1)S(1)} %get-tuple-element.44), channel_id=1, source_target_pairs={{0,1},{1,2},{2,3},{3,4},{4,5},{5,6},{6,7},{7,8},{8,9},{9,10},{10,1... | collective-permute-start | bytes 344072 | tf_op jit(solution)/shard_map/ppermute | solution.py:33
  45.1 0.0 collective-permute-done.5
  45.1 3.1 %collective-permute-start.6 = (f32[128,128]{1,0:T(8,128)S(1)}, f32[128,128]{1,0:T(8,128)S(1)}, u32[]{:S(2)}, u32[]{:S(2)}) collective-permute-start(f32[128,128]{1,0:T(8,128)S(1)} %add.22), channel_id=1, source_target_pairs={{0,4},{1,5},{2,6},{3,7},{4,0},{5,1},{6,2},{7,3},{8,12},{9,13},{10,... | collective-permute-start | bytes 196616 | tf_op jit(solution)/shard_map/ppermute | solution.py:37
  48.2 1.3 %collective-permute-start.9 = (bf16[192,32]{1,0:T(8,128)(2,1)S(1)}, bf16[192,32]{1,0:T(8,128)(2,1)S(1)}, u32[]{:S(2)}, u32[]{:S(2)}) collective-permute-start(bf16[192,32]{1,0:T(8,128)(2,1)S(1)} %get-tuple-element.45), channel_id=1, source_target_pairs={{1,0},{2,1},{3,2},{4,3},{5,4},{6,5},{7,6},{8,7},{9,8},{10,9},{11,1... | collective-permute-start | bytes 36872 | tf_op jit(solution)/shard_map/ppermute | solution.py:33
  49.5 1.1 %collective-permute-done.6 = f32[128,128]{1,0:T(8,128)S(1)} collective-permute-done((f32[128,128]{1,0:T(8,128)S(1)}, f32[128,128]{1,0:T(8,128)S(1)}, u32[]{:S(2)}, u32[]{:S(2)}) %collective-permute-start.6) | collective-permute-done | bytes 65568 | tf_op jit(solution)/shard_map/ppermute | solution.py:37
  50.6 8.0 %collective-permute-start.7 = (f32[128,128]{1,0:T(8,128)S(1)}, f32[128,128]{1,0:T(8,128)S(1)}, u32[]{:S(2)}, u32[]{:S(2)}) collective-permute-start(f32[128,128]{1,0:T(8,128)S(1)} %add.23), channel_id=1, source_target_pairs={{0,8},{1,9},{2,10},{3,11},{4,12},{5,13},{6,14},{7,15},{8,0},{9,1},... | collective-permute-start | bytes 196616 | tf_op jit(solution)/shard_map/ppermute | solution.py:37
  58.6 0.0 collective-permute-done.9.refs_4_
  58.6 0.0 collective-permute-done.8.refs_3_
  58.6 4.6 %conv_out.1 = bf16[96,4096]{1,0:T(8,128)(2,1)} custom-call(s32[1,6]{1,0:T(1,128)S(1)} %bitcast.13, bf16[96,4096]{1,0:T(8,128)(2,1)S(1)} %get-tuple-element.28.f.refs_1_, bf16[6,96,256]{2,1,0:T(8,128)(2,1)S(1)} %get-tuple-element.43.refs_2_, bf16[224,256]{1,0:T(8,128)(2,1)S(1)} %collective-permute-done.8.refs_3_, ...), custom_call_target="tpu_custom_call" | custom-call | flops 4076863488 | bytes 4194304 | tf_op jit(solution)/shard_map/conv_out/pallas_call | solution.py:236
  63.2 0.0 collective-permute-done.7
  63.2 0.7 broadcast_in_dim.10
  63.9 3.6 %all-to-all-start.1 = ((bf16[8,128,128]{2,1,0:T(8,128)(2,1)}), bf16[8,128,128]{2,1,0:T(8,128)(2,1)S(1)}, u32[]{:S(2)}, u32[]{:S(2)}) async-start(bf16[8,128,128]{2,1,0:T(8,128)(2,1)} %broadcast_in_dim.10), calls=%async_computation.1 | async-start | bytes 524288 | tf_op jit(solution)/shard_map/all_to_all | solution.py:434
  67.5 4.5 %conv_back.1 = bf16[96,4096]{1,0:T(8,128)(2,1)} custom-call(s32[1,6]{1,0:T(1,128)S(1)} %bitcast.14, bf16[96,4096]{1,0:T(8,128)(2,1)S(1)} %get-tuple-element.29.g.refs_1_, bf16[6,96,256]{2,1,0:T(8,128)(2,1)S(1)} %get-tuple-element.43.refs_2_, bf16[224,256]{1,0:T(8,128)(2,1)S(1)} %collective-permute-done.8.refs_3_, ...), custom_call_target="tpu_custom_call" | custom-call | flops 4076863488 | bytes 4194304 | tf_op jit(solution)/shard_map/conv_back/pallas_call | solution.py:236
  72.0 1.6 %all-to-all-done.1 = bf16[8,128,128]{2,1,0:T(8,128)(2,1)S(1)} async-done(((bf16[8,128,128]{2,1,0:T(8,128)(2,1)}), bf16[8,128,128]{2,1,0:T(8,128)(2,1)S(1)}, u32[]{:S(2)}, u32[]{:S(2)}) %all-to-all-start.1) | async-done | bytes 262176 | tf_op jit(solution)/shard_map/all_to_all | solution.py:434
  73.6 4.7 %collective-permute-start.10 = (bf16[1024,128]{1,0:T(8,128)(2,1)S(1)}, bf16[1024,128]{1,0:T(8,128)(2,1)S(1)}, u32[]{:S(2)}, u32[]{:S(2)}) collective-permute-start(bf16[1024,128]{1,0:T(8,128)(2,1)S(1)} %bitcast.9), channel_id=1, source_target_pairs={{0,16},{16,0},{32,48},{48,32},{64,80},{80,64},{96,112},{112,96},{1... | collective-permute-start | bytes 786440 | tf_op jit(solution)/shard_map/ppermute | solution.py:37
  78.3 1.2 %collective-permute-done.10.other = bf16[1024,128]{1,0:T(8,128)(2,1)S(1)} collective-permute-done((bf16[1024,128]{1,0:T(8,128)(2,1)S(1)}, bf16[1024,128]{1,0:T(8,128)(2,1)S(1)}, u32[]{:S(2)}, u32[]{:S(2)}) %collective-permute-start.10) | collective-permute-done | bytes 262176 | tf_op jit(solution)/shard_map/ppermute | solution.py:37
  79.5 1.4 %shard_map.80 = f32[96,2592]{1,0:T(8,128)} custom-call(s32[1]{0:T(128)} %bitcast.1.place, bf16[1024,128]{1,0:T(8,128)(2,1)S(1)} %bitcast.10, bf16[1024,128]{1,0:T(8,128)(2,1)S(1)} %collective-permute-done.10.other), custom_call_target="tpu_custom_call" | custom-call | flops 1048576 | bytes 2097152 | tf_op jit(solution)/shard_map/pallas_call | solution.py:450
  (5 shorter events, 0.1 us)
Async XLA Ops:
  2.5 10.8 %collective-permute-start.2 = (bf16[208,256]{1,0:T(8,128)(2,1)S(1)}, bf16[208,256]{1,0:T(8,128)(2,1)S(1)}, u32[]{:S(2)}, u32[]{:S(2)}) collective-permute-start(bf16[208,256]{1,0:T(8,128)(2,1)S(1)} %get-tuple-element.34), channel_id=1, source_target_pairs={{1,0},{2,1},{3,2},{4,3},{5,4},{6,5},{7,6},{8,7},{9,8},{10,9},{11,1... | collective-permute-start | bytes 319496 | tf_op jit(solution)/shard_map/ppermute | solution.py:33
  4.1 9.2 %collective-permute-start = (bf16[208,256]{1,0:T(8,128)(2,1)S(1)}, bf16[208,256]{1,0:T(8,128)(2,1)S(1)}, u32[]{:S(2)}, u32[]{:S(2)}) collective-permute-start(bf16[208,256]{1,0:T(8,128)(2,1)S(1)} %get-tuple-element.32), channel_id=1, source_target_pairs={{0,16},{16,32},{32,48},{48,64},{64,80},{80,96},{96,112},{112,128},... | collective-permute-start | bytes 319496 | tf_op jit(solution)/shard_map/ppermute | solution.py:33
  8.6 6.1 %collective-permute-start.1 = (bf16[208,256]{1,0:T(8,128)(2,1)S(1)}, bf16[208,256]{1,0:T(8,128)(2,1)S(1)}, u32[]{:S(2)}, u32[]{:S(2)}) collective-permute-start(bf16[208,256]{1,0:T(8,128)(2,1)S(1)} %get-tuple-element.33), channel_id=1, source_target_pairs={{16,0},{32,16},{48,32},{64,48},{80,64},{96,80},{112,96},{128,112},... | collective-permute-start | bytes 319496 | tf_op jit(solution)/shard_map/ppermute | solution.py:33
  14.7 0.7 copy-start
  17.4 2.0 %collective-permute-start.3 = (f32[1024,128]{1,0:T(8,128)S(1)}, f32[1024,128]{1,0:T(8,128)S(1)}, u32[]{:S(2)}, u32[]{:S(2)}) collective-permute-start(f32[1024,128]{1,0:T(8,128)S(1)} %get-tuple-element.36), channel_id=1, source_target_pairs={{0,16},{16,0},{32,48},{48,32},{64,80},{80,64},{96,112},{112,96},{1... | collective-permute-start | bytes 1572872 | tf_op jit(solution)/shard_map/ppermute | solution.py:37
  20.2 12.7 %all-to-all-start = ((bf16[8,128,128]{2,1,0:T(8,128)(2,1)}), bf16[8,128,128]{2,1,0:T(8,128)(2,1)S(1)}, u32[]{:S(2)}, u32[]{:S(2)}) async-start(bf16[8,128,128]{2,1,0:T(8,128)(2,1)} %bitcast.5), calls=%async_computation | async-start | bytes 524288 | tf_op jit(solution)/shard_map/all_to_all | solution.py:427
  32.9 5.6 %collective-permute-start.4 = (f32[128,128]{1,0:T(8,128)S(1)}, f32[128,128]{1,0:T(8,128)S(1)}, u32[]{:S(2)}, u32[]{:S(2)}) collective-permute-start(f32[128,128]{1,0:T(8,128)S(1)} %convert_reduce_fusion), channel_id=1, source_target_pairs={{0,1},{1,0},{2,3},{3,2},{4,5},{5,4},{6,7},{7,6},{8,9},{9,8},{10,11... | collective-permute-start | bytes 196616 | tf_op jit(solution)/shard_map/ppermute | solution.py:37
  38.5 6.6 %collective-permute-start.5 = (f32[128,128]{1,0:T(8,128)S(1)}, f32[128,128]{1,0:T(8,128)S(1)}, u32[]{:S(2)}, u32[]{:S(2)}) collective-permute-start(f32[128,128]{1,0:T(8,128)S(1)} %add.21), channel_id=1, source_target_pairs={{0,2},{1,3},{2,0},{3,1},{4,6},{5,7},{6,4},{7,5},{8,10},{9,11},{10,... | collective-permute-start | bytes 196616 | tf_op jit(solution)/shard_map/ppermute | solution.py:37
  42.5 16.1 %collective-permute-start.8 = (bf16[224,256]{1,0:T(8,128)(2,1)S(1)}, bf16[224,256]{1,0:T(8,128)(2,1)S(1)}, u32[]{:S(2)}, u32[]{:S(2)}) collective-permute-start(bf16[224,256]{1,0:T(8,128)(2,1)S(1)} %get-tuple-element.44), channel_id=1, source_target_pairs={{0,1},{1,2},{2,3},{3,4},{4,5},{5,6},{6,7},{7,8},{8,9},{9,10},{10,1... | collective-permute-start | bytes 344072 | tf_op jit(solution)/shard_map/ppermute | solution.py:33
  45.1 5.4 %collective-permute-start.6 = (f32[128,128]{1,0:T(8,128)S(1)}, f32[128,128]{1,0:T(8,128)S(1)}, u32[]{:S(2)}, u32[]{:S(2)}) collective-permute-start(f32[128,128]{1,0:T(8,128)S(1)} %add.22), channel_id=1, source_target_pairs={{0,4},{1,5},{2,6},{3,7},{4,0},{5,1},{6,2},{7,3},{8,12},{9,13},{10,... | collective-permute-start | bytes 196616 | tf_op jit(solution)/shard_map/ppermute | solution.py:37
  48.2 10.4 %collective-permute-start.9 = (bf16[192,32]{1,0:T(8,128)(2,1)S(1)}, bf16[192,32]{1,0:T(8,128)(2,1)S(1)}, u32[]{:S(2)}, u32[]{:S(2)}) collective-permute-start(bf16[192,32]{1,0:T(8,128)(2,1)S(1)} %get-tuple-element.45), channel_id=1, source_target_pairs={{1,0},{2,1},{3,2},{4,3},{5,4},{6,5},{7,6},{8,7},{9,8},{10,9},{11,1... | collective-permute-start | bytes 36872 | tf_op jit(solution)/shard_map/ppermute | solution.py:33
  50.6 12.6 %collective-permute-start.7 = (f32[128,128]{1,0:T(8,128)S(1)}, f32[128,128]{1,0:T(8,128)S(1)}, u32[]{:S(2)}, u32[]{:S(2)}) collective-permute-start(f32[128,128]{1,0:T(8,128)S(1)} %add.23), channel_id=1, source_target_pairs={{0,8},{1,9},{2,10},{3,11},{4,12},{5,13},{6,14},{7,15},{8,0},{9,1},... | collective-permute-start | bytes 196616 | tf_op jit(solution)/shard_map/ppermute | solution.py:37
  63.9 9.7 %all-to-all-start.1 = ((bf16[8,128,128]{2,1,0:T(8,128)(2,1)}), bf16[8,128,128]{2,1,0:T(8,128)(2,1)S(1)}, u32[]{:S(2)}, u32[]{:S(2)}) async-start(bf16[8,128,128]{2,1,0:T(8,128)(2,1)} %broadcast_in_dim.10), calls=%async_computation.1 | async-start | bytes 524288 | tf_op jit(solution)/shard_map/all_to_all | solution.py:434
  73.6 5.9 %collective-permute-start.10 = (bf16[1024,128]{1,0:T(8,128)(2,1)S(1)}, bf16[1024,128]{1,0:T(8,128)(2,1)S(1)}, u32[]{:S(2)}, u32[]{:S(2)}) collective-permute-start(bf16[1024,128]{1,0:T(8,128)(2,1)S(1)} %bitcast.9), channel_id=1, source_target_pairs={{0,16},{16,0},{32,48},{48,32},{64,80},{80,64},{96,112},{112,96},{1... | collective-permute-start | bytes 786440 | tf_op jit(solution)/shard_map/ppermute | solution.py:37
